TPU v7x, 128 devices: a whole 4x4x4 slice. The times are simulated.
128 devices in a mesh: arrow: 4 (over z_lo, core), blk: 32 (over x, y, z_hi).
Axes of the slice: x: 4, y: 4, z: 4 (z_hi: 2, z_lo: 2; z = z_hi * 2 + z_lo), core: 2. Of those that a mesh axis runs over, the one named last changes fastest.
Arguments:
- features: bfloat16 [32768, 512], P(('arrow', 'blk')), may hold values from -6 to 6
- positions: int32 [4, 32768], P(None, ('arrow', 'blk')), may hold values from 0 to 32767, as said below
- diag_values: bfloat16 [4096, 32768], P('arrow', 'blk'), may hold values from -0.1875 to 0.1875
- column_values: bfloat16 [4096, 32768], P('arrow', 'blk'), may hold values from -0.1875 to 0.1875
- row_values: bfloat16 [4096, 32768], P('arrow', 'blk'), may hold values from -0.03125 to 0.03125
- tile_masks: int32 [3, 32, 256], P(None, 'arrow', 'blk'), may hold values from 0 to 1, as said below
- up_weight: bfloat16 [1024, 4096], replicated, may hold values from -0.1875 to 0.1875
- down_weight: bfloat16 [4096, 512], replicated, may hold values from -0.09375 to 0.09375
Outputs:
- node_out: bfloat16 [32768, 512], P(('arrow', 'blk'))
Inputs may be any that keep to these rules, and one draw needn't show every extreme that they name: For each arrow, positions is a permutation of the nodes. The 256 nodes of one device put at most 12 nodes into any one block of 1024 positions of one arrow, and exactly 12 into some block. `tile_masks`: 1 marks a stored tile, 0 an empty one.
All inputs are finite; a program needn't handle non-finite values.
Results may differ from a plain program's by a relative error of at most 0.0085.
Values may be sent and summed in bfloat16 or wider, within the bound.
No kernel may reach another device: no remote copies, remote signals or barrier semaphores. Data moves between devices by JAX's collectives and lax.ppermute only.
A program may use at most 64 MiB of HBM per device.

v0:
```python
import jax
import jax.numpy as jnp
from jax import lax
from jax.sharding import PartitionSpec as P


def spread(block, axis, source):
    block = jnp.where(lax.axis_index(axis) == source, block, jnp.zeros_like(block))
    return lax.psum(block, axis)


def masked_block(values, tiles):
    tile_count = tiles.shape[0]
    tile_edge = values.shape[0] // tile_count
    shaped = values.reshape(tile_count, tile_edge, tile_count, tile_edge)
    keep_mask = tiles.astype(values.dtype)[:, None, :, None]
    return (shaped * keep_mask).reshape(values.shape)


def body(
    features, positions, diag_values, column_values, row_values, tile_masks, up_weight, down_weight
):
    row_count = features.shape[0]
    feat_width = features.shape[1]
    arrow_count = positions.shape[0]
    block_count = lax.axis_size("blk")
    device_count = arrow_count * block_count
    block_rows = diag_values.shape[0]
    capacity = row_count // block_count + max(row_count // (2 * block_count), 1)
    flat_pos = positions.reshape(-1)
    arrow_ids = jnp.repeat(jnp.arange(arrow_count, dtype=jnp.int32), row_count)
    target_dev = arrow_ids * block_count + flat_pos // block_rows
    within_pos = flat_pos % block_rows
    onehot_dest = (
        target_dev[:, None] == jnp.arange(device_count, dtype=jnp.int32)[None, :]
    ).astype(jnp.int32)
    slot_rank = jnp.sum((jnp.cumsum(onehot_dest, axis=0) - 1) * onehot_dest, axis=1)
    slot_index = target_dev * capacity + slot_rank
    source_rows = jnp.tile(features, (arrow_count, 1))
    send_rows = (
        jnp.zeros((device_count * capacity, feat_width), features.dtype)
        .at[slot_index]
        .set(source_rows)
    )
    send_pos = (
        jnp.full((device_count * capacity,), block_rows, jnp.int32).at[slot_index].set(within_pos)
    )
    recv_rows, recv_pos = (
        lax.all_to_all(
            send_rows.reshape(device_count, capacity, feat_width),
            ("arrow", "blk"),
            split_axis=0,
            concat_axis=0,
            tiled=True,
        ),
        lax.all_to_all(
            send_pos.reshape(device_count, capacity),
            ("arrow", "blk"),
            split_axis=0,
            concat_axis=0,
            tiled=True,
        ),
    )
    recv_flat = recv_pos.reshape(-1)
    block_feats = (
        jnp.zeros((block_rows, feat_width), features.dtype)
        .at[recv_flat]
        .set(recv_rows.reshape(-1, feat_width), mode="drop")
    )
    head_block = spread(block_feats, "blk", 0)
    diag_full = masked_block(diag_values, tile_masks[0])
    column_full = masked_block(column_values, tile_masks[1])
    row_full = masked_block(row_values, tile_masks[2])
    arm_term = jnp.dot(row_full, block_feats, preferred_element_type=jnp.float32)
    local_sum = jnp.dot(diag_full, block_feats, preferred_element_type=jnp.float32)
    local_sum = local_sum + jnp.dot(column_full, head_block, preferred_element_type=jnp.float32)
    is_head = lax.axis_index("blk") == 0
    arm_total = lax.psum(arm_term.astype(jnp.bfloat16), "blk").astype(jnp.float32)
    results = jnp.where(is_head, local_sum + arm_total, local_sum).astype(jnp.bfloat16)
    picked = results[jnp.minimum(recv_flat, block_rows - 1)]
    returned = lax.all_to_all(
        picked.reshape(device_count, capacity, feat_width),
        ("arrow", "blk"),
        split_axis=0,
        concat_axis=0,
        tiled=True,
    )
    mine = returned.reshape(device_count * capacity, feat_width)[slot_index].reshape(
        arrow_count, row_count, feat_width
    )
    aggregate = jnp.sum(mine.astype(jnp.float32), axis=0).astype(jnp.bfloat16)
    joined = jnp.concatenate([features, aggregate], axis=1)
    hidden = jax.nn.silu(jnp.dot(joined, up_weight, preferred_element_type=jnp.float32)).astype(
        jnp.bfloat16
    )
    return jnp.dot(hidden, down_weight, preferred_element_type=jnp.float32).astype(jnp.bfloat16)


def solution(mesh):
    in_specs = (
        P(("arrow", "blk"), None),
        P(None, ("arrow", "blk")),
        P("arrow", "blk"),
        P("arrow", "blk"),
        P("arrow", "blk"),
        P(None, "arrow", "blk"),
        P(),
        P(),
    )
    out_specs = P(("arrow", "blk"), None)
    return jax.shard_map(body, mesh=mesh, in_specs=in_specs, out_specs=out_specs, check_vma=False)
```

profile of v0, /device:TPU:1, one launch (start us, length us, event | category | flops | bytes accessed | tf_op | source)
XLA Modules:
  0.0 514.9 jit_solution(13993231295632980102)
XLA Ops:
  6.5 0.0 copy-start.1
  6.5 0.0 copy-start
  6.6 0.7 reshape.255
  7.3 0.1 copy.12
  7.4 0.2 fusion.23
  7.7 0.1 copy.13
  7.8 0.0 copy-done.1
  7.9 0.4 fusion.22
  8.3 4.3 scatter_custom_fusion
  12.6 0.7 all_to_all.12
  13.4 11.5 %all-to-all-start = ((s32[128,1,12]{2,1,0:T(1,128)}), s32[128,1,12]{2,1,0:T(1,128)S(1)}, u32[]{:S(2)}, u32[]{:S(2)}) async-start(s32[128,1,12]{2,1,0:T(1,128)} %bitcast.6), calls=%async_computation | async-start | bytes 131072 | tf_op jit(solution)/shard_map/all_to_all | solution.py:56
  24.9 0.0 copy-done
  24.9 0.1 tile.4
  25.0 5.6 %scatter_custom_fusion.1 = bf16[1536,512]{1,0:T(8,128)(2,1)S(1)} fusion(s32[1024]{0:T(1024)S(1)} %bitcast.66, bf16[1024,512]{1,0:T(8,128)(2,1)S(1)} %bitcast.61, bf16[]{:T(256)} %constant.47.clone.1), kind=kCustom, calls=%fused_computation.21 | custom fusion | bytes 1572866 | tf_op jit(solution)/shard_map/scatter | solution.py:43
  30.5 1.5 reshape.258
  32.1 2.3 all-to-all-done
  34.4 7.4 %all-to-all-start.1 = ((bf16[128,12,512]{2,1,0:T(8,128)(2,1)}), bf16[128,12,512]{2,1,0:T(8,128)(2,1)S(1)}, u32[]{:S(2)}, u32[]{:S(2)}) async-start(bf16[128,12,512]{2,1,0:T(8,128)(2,1)} %reshape.258), calls=%async_computation.1 | async-start | bytes 4194304 | tf_op jit(solution)/shard_map/all_to_all | solution.py:49
  41.8 0.0 all-reduce.3.cloned.1.call-start
  41.9 0.0 copy-done.2
  41.9 0.5 broadcast.253
  42.5 0.8 reduce.8
  43.3 0.1 reshape.257
  43.4 28.6 %all-to-all-done.1 = bf16[128,12,512]{2,1,0:T(8,128)(2,1)S(1)} async-done(((bf16[128,12,512]{2,1,0:T(8,128)(2,1)}), bf16[128,12,512]{2,1,0:T(8,128)(2,1)S(1)}, u32[]{:S(2)}, u32[]{:S(2)}) %all-to-all-start.1) | async-done | bytes 1572896 | tf_op jit(solution)/shard_map/all_to_all | solution.py:49
  72.1 1.3 reshape.299
  73.4 8.2 %scatter_custom_fusion.2 = bf16[1024,512]{1,0:T(8,128)(2,1)S(1)} fusion(s32[1536]{0:T(1024)S(1)} %get-tuple-element.6, bf16[1536,512]{1,0:T(8,128)(2,1)} %reshape.299, bf16[]{:T(256)} %constant.47.clone.1), kind=kCustom, calls=%fused_computation.34 | custom fusion | bytes 1049088 | tf_op jit(solution)/shard_map/scatter | solution.py:68
  81.6 0.0 copy-start.3
  81.6 1.1 broadcast_select_fusion
  82.7 0.3 mul.97
  83.0 0.6 copy-done.3
  83.6 2.2 fusion.8
  85.8 0.0 all-reduce.3.cloned.1.call-update
  85.8 332.1 %all-reduce.3.cloned.1.call-done = (bf16[1024,512]{1,0:T(8,128)(2,1)}, bf16[1024,512]{1,0:T(8,128)(2,1)}) async-done(((bf16[1024,512]{1,0:T(8,128)(2,1)}, bf16[1024,512]{1,0:T(8,128)(2,1)}), (bf16[1024,512]{1,0:T(8,128)(2,1)}, bf16[1024,512]{1,0:T(8,128)(2,1)})) %all-reduce.3.cloned.1.call-update) | async-done | bytes 2097168 | tf_op jit(solution)/shard_map/psum | solution.py:78
  417.9 0.3 mul.94
  418.3 0.9 copy-done.6
  419.1 2.9 fusion.3
  422.1 0.0 copy-start.4
  422.1 0.3 mul.83
  422.4 0.0 copy-done.5
  422.4 1.2 copy-done.4
  423.7 1.3 fusion
  425.0 4.8 gather_fusion
  429.8 1.5 reshape.260
  431.3 31.3 %all-to-all-start.2 = ((bf16[128,12,512]{2,1,0:T(8,128)(2,1)}), bf16[128,12,512]{2,1,0:T(8,128)(2,1)}, u32[]{:S(2)}, u32[]{:S(2)}) async-start(bf16[128,12,512]{2,1,0:T(8,128)(2,1)} %reshape.260), calls=%async_computation.2 | async-start | bytes 4194304 | tf_op jit(solution)/shard_map/all_to_all | solution.py:81
  462.7 29.9 %all-to-all-done.2 = bf16[128,12,512]{2,1,0:T(8,128)(2,1)} async-done(((bf16[128,12,512]{2,1,0:T(8,128)(2,1)}), bf16[128,12,512]{2,1,0:T(8,128)(2,1)}, u32[]{:S(2)}, u32[]{:S(2)}) %all-to-all-start.2) | async-done | bytes 1572896 | tf_op jit(solution)/shard_map/all_to_all | solution.py:81
  492.5 2.5 reshape.261
  495.0 4.0 gather_fusion.1
  499.0 0.2 reduce_sum.25
  499.2 8.8 %fusion.9 = bf16[256,512]{1,0:T(8,128)(2,1)} fusion(bf16[4096,512]{1,0:T(8,128)(2,1)} %param.15, bf16[1024,4096]{1,0:T(8,128)(2,1)} %param.14, bf16[256,512]{1,0:T(8,128)(2,1)S(1)} %reduce_sum.25, bf16[256,512]{1,0:T(8,128)(2,1)S(1)} %copy-done), kind=kOutput, calls=%fused_computation.19 | convolution fusion | flops 3227648000 | bytes 13369344 | tf_op jit(solution)/shard_map/dot_general | solution.py:96
  (23 shorter events, 0.2 us)
Async XLA Ops:
  6.5 1.3 copy-start.1
  6.5 18.3 %copy-start = (bf16[256,512]{1,0:T(8,128)(2,1)S(1)}, bf16[256,512]{1,0:T(8,128)(2,1)}, u32[]{:S(2)}) copy-start(bf16[256,512]{1,0:T(8,128)(2,1)} %param.8) | copy-start | bytes 786436
  13.4 21.0 %all-to-all-start = ((s32[128,1,12]{2,1,0:T(1,128)}), s32[128,1,12]{2,1,0:T(1,128)S(1)}, u32[]{:S(2)}, u32[]{:S(2)}) async-start(s32[128,1,12]{2,1,0:T(1,128)} %bitcast.6), calls=%async_computation | async-start | bytes 131072 | tf_op jit(solution)/shard_map/all_to_all | solution.py:56
  32.1 9.8 %copy-start.2 = (s32[3,8,8]{2,1,0:T(8,128)S(1)}, s32[3,8,8]{2,1,0:T(8,128)}, u32[]{:S(2)}) copy-start(s32[3,8,8]{2,1,0:T(8,128)} %param.13) | copy-start | bytes 2308
  34.4 37.7 %all-to-all-start.1 = ((bf16[128,12,512]{2,1,0:T(8,128)(2,1)}), bf16[128,12,512]{2,1,0:T(8,128)(2,1)S(1)}, u32[]{:S(2)}, u32[]{:S(2)}) async-start(bf16[128,12,512]{2,1,0:T(8,128)(2,1)} %reshape.258), calls=%async_computation.1 | async-start | bytes 4194304 | tf_op jit(solution)/shard_map/all_to_all | solution.py:49
  41.8 376.1 %all-reduce.3.cloned.1.call-start = ((), (), s32[]{:S(2)}) async-start(), calls=%async_computation.3 | async-start | bytes 4194304 | tf_op jit(solution)/shard_map/psum | solution.py:78
  81.6 2.0 copy-start.3
  417.9 1.2 copy-start.6
  419.1 3.3 copy-start.5
  422.1 1.6 copy-start.4
  431.3 61.2 %all-to-all-start.2 = ((bf16[128,12,512]{2,1,0:T(8,128)(2,1)}), bf16[128,12,512]{2,1,0:T(8,128)(2,1)}, u32[]{:S(2)}, u32[]{:S(2)}) async-start(bf16[128,12,512]{2,1,0:T(8,128)(2,1)} %reshape.260), calls=%async_computation.2 | async-start | bytes 4194304 | tf_op jit(solution)/shard_map/all_to_all | solution.py:81
Sparse Core Ops, SparseCore 0:
  85.9 331.9 all-reduce.2
where the time goes:
time: 515 us
  waiting for transfers between devices  393 us (76%)
  starting transfers between devices  50.3 us (10%)
  local copies, waits for them, and re-layouts  39.8 us (8%)
  matrix products  15.3 us (3%)
  between operations  13.7 us (3%)
    psum x1, waiting for transfers between devices, body(): lax.psum(arm_term.astype(jnp.bfloat16), 'blk').astype(jnp.float32)  332 us
    all_to_all x1, starting transfers between devices, body(): lax.all_to_all(picked.reshape(device_count, capacity, feat_width), ('arro...  31.3 us
    all_to_all x1, waiting for transfers between devices, body(): lax.all_to_all(picked.reshape(device_count, capacity, feat_width), ('arro...  29.9 us
    all_to_all x1, waiting for transfers between devices, body(): lax.all_to_all(send_rows.reshape(device_count, capacity, feat_width), ('a...  28.6 us
    all_to_all x1, starting transfers between devices, body(): lax.all_to_all(send_pos.reshape(device_count, capacity), ('arrow', 'blk')...  11.5 us
  transfers between devices with their start and end apart: 4, of which 4 were waited for; matrix products, arithmetic and copies ran while one was open for 2% of the time, Pallas kernels for 0%

commit v1 on v0

v1 whole, which is shorter than its diff:
```python
import jax
import jax.numpy as jnp
from jax import lax
from jax.sharding import PartitionSpec as P

BF = jnp.bfloat16
F32 = jnp.float32


def exchange(block):
    return lax.all_to_all(block, ("arrow", "blk"), split_axis=0, concat_axis=0, tiled=True)


def masked_block(values, tiles):
    tile_count = tiles.shape[0]
    tile_edge = values.shape[0] // tile_count
    shaped = values.reshape(tile_count, tile_edge, tile_count, tile_edge)
    keep_mask = tiles.astype(values.dtype)[:, None, :, None]
    return (shaped * keep_mask).reshape(values.shape)


def body(
    features, positions, diag_values, column_values, row_values, tile_masks, up_weight, down_weight
):
    row_count, width = features.shape
    arrows = positions.shape[0]
    blocks = lax.axis_size("blk")
    devices = arrows * blocks
    block_rows = diag_values.shape[0]
    rows = devices * 8

    block_of = positions // block_rows
    within = positions % block_rows
    member = block_of[:, None, :] == jnp.arange(blocks, dtype=jnp.int32)[None, :, None]
    member = member.reshape(devices, row_count)
    node = jnp.arange(row_count, dtype=jnp.int32)
    before = (node[:, None] < node[None, :]).astype(BF)
    rank = jnp.dot(member.astype(BF), before, preferred_element_type=F32)
    rank = jnp.where(member, rank, -1.0)
    head_rank = rank.reshape(arrows, blocks, row_count)[:, :1, :]
    head_rank = jnp.broadcast_to(head_rank, (arrows, blocks, row_count)).reshape(rank.shape)
    r = jnp.arange(8, dtype=jnp.int32)[None, :, None]
    rank, head_rank = rank[:, None, :], head_rank[:, None, :]
    rf = r.astype(F32)
    picks = [
        rank == rf,
        jnp.where(r < 4, rank, head_rank) == jnp.where(r < 4, rf + 8, rf + 4),
        head_rank == rf,
    ]
    picks = [p.astype(BF).reshape(rows, row_count) for p in picks]

    coded = jnp.stack([within // 32 + 1, within % 32], axis=-1).astype(BF)
    sent = [jnp.dot(p, features, preferred_element_type=F32).astype(BF) for p in picks]
    places = []
    for p in picks:
        part = p.reshape(arrows, rows // arrows, row_count)
        place = jnp.einsum("amn,anc->amc", part, coded, preferred_element_type=F32)
        places.append(place.reshape(rows, 2))
    places = jnp.concatenate(places, axis=1).astype(BF)
    places = jnp.pad(places, ((0, 0), (0, 128 - places.shape[1])))
    message = jnp.concatenate(sent + [places], axis=1).reshape(devices, 8, 3 * width + 128)
    got = exchange(message).reshape(rows, 3 * width + 128)

    got_rows = [got[:, q * width : (q + 1) * width] for q in range(3)]
    codes = got[:, 3 * width :].astype(F32)
    slot_pos = [
        ((codes[:, 2 * q] - 1.0) * 32.0 + codes[:, 2 * q + 1]).astype(jnp.int32) for q in range(3)
    ]
    is_main = (jnp.arange(rows, dtype=jnp.int32) % 8) < 4
    spots = [
        slot_pos[0],
        jnp.where(is_main, slot_pos[1], -1),
        jnp.where(is_main, -1, slot_pos[1]),
        slot_pos[2],
    ]
    place_ids = jnp.arange(block_rows, dtype=jnp.int32)
    puts = [(place_ids[:, None] == s[None, :]).astype(BF) for s in spots]
    takes = [(s[:, None] == place_ids[None, :]).astype(BF) for s in spots]

    def mm(a, b):
        return jnp.dot(a, b, preferred_element_type=F32)

    block_feats = (mm(puts[0], got_rows[0]) + mm(puts[1], got_rows[1])).astype(BF)
    head_feats = (mm(puts[2], got_rows[1]) + mm(puts[3], got_rows[2])).astype(BF)
    diag_full = masked_block(diag_values, tile_masks[0])
    column_full = masked_block(column_values, tile_masks[1])
    row_full = masked_block(row_values, tile_masks[2])
    arm_term = mm(row_full, block_feats).astype(BF)
    local = (mm(diag_full, block_feats) + mm(column_full, head_feats)).astype(BF)
    back = [
        mm(takes[0], local).astype(BF),
        (mm(takes[1], local) + mm(takes[2], arm_term)).astype(BF),
        mm(takes[3], arm_term).astype(BF),
    ]
    reply = jnp.concatenate(back, axis=1).reshape(devices, 8, 3 * width)
    reply = exchange(reply).reshape(rows, 3 * width)

    aggregate = 0.0
    for q in range(3):
        aggregate = aggregate + lax.dot_general(
            picks[q],
            reply[:, q * width : (q + 1) * width],
            (((0,), (0,)), ((), ())),
            preferred_element_type=F32,
        )
    aggregate = aggregate.astype(BF)
    joined = jnp.concatenate([features, aggregate], axis=1)
    hidden = jax.nn.silu(mm(joined, up_weight)).astype(BF)
    return mm(hidden, down_weight).astype(BF)


def solution(mesh):
    in_specs = (
        P(("arrow", "blk"), None),
        P(None, ("arrow", "blk")),
        P("arrow", "blk"),
        P("arrow", "blk"),
        P("arrow", "blk"),
        P(None, "arrow", "blk"),
        P(),
        P(),
    )
    out_specs = P(("arrow", "blk"), None)
    return jax.shard_map(body, mesh=mesh, in_specs=in_specs, out_specs=out_specs, check_vma=False)
```

time: 515 us -> 160 us (0.31)
  waiting for transfers between devices: 393 us -> 43.5 us
  blocking collectives: 0 us -> 47.2 us
  starting transfers between devices: 50.3 us -> 11.7 us
  local copies, waits for them, and re-layouts: 39.8 us -> 9.83 us
  matrix products: 15.3 us -> 41.7 us
  between operations: 13.7 us -> 0.43 us
    psum x1 -> x0, waiting for transfers between devices: 332 us -> none  [body(): lax.psum(arm_term.astype(jnp.bfloat16), 'blk').astype(jnp.float32)]
    all_to_all x0 -> x1, blocking collectives: none -> 47.2 us  [exchange(): lax.all_to_all(block, ('arrow', 'blk'), split_axis=0, concat_axis=0, tile...]
    all_to_all x3 -> x1, starting transfers between devices: 50.3 us -> 11.7 us  [exchange(): lax.all_to_all(block, ('arrow', 'blk'), split_axis=0, concat_axis=0, tile...]
    dot_general x4 -> x21, matrix products: 15.3 us -> 41.7 us  [the longest x11 32.6 us: mm(): return jnp.dot(a, b, preferred_element_type=F32)]
    scatter x3 -> x0, local copies, waits for them, and re-layouts: 18.1 us -> none  [the longest x1 8.18 us: body(): block_feats = jnp.zeros((block_rows, feat_width), features.dtype).at[recv...]
    all_to_all x3 -> x1, waiting for transfers between devices: 60.8 us -> 43.5 us  [exchange(): lax.all_to_all(block, ('arrow', 'blk'), split_axis=0, concat_axis=0, tile...]
    gather x2 -> x0, local copies, waits for them, and re-layouts: 8.78 us -> none  [the longest x1 4.81 us: body(): picked = results[jnp.minimum(recv_flat, block_rows - 1)]]
    reshape x6 -> x0, local copies, waits for them, and re-layouts: 7.68 us -> none  [the longest x1 2.47 us: body(): returned.reshape(device_count * capacity, feat_width)[slot_index]]
  transfers between devices with their start and end apart: 4 -> 1, of which waited for: 4 -> 1; matrix products, arithmetic and copies ran while one was open for 2% -> 0% of each run, Pallas kernels for 0% -> 0%
where the time goes in v1:
time: 160 us
  blocking collectives  47.2 us (30%)
  waiting for transfers between devices  43.5 us (27%)
  matrix products  41.7 us (26%)
  starting transfers between devices  11.7 us (7%)
  local copies, waits for them, and re-layouts  9.83 us (6%)
  other arithmetic  5.4 us (3%)
    all_to_all x1, blocking collectives, exchange(): lax.all_to_all(block, ('arrow', 'blk'), split_axis=0, concat_axis=0, tile...  47.2 us
    all_to_all x1, waiting for transfers between devices, exchange(): lax.all_to_all(block, ('arrow', 'blk'), split_axis=0, concat_axis=0, tile...  43.5 us
    dot_general x11, matrix products, mm(): return jnp.dot(a, b, preferred_element_type=F32)  32.6 us
    all_to_all x1, starting transfers between devices, exchange(): lax.all_to_all(block, ('arrow', 'blk'), split_axis=0, concat_axis=0, tile...  11.7 us
    dot_general x3, matrix products, body(): jnp.dot(p, features, preferred_element_type=F32).astype(BF)  5.91 us
    concatenate x1, local copies, waits for them, and re-layouts, body(): jnp.concatenate(sent + [places], axis=1)  3.64 us
  transfers between devices with their start and end apart: 1, of which 1 were waited for; matrix products, arithmetic and copies ran while one was open for 0% of the time, Pallas kernels for 0%

profile of v1, /device:TPU:1, one launch (start us, length us, event | category | flops | bytes accessed | tf_op | source)
XLA Modules:
  0.0 159.8 jit_solution(1756026959768057338)
XLA Ops:
  0.0 0.7 fusion.99
  0.7 0.1 eq.216
  0.8 0.1 bitcast_compare_fusion.14
  0.9 0.2 convolution_select_fusion
  1.1 0.1 eq.232
  1.2 0.1 eq.236
  1.3 0.1 broadcast_in_dim.92
  1.5 0.1 eq.222
  1.6 2.6 %convolution_convert_fusion.2 = bf16[1024,512]{0,1:T(8,128)(2,1)} fusion(bf16[256,512]{1,0:T(8,128)(2,1)} %param.8, f32[1024]{0:T(1024)S(1)} %eq.222, f32[128,256]{1,0:T(8,128)S(1)} %convolution_select_fusion), kind=kOutput, calls=%fused_computation.49 | convolution fusion | flops 269221888 | bytes 1445888 | tf_op jit(solution)/shard_map/dot_general | solution.py:53
  4.2 0.0 copy-start
  4.2 2.6 %convolution_convert_fusion = bf16[1024,512]{0,1:T(8,128)(2,1)} fusion(bf16[256,512]{1,0:T(8,128)(2,1)} %param.8, f32[128,256]{1,0:T(8,128)S(1)} %bitcast.108, f32[1024]{0:T(1024)S(1)} %eq.222), kind=kOutput, calls=%fused_computation.47 | convolution fusion | flops 269221888 | bytes 1445888 | tf_op jit(solution)/shard_map/dot_general | solution.py:53
  6.7 0.1 broadcast_in_dim.89
  6.8 0.1 eq.219
  6.9 0.6 bitcast_compare_fusion.1
  7.5 0.3 convolution_convert_fusion.5
  7.7 0.3 convolution_convert_fusion.4
  8.0 0.3 convolution_convert_fusion.3
  8.2 0.1 eq.226
  8.3 0.1 broadcast_in_dim.84
  8.5 0.8 convolution_convert_fusion.1
  9.3 1.8 %pad_maximum_fusion = bf16[1024,1664]{0,1:T(8,128)(2,1)S(1)} fusion(bf16[1024,128]{0,1:T(8,128)(2,1)S(1)} %fusion.88, bf16[1024,512]{0,1:T(8,128)(2,1)} %convolution_convert_fusion, bf16[1024,512]{0,1:T(8,128)(2,1)S(1)} %convolution_convert_fusion.1, bf16[1024,512]{0,1:T(8,128)(2,1)} %convolution_convert_fusion.2), kind=kLoop, calls=%fused_computation.17 | loop fusion | flops 13631488 | bytes 6815744 | tf_op jit(solution)/shard_map/concatenate | solution.py:61
  11.1 3.6 %copy.15 = bf16[1024,1664]{1,0:T(8,128)(2,1)} copy(bf16[1024,1664]{0,1:T(8,128)(2,1)S(1)} %pad_maximum_fusion) | data formatting | bytes 6815744 | tf_op jit(solution)/shard_map/concatenate | solution.py:61
  14.7 11.7 %all-to-all-start = ((bf16[128,8,1664]{2,1,0:T(8,128)(2,1)}), bf16[128,8,1664]{2,1,0:T(8,128)(2,1)S(1)}, u32[]{:S(2)}, u32[]{:S(2)}) async-start(bf16[128,8,1664]{2,1,0:T(8,128)(2,1)} %bitcast.12), calls=%async_computation | async-start | bytes 6815744 | tf_op jit(solution)/shard_map/all_to_all | solution.py:11
  26.5 43.5 %all-to-all-done = bf16[128,8,1664]{2,1,0:T(8,128)(2,1)S(1)} async-done(((bf16[128,8,1664]{2,1,0:T(8,128)(2,1)}), bf16[128,8,1664]{2,1,0:T(8,128)(2,1)S(1)}, u32[]{:S(2)}, u32[]{:S(2)}) %all-to-all-start) | async-done | bytes 3407904 | tf_op jit(solution)/shard_map/all_to_all | solution.py:11
  70.0 1.8 %select_reduce_fusion = (s32[1024]{0:T(1024)}, s32[1024]{0:T(1024)}, s32[1024]{0:T(1024)}, s32[1024]{0:T(1024)S(1)}, s32[1024]{0:T(1024)S(1)}) fusion(f32[1024,128]{1,0:T(8,128)S(1)} %slice_convert_fusion), kind=kLoop, calls=%fused_computation.97 | loop fusion | flops 21504 | bytes 45056 | tf_op jit(solution)/shard_map/jit(_where)/select_n | solution.py:73
  71.8 2.6 %fusion.3 = f32[1024,512]{1,0:T(8,128)} fusion(s32[1024]{0:T(1024)S(1)} %get-tuple-element.16, bf16[1024,1664]{1,0:T(8,128)(2,1)S(1)} %bitcast.97), kind=kOutput, calls=%fused_computation.12 | convolution fusion | flops 1074790400 | bytes 3149824 | tf_op jit(solution)/shard_map/dot_general | solution.py:81
  74.4 1.3 fusion.1
  75.7 2.3 %add_convert_fusion.3 = bf16[1024,512]{1,0:T(8,128)(2,1)} fusion(f32[1024,512]{1,0:T(8,128)S(1)} %fusion.1, s32[1024]{0:T(1024)S(1)} %get-tuple-element.17, bf16[1024,1664]{1,0:T(8,128)(2,1)S(1)} %bitcast.99), kind=kOutput, calls=%fused_computation.36 | convolution fusion | flops 1075838976 | bytes 4198400 | tf_op jit(solution)/shard_map/dot_general | solution.py:81
  77.9 1.6 %mul.73 = bf16[8,128,8,128]{3,2,1,0:T(8,128)(2,1)} broadcast(bf16[8,8]{1,0:T(8,128)(2,1)S(1)} %get-tuple-element.15), dimensions={0,2} | broadcast | bytes 2097280 | tf_op jit(solution)/shard_map/mul | solution.py:19
  79.6 6.5 %fusion.10 = f32[1024,512]{1,0:T(8,128)} fusion(bf16[1024,1024]{1,0:T(8,128)(2,1)} %param.11, bf16[128,8,8,128]{3,2,1,0:T(8,128)(2,1)} %bitcast.104, f32[1024,512]{1,0:T(8,128)} %fusion.3, s32[1024]{0:T(1024)} %get-tuple-element.7, bf16[1024,1664]{1,0:T(8,128)(2,1)S(1)} %bitcast.100), kind=kOutput, calls=%fused_computation.23 | convolution fusion | flops 2150629376 | bytes 9441280 | tf_op jit(solution)/shard_map/dot_general | solution.py:81
  86.1 0.3 mul.69
  86.5 3.8 %add_convert_fusion.1 = bf16[1024,512]{1,0:T(8,128)(2,1)S(1)} fusion(f32[1024,512]{1,0:T(8,128)} %fusion.10, bf16[1024,512]{1,0:T(8,128)(2,1)} %add_convert_fusion.3, bf16[1024,1024]{1,0:T(8,128)(2,1)} %param.10, bf16[128,8,8,128]{3,2,1,0:T(8,128)(2,1)S(1)} %bitcast.105), kind=kOutput, calls=%fused_computation.32 | convolution fusion | flops 1075838976 | bytes 8388608 | tf_op jit(solution)/shard_map/dot_general | solution.py:81
  90.3 1.5 fusion.25
  91.8 0.0 copy-start.14
  91.8 1.5 fusion.5
  93.3 0.3 mul.77
  93.6 0.0 copy-done.15
  93.6 1.5 fusion.23
  95.2 1.5 fusion.24
  96.7 1.5 add_convert_fusion
  98.1 0.4 pad_maximum_fusion.1
  98.5 2.9 %copy.16 = bf16[1024,1536]{1,0:T(8,128)(2,1)} copy(bf16[1024,1536]{0,1:T(8,128)(2,1)S(1)} %pad_maximum_fusion.1) | data formatting | bytes 6291456 | tf_op jit(solution)/shard_map/concatenate | solution.py:95
  101.5 47.2 %all_to_all.10 = bf16[128,8,1536]{2,1,0:T(8,128)(2,1)S(1)} all-to-all(bf16[128,8,1536]{2,1,0:T(8,128)(2,1)} %bitcast.93), channel_id=1, replica_groups=mesh['arrow'=4,'blk'=32] {'arrow','blk'}, dimensions={0} | all-to-all | bytes 6291456 | tf_op jit(solution)/shard_map/all_to_all | solution.py:11
  148.7 0.0 copy-start.3
  148.7 0.9 fusion.33
  149.5 0.7 fusion.29
  150.2 0.7 fusion.30
  151.0 8.8 %fusion.31 = bf16[256,512]{1,0:T(8,128)(2,1)} fusion(bf16[4096,512]{1,0:T(8,128)(2,1)} %param.15, bf16[1024,4096]{1,0:T(8,128)(2,1)} %param.14, bf16[256,512]{1,0:T(8,128)(2,1)S(1)} %fusion.30, bf16[256,512]{1,0:T(8,128)(2,1)S(1)} %copy-done.3), kind=kOutput, calls=%fused_computation.58 | convolution fusion | flops 3227648000 | bytes 13369344 | tf_op jit(solution)/shard_map/dot_general | solution.py:81
  (48 shorter events, 0.2 us)
Async XLA Ops:
  4.2 4.3 %copy-start = (f32[4,32,256]{2,1,0:T(8,128)}, f32[4,32,256]{2,1,0:T(8,128)S(1)}, u32[]{:S(2)}) copy-start(f32[4,32,256]{2,1,0:T(8,128)S(1)} %broadcast_in_dim.87) | copy-start | bytes 393220
  6.7 1.7 %copy-start.2 = (bf16[256,512]{1,0:T(8,128)(2,1)S(1)}, bf16[256,512]{1,0:T(8,128)(2,1)}, u32[]{:S(2)}) copy-start(bf16[256,512]{1,0:T(8,128)(2,1)} %param.8) | copy-start | bytes 786436
  8.3 0.9 copy-start.10
  8.5 0.8 copy-start.12
  14.7 11.7 %copy-start.4 = (s32[3,8,8]{2,1,0:T(8,128)S(1)}, s32[3,8,8]{2,1,0:T(8,128)}, u32[]{:S(2)}) copy-start(s32[3,8,8]{2,1,0:T(8,128)} %param.13) | copy-start | bytes 2308
  14.7 55.2 %all-to-all-start = ((bf16[128,8,1664]{2,1,0:T(8,128)(2,1)}), bf16[128,8,1664]{2,1,0:T(8,128)(2,1)S(1)}, u32[]{:S(2)}, u32[]{:S(2)}) async-start(bf16[128,8,1664]{2,1,0:T(8,128)(2,1)} %bitcast.12), calls=%async_computation | async-start | bytes 6815744 | tf_op jit(solution)/shard_map/all_to_all | solution.py:11
  71.8 2.6 %copy-start.8 = (s32[1024]{0:T(1024)}, s32[1024]{0:T(1024)S(1)}, u32[]{:S(2)}) copy-start(s32[1024]{0:T(1024)S(1)} %get-tuple-element.8) | copy-start | bytes 12292
  86.5 3.8 %copy-start.9 = (s32[1024]{0:T(1024)S(1)}, s32[1024]{0:T(1024)}, u32[]{:S(2)}) copy-start(s32[1024]{0:T(1024)} %copy-done.8) | copy-start | bytes 12292
  90.3 1.5 copy-start.7
  91.8 1.8 %copy-start.14 = (bf16[1024,1024]{1,0:T(8,128)(2,1)S(1)}, bf16[1024,1024]{1,0:T(8,128)(2,1)}, u32[]{:S(2)}) copy-start(bf16[1024,1024]{1,0:T(8,128)(2,1)} %param.12) | copy-start | bytes 6291460
  91.8 1.8 %copy-start.15 = (bf16[1024,512]{1,0:T(8,128)(2,1)S(1)}, bf16[1024,512]{1,0:T(8,128)(2,1)}, u32[]{:S(2)}) copy-start(bf16[1024,512]{1,0:T(8,128)(2,1)} %add_convert_fusion.3) | copy-start | bytes 3145732
  93.6 1.5 copy-start.6
  95.2 1.5 copy-start.5
  101.5 47.2 %copy-start.1 = (f32[4,32,256]{2,1,0:T(8,128)S(1)}, f32[4,32,256]{2,1,0:T(8,128)}, u32[]{:S(2)}) copy-start(f32[4,32,256]{2,1,0:T(8,128)} %copy-done) | copy-start | bytes 393220
  101.5 47.2 %copy-start.11 = (f32[1024]{0:T(1024)S(1)}, f32[1024]{0:T(1024)}, u32[]{:S(2)}) copy-start(f32[1024]{0:T(1024)} %copy-done.10) | copy-start | bytes 12292
  101.5 47.2 %copy-start.13 = (pred[1024]{0:T(1024)(128)(4,1)S(1)}, pred[1024]{0:T(1024)(128)(4,1)}, u32[]{:S(2)}) copy-start(pred[1024]{0:T(1024)(128)(4,1)} %copy-done.12) | copy-start | bytes 3076
  148.7 2.3 %copy-start.3 = (bf16[256,512]{1,0:T(8,128)(2,1)S(1)}, bf16[256,512]{1,0:T(8,128)(2,1)}, u32[]{:S(2)}) copy-start(bf16[256,512]{1,0:T(8,128)(2,1)} %param.8) | copy-start | bytes 786436

commit v2 on v1

v2 whole, which is shorter than its diff:
```python
import functools

import jax
import jax.numpy as jnp
from jax import lax
from jax.experimental import pallas as pl
from jax.experimental.pallas import tpu as pltpu
from jax.sharding import PartitionSpec as P

BF = jnp.bfloat16
F32 = jnp.float32
VM = pl.BlockSpec(memory_space=pltpu.VMEM)
HB = pl.BlockSpec(memory_space=pltpu.HBM)
MIB = 1 << 20


def exchange(block):
    return lax.all_to_all(block, ("arrow", "blk"), split_axis=0, concat_axis=0, tiled=True)


def mm(a, b):
    return jnp.dot(a, b, preferred_element_type=F32)


def mm_nt(a, b):
    return lax.dot_general(a, b, (((1,), (1,)), ((), ())), preferred_element_type=F32)


def in_hbm(x):
    return pltpu.with_memory_space_constraint(x, pltpu.HBM)


def onehot(mask):
    return jnp.where(mask, 1.0, 0.0).astype(BF)


def slot_targets(r):
    return jnp.where(r < 4, r + 8, r + 4).astype(F32)


def pack_kernel(block_rows, width, feat_ref, pos_ref, out_ref):
    nodes = feat_ref.shape[0]
    rows = out_ref.shape[0]
    feats = feat_ref[...]
    n0 = lax.broadcasted_iota(jnp.int32, (nodes, nodes), 0)
    n1 = lax.broadcasted_iota(jnp.int32, (nodes, nodes), 1)
    before = onehot(n0 < n1)
    slot = lax.broadcasted_iota(jnp.int32, (rows, nodes), 0)
    r = slot % 8
    rf = r.astype(F32)
    code_row = lax.broadcasted_iota(jnp.int32, (128, nodes), 0)
    pos = pos_ref[pl.ds(pl.program_id(0), 1), :]
    within = pos % block_rows
    member = pos // block_rows == slot // 8
    rank = jnp.where(member, mm(onehot(member), before), -1.0)
    head = jnp.broadcast_to(rank[0:1, :], rank.shape)
    picks = (
        onehot(rank == rf),
        onehot(jnp.where(r < 4, rank, head) == slot_targets(r)),
        onehot(head == rf),
    )
    high = (within // 32 + 1).astype(F32)
    low = (within % 32).astype(F32)
    codes = jnp.zeros((rows, 128), F32)
    for q in range(3):
        out_ref[:, q * width : (q + 1) * width] = mm(picks[q], feats).astype(BF)
        table = jnp.where(code_row == 2 * q, high, jnp.where(code_row == 2 * q + 1, low, 0.0))
        codes = codes + mm_nt(picks[q], table.astype(BF))
    out_ref[:, 3 * width :] = codes.astype(BF)


def gather_kernel(arrows, block_rows, pos_ref, out_ref):
    nodes = out_ref.shape[0]
    total = out_ref.shape[1] // 3
    rows = total // arrows
    n0 = lax.broadcasted_iota(jnp.int32, (nodes, nodes), 0)
    n1 = lax.broadcasted_iota(jnp.int32, (nodes, nodes), 1)
    before = onehot(n1 < n0)
    slot = lax.broadcasted_iota(jnp.int32, (nodes, rows), 1)
    block = slot // 8
    r = slot % 8
    rf = r.astype(F32)
    goal = slot_targets(r)
    for a in range(arrows):
        member = pos_ref[:, a : a + 1] // block_rows == block
        rank = jnp.where(member, mm(before, onehot(member)), -1.0)
        head = jnp.broadcast_to(rank[:, 0:1], rank.shape)
        picks = (
            onehot(rank == rf),
            onehot(jnp.where(r < 4, rank, head) == goal),
            onehot(head == rf),
        )
        for q in range(3):
            base = q * total + a * rows
            out_ref[:, base : base + rows] = picks[q]


def middle_kernel(
    width, got_ref, mask_ref, diag_hbm, col_hbm, row_hbm, out_hbm,
    w_ref, x_ref, x0_ref, y_ref, t_ref, p_ref, pt_ref, out_ref, w_sem, out_sem,
):
    slots = got_ref.shape[0]
    size = x_ref.shape[0]
    step = 256
    loads = [
        pltpu.make_async_copy(src, w_ref.at[k], w_sem.at[k])
        for k, src in enumerate((diag_hbm, col_hbm, row_hbm))
    ]
    for copy in loads:
        copy.start()
    codes = got_ref[:, 3 * width :].astype(F32)
    place = (codes - 1.0) * 32.0 + pltpu.roll(codes, 127, 1)
    p_ref[...] = place
    pt_ref[...] = place.T
    lane = lax.broadcasted_iota(jnp.int32, (1, slots), 1) % 8 < 4
    sub = lax.broadcasted_iota(jnp.int32, (step, 1), 0) % 8 < 4

    def unpack(c, carry):
        ids = (lax.broadcasted_iota(jnp.int32, (step, slots), 0) + c * step).astype(F32)
        mid = pt_ref[2:3, :]
        a0 = onehot(pt_ref[0:1, :] == ids)
        a1 = onehot(jnp.where(lane, mid, -1.0) == ids)
        b1 = onehot(jnp.where(lane, -1.0, mid) == ids)
        b2 = onehot(pt_ref[4:5, :] == ids)
        g0 = got_ref[:, 0:width]
        g1 = got_ref[:, width : 2 * width]
        g2 = got_ref[:, 2 * width : 3 * width]
        span = pl.ds(pl.multiple_of(c * step, step), step)
        x_ref[span, :] = (mm(a0, g0) + mm(a1, g1)).astype(BF)
        x0_ref[span, :] = (mm(b1, g1) + mm(b2, g2)).astype(BF)
        return carry

    lax.fori_loop(0, size // step, unpack, 0)
    for copy in loads:
        copy.wait()
    tiles = mask_ref.shape[0] // 3
    edge = size // tiles

    def multiply(c, carry):
        span = pl.ds(pl.multiple_of(c * edge, edge), edge)
        kept = []
        for k in range(3):
            keep = jnp.broadcast_to(mask_ref[pl.ds(k * tiles + c, 1), :], (edge, size))
            kept.append(w_ref[k, span, :] * keep.astype(BF))
        x = x_ref[...]
        t_ref[span, :] = mm(kept[2], x).astype(BF)
        y_ref[span, :] = (mm(kept[0], x) + mm(kept[1], x0_ref[...])).astype(BF)
        return carry

    lax.fori_loop(0, tiles, multiply, 0)

    def store(c):
        span = pl.ds(pl.multiple_of(c * step, step), step)
        return pltpu.make_async_copy(out_ref.at[span, :], out_hbm.at[span, :], out_sem.at[c])

    def pack(c, carry):
        span = pl.ds(pl.multiple_of(c * step, step), step)
        ids = lax.broadcasted_iota(jnp.int32, (step, size), 1).astype(F32)
        mid = p_ref[span, 2:3]
        a0 = onehot(p_ref[span, 0:1] == ids)
        a1 = onehot(jnp.where(sub, mid, -1.0) == ids)
        b1 = onehot(jnp.where(sub, -1.0, mid) == ids)
        b2 = onehot(p_ref[span, 4:5] == ids)
        y = y_ref[...]
        t = t_ref[...]
        out_ref[span, 0:width] = mm(a0, y).astype(BF)
        out_ref[span, width : 2 * width] = (mm(a1, y) + mm(b1, t)).astype(BF)
        out_ref[span, 2 * width : 3 * width] = mm(b2, t).astype(BF)
        store(c).start()
        return carry

    lax.fori_loop(0, slots // step, pack, 0)
    for c in range(slots // step):
        store(c).wait()


CHUNK = 512


def tail_kernel(
    width, reply_ref, pick_hbm, pre_hbm, up_hbm, down_hbm, out_ref,
    pick_ref, pre_ref, up_ref, down_ref, agg_ref, acc_ref, pick_sem, sem,
):
    slots = reply_ref.shape[0]
    count = down_ref.shape[0] // CHUNK

    def loads(c):
        span = pl.ds(pl.multiple_of(c * CHUNK, CHUNK), CHUNK)
        return (
            pltpu.make_async_copy(up_hbm.at[width:, span], up_ref.at[:, span], sem.at[0, c]),
            pltpu.make_async_copy(pre_hbm.at[:, span], pre_ref.at[:, span], sem.at[1, c]),
            pltpu.make_async_copy(down_hbm.at[span, :], down_ref.at[span, :], sem.at[2, c]),
        )

    first = pltpu.make_async_copy(pick_hbm, pick_ref, pick_sem)
    first.start()
    for c in range(count):
        for copy in loads(c):
            copy.start()
    first.wait()
    total = jnp.zeros(agg_ref.shape, F32)
    for q in range(3):
        total = total + mm(
            pick_ref[:, q * slots : (q + 1) * slots], reply_ref[:, q * width : (q + 1) * width]
        )
    agg_ref[...] = total.astype(BF)
    acc_ref[...] = jnp.zeros(acc_ref.shape, F32)

    def chunk(c, carry):
        span = pl.ds(pl.multiple_of(c * CHUNK, CHUNK), CHUNK)
        for copy in loads(c):
            copy.wait()
        v = pre_ref[:, span] + mm(agg_ref[...], up_ref[:, span])
        hidden = (v / (1.0 + jnp.exp(-v))).astype(BF)
        acc_ref[...] += mm(hidden, down_ref[span, :])
        return carry

    lax.fori_loop(0, count, chunk, 0)
    out_ref[...] = acc_ref[...].astype(BF)


def body(
    features, positions, diag_values, column_values, row_values, tile_masks, up_weight, down_weight
):
    row_count, width = features.shape
    arrows = positions.shape[0]
    devices = arrows * lax.axis_size("blk")
    size = diag_values.shape[0]
    hidden = down_weight.shape[0]
    tiles = tile_masks.shape[1]
    rows = devices * 8
    longest = 3 * width + 128

    message = pl.pallas_call(
        functools.partial(pack_kernel, size, width),
        grid=(arrows,),
        in_specs=[
            pl.BlockSpec(features.shape, lambda a: (0, 0)),
            pl.BlockSpec(positions.shape, lambda a: (0, 0)),
        ],
        out_specs=pl.BlockSpec((rows // arrows, longest), lambda a: (a, 0)),
        out_shape=pltpu.HBM((rows, longest), BF),
        compiler_params=pltpu.CompilerParams(vmem_limit_bytes=16 * MIB),
        name="pack",
    )(features, positions)
    got = exchange(message.reshape(devices, 8, longest)).reshape(rows, longest)

    gather = pl.pallas_call(
        functools.partial(gather_kernel, arrows, size),
        in_specs=[VM],
        out_specs=VM,
        out_shape=jax.ShapeDtypeStruct((row_count, 3 * rows), BF),
        compiler_params=pltpu.CompilerParams(vmem_limit_bytes=16 * MIB),
        name="gather",
    )(positions.T)
    pre = mm(features, up_weight[:width])
    keep = jnp.repeat(tile_masks.astype(F32), size // tiles, axis=2).reshape(3 * tiles, size)

    reply = pl.pallas_call(
        functools.partial(middle_kernel, width),
        in_specs=[VM, VM, HB, HB, HB],
        out_specs=HB,
        out_shape=pltpu.HBM((rows, 3 * width), BF),
        scratch_shapes=[pltpu.VMEM((3, size, size), BF)]
        + [pltpu.VMEM((size, width), BF)] * 4
        + [
            pltpu.VMEM((rows, 128), F32),
            pltpu.VMEM((128, rows), F32),
            pltpu.VMEM((rows, 3 * width), BF),
            pltpu.SemaphoreType.DMA((3,)),
            pltpu.SemaphoreType.DMA((rows // 256,)),
        ],
        compiler_params=pltpu.CompilerParams(vmem_limit_bytes=40 * MIB),
        name="middle",
    )(got, keep, in_hbm(diag_values), in_hbm(column_values), in_hbm(row_values))
    reply = exchange(reply.reshape(devices, 8, 3 * width)).reshape(rows, 3 * width)

    return pl.pallas_call(
        functools.partial(tail_kernel, width),
        in_specs=[VM, HB, HB, HB, HB],
        out_specs=VM,
        out_shape=jax.ShapeDtypeStruct((row_count, width), BF),
        scratch_shapes=[
            pltpu.VMEM((row_count, 3 * rows), BF),
            pltpu.VMEM((row_count, hidden), F32),
            pltpu.VMEM((width, hidden), BF),
            pltpu.VMEM((hidden, width), BF),
            pltpu.VMEM((row_count, width), BF),
            pltpu.VMEM((row_count, width), F32),
            pltpu.SemaphoreType.DMA,
            pltpu.SemaphoreType.DMA((3, hidden // CHUNK)),
        ],
        compiler_params=pltpu.CompilerParams(vmem_limit_bytes=40 * MIB),
        name="tail",
    )(reply, in_hbm(gather), in_hbm(pre), in_hbm(up_weight), in_hbm(down_weight))


def solution(mesh):
    in_specs = (
        P(("arrow", "blk"), None),
        P(None, ("arrow", "blk")),
        P("arrow", "blk"),
        P("arrow", "blk"),
        P("arrow", "blk"),
        P(None, "arrow", "blk"),
        P(),
        P(),
    )
    out_specs = P(("arrow", "blk"), None)
    return jax.shard_map(body, mesh=mesh, in_specs=in_specs, out_specs=out_specs, check_vma=False)
```

time: 160 us -> 136 us (0.85)
  blocking collectives: 47.2 us -> 0 us
  matrix products: 41.7 us -> 5.39 us
  waiting for transfers between devices: 43.5 us -> 77 us
  Pallas kernels: 0 us -> 32.4 us
  local copies, waits for them, and re-layouts: 9.83 us -> 3.19 us
  starting transfers between devices: 11.7 us -> 17.6 us
  other arithmetic: 5.4 us -> 0.01 us
    all_to_all x1 -> x0, blocking collectives: 47.2 us -> none  [exchange(): lax.all_to_all(block, ('arrow', 'blk'), split_axis=0, concat_axis=0, tile...]
    all_to_all x1 -> x2, waiting for transfers between devices: 43.5 us -> 77 us  [exchange(): lax.all_to_all(block, ('arrow', 'blk'), split_axis=0, concat_axis=0, tile...]
    pallas_call x0 -> x4, Pallas kernels: none -> 32.4 us  [the longest x1 16.1 us: body(): pl.pallas_call(functools.partial(middle_kernel, width), in_specs=[VM, VM,...]
    dot_general x11 -> x1, matrix products: 32.6 us -> 5.39 us  [mm(): return jnp.dot(a, b, preferred_element_type=F32)]
    dot_general x10 -> x0, matrix products: 9.1 us -> none  [the longest x3 5.91 us: body(): jnp.dot(p, features, preferred_element_type=F32).astype(BF)]
    concatenate x2 -> x0, local copies, waits for them, and re-layouts: 6.59 us -> none  [the longest x1 3.64 us: body(): jnp.concatenate(sent + [places], axis=1)]
    all_to_all x1 -> x2, starting transfers between devices: 11.7 us -> 17.6 us  [exchange(): lax.all_to_all(block, ('arrow', 'blk'), split_axis=0, concat_axis=0, tile...]
    unnamed x33 -> x13, local copies, waits for them, and re-layouts: 0.08 us -> 3.04 us
  transfers between devices with their start and end apart: 1 -> 2, of which waited for: 1 -> 2; matrix products, arithmetic and copies ran while one was open for 0% -> 4% of each run, Pallas kernels for 0% -> 1%
where the time goes in v2:
time: 136 us
  waiting for transfers between devices  77 us (57%)
  Pallas kernels  32.4 us (24%)
  starting transfers between devices  17.6 us (13%)
  matrix products  5.39 us (4%)
  local copies, waits for them, and re-layouts  3.19 us (2%)
    all_to_all x2, waiting for transfers between devices, exchange(): lax.all_to_all(block, ('arrow', 'blk'), split_axis=0, concat_axis=0, tile...  77 us
    all_to_all x2, starting transfers between devices, exchange(): lax.all_to_all(block, ('arrow', 'blk'), split_axis=0, concat_axis=0, tile...  17.6 us
    pallas_call x1, Pallas kernels, body(): pl.pallas_call(functools.partial(middle_kernel, width), in_specs=[VM, VM,...  16.1 us
    pallas_call x1, Pallas kernels, body(): pl.pallas_call(functools.partial(tail_kernel, width), in_specs=[VM, HB, H...  11.7 us
    dot_general x1, matrix products, mm(): return jnp.dot(a, b, preferred_element_type=F32)  5.39 us
    pallas_call x1, Pallas kernels, body(): pl.pallas_call(functools.partial(pack_kernel, size, width), grid=(arrows,...  3.82 us
    unnamed x13, local copies, waits for them, and re-layouts  3.04 us
  transfers between devices with their start and end apart: 2, of which 2 were waited for; matrix products, arithmetic and copies ran while one was open for 4% of the time, Pallas kernels for 1%

profile of v2, /device:TPU:1, one launch (start us, length us, event | category | flops | bytes accessed | tf_op | source)
XLA Modules:
  0.0 135.7 jit_solution(13587703432100022398)
XLA Ops:
  0.0 0.0 copy-start.1
  0.0 0.9 copy-done.1
  1.0 0.0 copy-start.3
  1.0 0.7 copy-done.3
  1.6 3.8 %pack.1 = bf16[1024,1664]{1,0:T(8,128)(2,1)} custom-call(bf16[256,512]{1,0:T(8,128)(2,1)S(1)} %copy-done.1, s32[4,256]{1,0:T(4,128)S(1)} %copy-done.3), custom_call_target="tpu_custom_call" | custom-call | tf_op jit(solution)/shard_map/pack/pallas_call | solution.py:234
  5.5 0.0 copy-start.5
  5.5 11.5 %all-to-all-start = ((bf16[128,8,1664]{2,1,0:T(8,128)(2,1)}), bf16[128,8,1664]{2,1,0:T(8,128)(2,1)S(1)}, u32[]{:S(2)}, u32[]{:S(2)}) async-start(bf16[128,8,1664]{2,1,0:T(8,128)(2,1)} %bitcast.11), calls=%async_computation | async-start | bytes 6815744 | tf_op jit(solution)/shard_map/all_to_all | solution.py:18
  17.0 0.0 copy-done.5
  17.0 0.1 copy.9
  17.0 0.1 broadcast_bitcast_fusion.mask_ref
  17.1 43.6 %all-to-all-done = bf16[128,8,1664]{2,1,0:T(8,128)(2,1)S(1)} async-done(((bf16[128,8,1664]{2,1,0:T(8,128)(2,1)}), bf16[128,8,1664]{2,1,0:T(8,128)(2,1)S(1)}, u32[]{:S(2)}, u32[]{:S(2)}) %all-to-all-start) | async-done | bytes 3407904 | tf_op jit(solution)/shard_map/all_to_all | solution.py:18
  60.7 16.1 %middle.1 = bf16[1024,1536]{1,0:T(8,128)(2,1)} custom-call(bf16[1024,1664]{1,0:T(8,128)(2,1)S(1)} %bitcast.8, f32[24,1024]{1,0:T(8,128)S(1)} %broadcast_bitcast_fusion.mask_ref, bf16[1024,1024]{1,0:T(8,128)(2,1)} %diag_hbm.1, bf16[1024,1024]{1,0:T(8,128)(2,1)} %col_hbm.1, bf16[1024,1024]{1,0:T(8,128)(2,1)} %row_hbm.1), custom_call_target="tpu_custom_call" | custom-call | tf_op jit(solution)/shard_map/middle/pallas_call | solution.py:259
  76.8 0.0 copy-start.4
  76.9 0.0 copy-start.2
  76.9 6.1 %all-to-all-start.1 = ((bf16[128,8,1536]{2,1,0:T(8,128)(2,1)}), bf16[128,8,1536]{2,1,0:T(8,128)(2,1)S(1)}, u32[]{:S(2)}, u32[]{:S(2)}) async-start(bf16[128,8,1536]{2,1,0:T(8,128)(2,1)} %bitcast.12), calls=%async_computation.1 | async-start | bytes 6291456 | tf_op jit(solution)/shard_map/all_to_all | solution.py:18
  83.0 0.0 copy-done.4
  83.0 0.1 copy.10
  83.1 0.7 gather.1.pick_hbm
  83.9 0.0 copy-start
  83.9 1.2 copy-done
  85.2 0.0 copy-done.2
  85.2 5.4 %fusion.pre_hbm = f32[256,4096]{1,0:T(8,128)} fusion(bf16[256,512]{1,0:T(8,128)(2,1)S(1)} %copy-done.2, bf16[1024,4096]{1,0:T(8,128)(2,1)} %up_hbm.1), kind=kOutput, calls=%fused_computation | convolution fusion | flops 1073741824 | bytes 8650752 | tf_op jit(solution)/shard_map/dot_general | solution.py:22
  90.5 33.5 %all-to-all-done.1 = bf16[128,8,1536]{2,1,0:T(8,128)(2,1)S(1)} async-done(((bf16[128,8,1536]{2,1,0:T(8,128)(2,1)}), bf16[128,8,1536]{2,1,0:T(8,128)(2,1)S(1)}, u32[]{:S(2)}, u32[]{:S(2)}) %all-to-all-start.1) | async-done | bytes 3145760 | tf_op jit(solution)/shard_map/all_to_all | solution.py:18
  124.0 11.7 %tail.1 = bf16[256,512]{1,0:T(8,128)(2,1)} custom-call(bf16[1024,1536]{1,0:T(8,128)(2,1)S(1)} %bitcast.9, bf16[256,3072]{1,0:T(8,128)(2,1)} %copy-done, f32[256,4096]{1,0:T(8,128)} %fusion.pre_hbm, bf16[1024,4096]{1,0:T(8,128)(2,1)} %up_hbm.1, bf16[4096,512]{1,0:T(8,128)(2,1)} %down_hbm.1), custom_call_target="tpu_custom_call" | custom-call | tf_op jit(solution)/shard_map/tail/pallas_call | solution.py:278
  (1 shorter events, 0.0 us)
Async XLA Ops:
  0.0 0.9 copy-start.1
  1.0 0.7 copy-start.3
  5.5 11.5 %copy-start.5 = (s32[3,8,8]{2,1,0:T(8,128)S(1)}, s32[3,8,8]{2,1,0:T(8,128)}, u32[]{:S(2)}) copy-start(s32[3,8,8]{2,1,0:T(8,128)} %param.13) | copy-start | bytes 2308
  5.5 55.2 %all-to-all-start = ((bf16[128,8,1664]{2,1,0:T(8,128)(2,1)}), bf16[128,8,1664]{2,1,0:T(8,128)(2,1)S(1)}, u32[]{:S(2)}, u32[]{:S(2)}) async-start(bf16[128,8,1664]{2,1,0:T(8,128)(2,1)} %bitcast.11), calls=%async_computation | async-start | bytes 6815744 | tf_op jit(solution)/shard_map/all_to_all | solution.py:18
  76.8 6.1 %copy-start.4 = (s32[4,256]{1,0:T(4,128)S(1)}, s32[4,256]{1,0:T(4,128)}, u32[]{:S(2)}) copy-start(s32[4,256]{1,0:T(4,128)} %pos_ref.1) | copy-start | bytes 12292
  76.9 8.3 %copy-start.2 = (bf16[256,512]{1,0:T(8,128)(2,1)S(1)}, bf16[256,512]{1,0:T(8,128)(2,1)}, u32[]{:S(2)}) copy-start(bf16[256,512]{1,0:T(8,128)(2,1)} %feat_ref.1) | copy-start | bytes 786436
  76.9 47.2 %all-to-all-start.1 = ((bf16[128,8,1536]{2,1,0:T(8,128)(2,1)}), bf16[128,8,1536]{2,1,0:T(8,128)(2,1)S(1)}, u32[]{:S(2)}, u32[]{:S(2)}) async-start(bf16[128,8,1536]{2,1,0:T(8,128)(2,1)} %bitcast.12), calls=%async_computation.1 | async-start | bytes 6291456 | tf_op jit(solution)/shard_map/all_to_all | solution.py:18
  83.9 1.3 copy-start

commit v3 on v2

v3 whole, which is shorter than its diff:
```python
import functools

import jax
import jax.numpy as jnp
from jax import lax
from jax.experimental import pallas as pl
from jax.experimental.pallas import tpu as pltpu
from jax.sharding import PartitionSpec as P

BF = jnp.bfloat16
F32 = jnp.float32
VM = pl.BlockSpec(memory_space=pltpu.VMEM)
HB = pl.BlockSpec(memory_space=pltpu.HBM)
MIB = 1 << 20


def exchange(block):
    return lax.all_to_all(block, ("arrow", "blk"), split_axis=0, concat_axis=0, tiled=True)


def mm(a, b):
    return jnp.dot(a, b, preferred_element_type=F32)


def mm_nt(a, b):
    return lax.dot_general(a, b, (((1,), (1,)), ((), ())), preferred_element_type=F32)


def in_hbm(x):
    return pltpu.with_memory_space_constraint(x, pltpu.HBM)


def onehot(mask):
    return jnp.where(mask, 1.0, 0.0).astype(BF)


def pack_kernel(
    block_rows, width, feat_hbm, pos_hbm, out_hbm, feat_ref, pos_ref, out_ref, in_sem, out_sem
):
    nodes = feat_ref.shape[0]
    arrows = pos_ref.shape[0]
    rows = out_ref.shape[0] // arrows
    loads = (
        pltpu.make_async_copy(pos_hbm, pos_ref, in_sem.at[0]),
        pltpu.make_async_copy(feat_hbm, feat_ref, in_sem.at[1]),
    )
    for copy in loads:
        copy.start()
    n0 = lax.broadcasted_iota(jnp.int32, (nodes, nodes), 0)
    n1 = lax.broadcasted_iota(jnp.int32, (nodes, nodes), 1)
    before = onehot(n0 < n1)
    slot = lax.broadcasted_iota(jnp.int32, (rows, nodes), 0)
    r = slot % 8
    rf = r.astype(F32)
    shared = (r // 2 + 8).astype(F32)
    code_row = lax.broadcasted_iota(jnp.int32, (128, nodes), 0)
    for copy in loads:
        copy.wait()
    feats = feat_ref[...]

    def store(a):
        span = pl.ds(a * rows, rows)
        return pltpu.make_async_copy(out_ref.at[span, :], out_hbm.at[span, :], out_sem.at[a])

    for a in range(arrows):
        pos = pos_ref[a : a + 1, :]
        within = pos % block_rows
        member = pos // block_rows == slot // 8
        rank = jnp.where(member, mm(onehot(member), before), -1.0)
        head = jnp.broadcast_to(rank[0:1, :], rank.shape)
        picks = (
            onehot(rank == rf),
            onehot(jnp.where(r % 2 == 0, rank, head) == shared),
            onehot(head == rf),
        )
        high = (within // 32 + 1).astype(F32)
        low = (within % 32).astype(F32)
        span = pl.ds(a * rows, rows)
        codes = jnp.zeros((rows, 128), F32)
        for q in range(3):
            out_ref[span, q * width : (q + 1) * width] = mm(picks[q], feats).astype(BF)
            table = jnp.where(code_row == 2 * q, high, jnp.where(code_row == 2 * q + 1, low, 0.0))
            codes = codes + mm_nt(picks[q], table.astype(BF))
        out_ref[span, 3 * width :] = codes.astype(BF)
        store(a).start()
    for a in range(arrows):
        store(a).wait()


def prep_kernel(arrows, block_rows, width, pos_ref, feat_ref, w_ref, key_ref, pre_ref, up_ref):
    pre_ref[0] = mm(feat_ref[...], w_ref[:width, :]).astype(pre_ref.dtype)
    up_ref[0] = w_ref[width:, :]

    @pl.when(pl.program_id(0) == 0)
    def _():
        nodes = feat_ref.shape[0]
        n0 = lax.broadcasted_iota(jnp.int32, (nodes, nodes), 0)
        n1 = lax.broadcasted_iota(jnp.int32, (nodes, nodes), 1)
        before = onehot(n1 < n0)
        slot = lax.broadcasted_iota(jnp.int32, (nodes, 256), 1)
        lane = lax.broadcasted_iota(jnp.int32, (nodes, 128), 1)
        keys = jnp.zeros((nodes, 128), F32)
        for a in range(arrows):
            block = pos_ref[:, a : a + 1] // block_rows
            member = block == slot // 8
            rank = jnp.where(member & (slot % 8 == 0), mm(before, onehot(member)), 0.0)
            key = jnp.sum(rank, axis=1, keepdims=True) + (block * 16).astype(F32)
            keys = jnp.where(lane == a, key, keys)
        key_ref[...] = keys


def middle_kernel(
    width, got_ref, mask_ref, diag_hbm, col_hbm, row_hbm, out_hbm,
    w_ref, x_ref, x0_ref, y_ref, t_ref, p_ref, pt_ref, out_ref, s_ref, gm_ref, gh_ref, w_sem, out_sem,
):
    slots = got_ref.shape[0]
    size = x_ref.shape[0]
    half = slots // 2
    step = 256
    lanes = range(0, width, 128)
    loads = [
        pltpu.make_async_copy(src, w_ref.at[k], w_sem.at[k])
        for k, src in enumerate((diag_hbm, col_hbm, row_hbm))
    ]
    for copy in loads:
        copy.start()
    codes = got_ref[:, 3 * width :].astype(F32)
    place = (codes - 1.0) * 32.0 + pltpu.roll(codes, 127, 1)
    p_ref[0:slots, :] = place
    pt_ref[:, 0:slots] = place.T
    for j in lanes:
        s_ref[j // 128] = got_ref[:, width + j : width + j + 128].astype(F32)
    for k, ref in enumerate((gm_ref, gh_ref)):
        part = p_ref[pl.ds(k, half, stride=2), :]
        at = slots + k * half
        p_ref[at : at + half, :] = part
        pt_ref[:, at : at + half] = part.T
        for j in lanes:
            ref[:, j : j + 128] = s_ref[j // 128, pl.ds(k, half, stride=2), :].astype(BF)

    def unpack(c, carry):
        def put(row, start, count):
            ids = (lax.broadcasted_iota(jnp.int32, (step, count), 0) + c * step).astype(F32)
            return onehot(pt_ref[row : row + 1, start : start + count] == ids)

        span = pl.ds(pl.multiple_of(c * step, step), step)
        x_ref[span, :] = (
            mm(put(0, 0, slots), got_ref[:, 0:width]) + mm(put(2, slots, half), gm_ref[...])
        ).astype(BF)
        x0_ref[span, :] = (
            mm(put(4, 0, slots), got_ref[:, 2 * width : 3 * width])
            + mm(put(2, slots + half, half), gh_ref[...])
        ).astype(BF)
        return carry

    lax.fori_loop(0, size // step, unpack, 0)
    for copy in loads:
        copy.wait()
    tiles = mask_ref.shape[0] // 3
    edge = size // tiles
    for c in range(tiles):
        span = slice(c * edge, (c + 1) * edge)
        kept = []
        for k in range(3):
            keep = jnp.broadcast_to(mask_ref[k * tiles + c : k * tiles + c + 1, :], (edge, size))
            kept.append(w_ref[k, span, :] * keep.astype(BF))
        t_ref[span, :] = mm(kept[2], x_ref[...]).astype(BF)
        y_ref[span, :] = (mm(kept[0], x_ref[...]) + mm(kept[1], x0_ref[...])).astype(BF)

    def store(c):
        span = pl.ds(c * step, step)
        return pltpu.make_async_copy(out_ref.at[span, :], out_hbm.at[span, :], out_sem.at[c])

    for c in range(slots // step):
        span = slice(c * step, (c + 1) * step)

        def take(base, count, col):
            ids = lax.broadcasted_iota(jnp.int32, (count, size), 1).astype(F32)
            at = base + c * count
            return onehot(p_ref[at : at + count, col : col + 1] == ids)

        out_ref[span, 0:width] = mm(take(0, step, 0), y_ref[...]).astype(BF)
        even = mm(take(slots, step // 2, 2), y_ref[...])
        odd = mm(take(slots + half, step // 2, 2), t_ref[...])
        for j in lanes:
            s_ref[j // 128, pl.ds(0, step // 2, stride=2), :] = even[:, j : j + 128]
            s_ref[j // 128, pl.ds(1, step // 2, stride=2), :] = odd[:, j : j + 128]
            out_ref[span, width + j : width + j + 128] = s_ref[j // 128, 0:step, :].astype(BF)
        out_ref[span, 2 * width : 3 * width] = mm(take(0, step, 4), t_ref[...]).astype(BF)
        store(c).start()
    for c in range(slots // step):
        store(c).wait()


def tail_kernel(
    width, arrows, reply_ref, key_ref, pre_hbm, up_hbm, down_hbm, out_ref,
    pick_ref, pre_ref, up_ref, down_ref, agg_ref, acc_ref, sem,
):
    slots = reply_ref.shape[0]
    count, _, chunk = pre_ref.shape
    loads = []
    for c in range(count):
        span = pl.ds(c * chunk, chunk)
        loads.append(
            (
                pltpu.make_async_copy(up_hbm.at[c], up_ref.at[c], sem.at[0, c]),
                pltpu.make_async_copy(pre_hbm.at[c], pre_ref.at[c], sem.at[1, c]),
                pltpu.make_async_copy(down_hbm.at[span, :], down_ref.at[span, :], sem.at[2, c]),
            )
        )
        for copy in loads[c]:
            copy.start()
    rows = slots // arrows
    lane = lax.broadcasted_iota(jnp.int32, (1, rows), 1)
    block = lane // 8 * 16
    r = lane % 8
    goals = (block + r, jnp.where(r % 2 == 0, block, 0) + 8 + r // 2, r)
    total = jnp.zeros(agg_ref.shape, F32)
    for q in range(3):
        goal = goals[q].astype(F32)
        for a in range(arrows):
            pick_ref[:, a * rows : (a + 1) * rows] = onehot(key_ref[:, a : a + 1] == goal)
        total = total + mm(pick_ref[...], reply_ref[:, q * width : (q + 1) * width])
    agg_ref[...] = total.astype(BF)
    acc_ref[...] = jnp.zeros(acc_ref.shape, F32)
    for c in range(count):
        loads[c][0].wait()
        loads[c][1].wait()
        half = 0.5 * (pre_ref[c].astype(F32) + mm(agg_ref[...], up_ref[c]))
        hidden = (half * jnp.tanh(half) + half).astype(BF)
        loads[c][2].wait()
        acc_ref[...] += mm(hidden, down_ref[c * chunk : (c + 1) * chunk, :])
    out_ref[...] = acc_ref[...].astype(BF)


CHUNK = 1024
PRE = BF


def params(limit):
    return pltpu.CompilerParams(vmem_limit_bytes=limit * MIB)


def body(
    features, positions, diag_values, column_values, row_values, tile_masks, up_weight, down_weight
):
    row_count, width = features.shape
    arrows = positions.shape[0]
    devices = arrows * lax.axis_size("blk")
    size = diag_values.shape[0]
    hidden = down_weight.shape[0]
    tiles = tile_masks.shape[1]
    rows = devices * 8
    longest = 3 * width + 128
    count = hidden // CHUNK
    dma = pltpu.SemaphoreType.DMA

    message = pl.pallas_call(
        functools.partial(pack_kernel, size, width),
        in_specs=[HB, HB],
        out_specs=HB,
        out_shape=pltpu.HBM((rows, longest), BF),
        scratch_shapes=[
            pltpu.VMEM(features.shape, BF),
            pltpu.VMEM(positions.shape, jnp.int32),
            pltpu.VMEM((rows, longest), BF),
            dma((2,)),
            dma((arrows,)),
        ],
        compiler_params=params(24),
        name="pack",
    )(in_hbm(features), in_hbm(positions))
    got = exchange(message.reshape(devices, 8, longest)).reshape(rows, longest)

    key, pre, up = pl.pallas_call(
        functools.partial(prep_kernel, arrows, size, width),
        grid=(count,),
        in_specs=[
            pl.BlockSpec((row_count, arrows), lambda c: (0, 0)),
            pl.BlockSpec((row_count, width), lambda c: (0, 0)),
            pl.BlockSpec((2 * width, CHUNK), lambda c: (0, c)),
        ],
        out_specs=[
            pl.BlockSpec((row_count, 128), lambda c: (0, 0)),
            pl.BlockSpec((1, row_count, CHUNK), lambda c: (c, 0, 0)),
            pl.BlockSpec((1, width, CHUNK), lambda c: (c, 0, 0)),
        ],
        out_shape=[
            jax.ShapeDtypeStruct((row_count, 128), F32),
            pltpu.HBM((count, row_count, CHUNK), PRE),
            pltpu.HBM((count, width, CHUNK), BF),
        ],
        compiler_params=params(20),
        name="prep",
    )(positions.T, in_hbm(features), in_hbm(up_weight))
    keep = jnp.repeat(tile_masks.astype(F32), size // tiles, axis=2).reshape(3 * tiles, size)

    reply = pl.pallas_call(
        functools.partial(middle_kernel, width),
        in_specs=[VM, VM, HB, HB, HB],
        out_specs=HB,
        out_shape=pltpu.HBM((rows, 3 * width), BF),
        scratch_shapes=[pltpu.VMEM((3, size, size), BF)]
        + [pltpu.VMEM((size, width), BF)] * 4
        + [
            pltpu.VMEM((2 * rows, 128), F32),
            pltpu.VMEM((128, 2 * rows), F32),
            pltpu.VMEM((rows, 3 * width), BF),
            pltpu.VMEM((width // 128, rows, 128), F32),
            pltpu.VMEM((rows // 2, width), BF),
            pltpu.VMEM((rows // 2, width), BF),
            dma((3,)),
            dma((rows // 256,)),
        ],
        compiler_params=params(40),
        name="middle",
    )(got, keep, in_hbm(diag_values), in_hbm(column_values), in_hbm(row_values))
    reply = exchange(reply.reshape(devices, 8, 3 * width)).reshape(rows, 3 * width)

    return pl.pallas_call(
        functools.partial(tail_kernel, width, arrows),
        in_specs=[VM, VM, HB, HB, HB],
        out_specs=VM,
        out_shape=jax.ShapeDtypeStruct((row_count, width), BF),
        scratch_shapes=[
            pltpu.VMEM((row_count, rows), BF),
            pltpu.VMEM((count, row_count, CHUNK), PRE),
            pltpu.VMEM((count, width, CHUNK), BF),
            pltpu.VMEM((hidden, width), BF),
            pltpu.VMEM((row_count, width), BF),
            pltpu.VMEM((row_count, width), F32),
            dma((3, count)),
        ],
        compiler_params=params(40),
        name="tail",
    )(reply, key, in_hbm(pre), in_hbm(up), in_hbm(down_weight))


def solution(mesh):
    in_specs = (
        P(("arrow", "blk"), None),
        P(None, ("arrow", "blk")),
        P("arrow", "blk"),
        P("arrow", "blk"),
        P("arrow", "blk"),
        P(None, "arrow", "blk"),
        P(),
        P(),
    )
    out_specs = P(("arrow", "blk"), None)
    return jax.shard_map(body, mesh=mesh, in_specs=in_specs, out_specs=out_specs, check_vma=False)
```

time: 136 us -> 126 us (0.926)
  matrix products: 5.39 us -> 0 us
  local copies, waits for them, and re-layouts: 3.19 us -> 0.3 us
    dot_general x1 -> x0, matrix products: 5.39 us -> none  [mm(): return jnp.dot(a, b, preferred_element_type=F32)]
    pallas_call x1, Pallas kernels: 16.1 us -> 12.4 us  [body(): pl.pallas_call(functools.partial(middle_kernel, width), in_specs=[VM, VM,...]
    unnamed x13 -> x5, local copies, waits for them, and re-layouts: 3.04 us -> 0.15 us
    pallas_call x3, Pallas kernels: 16.3 us -> 18.6 us  [the longest x1 8.36 us: body(): pl.pallas_call(functools.partial(prep_kernel, arrows, size, width), grid=...]
  transfers between devices with their start and end apart: 2 -> 2, of which waited for: 2 -> 2; matrix products, arithmetic and copies ran while one was open for 4% -> 0% of each run, Pallas kernels for 1% -> 7%
where the time goes in v3:
time: 126 us; the launch traced here: 125 us
  waiting for transfers between devices  76.1 us (60%)
  Pallas kernels  31.1 us (25%)
  starting transfers between devices  17.6 us (14%)
    all_to_all x2, waiting for transfers between devices, exchange(): lax.all_to_all(block, ('arrow', 'blk'), split_axis=0, concat_axis=0, tile...  76.1 us
    all_to_all x2, starting transfers between devices, exchange(): lax.all_to_all(block, ('arrow', 'blk'), split_axis=0, concat_axis=0, tile...  17.6 us
    pallas_call x1, Pallas kernels, body(): pl.pallas_call(functools.partial(middle_kernel, width), in_specs=[VM, VM,...  12.4 us
    pallas_call x1, Pallas kernels, body(): pl.pallas_call(functools.partial(prep_kernel, arrows, size, width), grid=...  8.36 us
    pallas_call x1, Pallas kernels, body(): pl.pallas_call(functools.partial(tail_kernel, width, arrows), in_specs=[V...  6.41 us
    pallas_call x1, Pallas kernels, body(): pl.pallas_call(functools.partial(pack_kernel, size, width), in_specs=[HB,...  3.87 us
  transfers between devices with their start and end apart: 2, of which 2 were waited for; matrix products, arithmetic and copies ran while one was open for 0% of the time, Pallas kernels for 7%

profile of v3, /device:TPU:1, one launch (start us, length us, event | category | flops | bytes accessed | tf_op | source)
XLA Modules:
  0.0 125.3 jit_solution(2074025361049530201)
XLA Ops:
  0.0 3.9 %pack.1 = bf16[1024,1664]{1,0:T(8,128)(2,1)} custom-call(bf16[256,512]{1,0:T(8,128)(2,1)} %feat_ref.1, s32[4,256]{1,0:T(4,128)} %pos_hbm.1), custom_call_target="tpu_custom_call" | custom-call | tf_op jit(solution)/shard_map/pack/pallas_call | solution.py:258
  3.9 0.0 copy-start.1
  3.9 11.5 %all-to-all-start = ((bf16[128,8,1664]{2,1,0:T(8,128)(2,1)}), bf16[128,8,1664]{2,1,0:T(8,128)(2,1)S(1)}, u32[]{:S(2)}, u32[]{:S(2)}) async-start(bf16[128,8,1664]{2,1,0:T(8,128)(2,1)} %bitcast.10), calls=%async_computation | async-start | bytes 6815744 | tf_op jit(solution)/shard_map/all_to_all | solution.py:18
  15.4 0.0 copy-done.1
  15.4 0.1 copy.9
  15.5 0.1 broadcast_bitcast_fusion.mask_ref
  15.6 43.6 %all-to-all-done = bf16[128,8,1664]{2,1,0:T(8,128)(2,1)S(1)} async-done(((bf16[128,8,1664]{2,1,0:T(8,128)(2,1)}), bf16[128,8,1664]{2,1,0:T(8,128)(2,1)S(1)}, u32[]{:S(2)}, u32[]{:S(2)}) %all-to-all-start) | async-done | bytes 3407904 | tf_op jit(solution)/shard_map/all_to_all | solution.py:18
  59.1 12.4 %middle.1 = bf16[1024,1536]{1,0:T(8,128)(2,1)} custom-call(bf16[1024,1664]{1,0:T(8,128)(2,1)S(1)} %bitcast.7, f32[24,1024]{1,0:T(8,128)S(1)} %broadcast_bitcast_fusion.mask_ref, bf16[1024,1024]{1,0:T(8,128)(2,1)} %diag_hbm.1, bf16[1024,1024]{1,0:T(8,128)(2,1)} %col_hbm.1, bf16[1024,1024]{1,0:T(8,128)(2,1)} %row_hbm.1), custom_call_target="tpu_custom_call" | custom-call | tf_op jit(solution)/shard_map/middle/pallas_call | solution.py:298
  71.6 0.0 copy-start
  71.6 6.1 %all-to-all-start.1 = ((bf16[128,8,1536]{2,1,0:T(8,128)(2,1)}), bf16[128,8,1536]{2,1,0:T(8,128)(2,1)S(1)}, u32[]{:S(2)}, u32[]{:S(2)}) async-start(bf16[128,8,1536]{2,1,0:T(8,128)(2,1)} %bitcast.11), calls=%async_computation.1 | async-start | bytes 6291456 | tf_op jit(solution)/shard_map/all_to_all | solution.py:18
  77.7 0.0 copy-done
  77.7 0.1 copy.10
  77.9 8.4 %prep.1 = (f32[256,128]{1,0:T(8,128)S(1)}, bf16[4,256,1024]{2,1,0:T(8,128)(2,1)}, bf16[4,512,1024]{2,1,0:T(8,128)(2,1)}) custom-call(s32[256,4]{1,0:T(8,128)S(1)} %bitcast.9, bf16[256,512]{1,0:T(8,128)(2,1)} %feat_ref.1, bf16[1024,4096]{1,0:T(8,128)(2,1)} %w_ref.1), custom_call_target="tpu_custom_call" | custom-call | tf_op jit(solution)/shard_map/prep/pallas_call | solution.py:275
  86.2 32.5 %all-to-all-done.1 = bf16[128,8,1536]{2,1,0:T(8,128)(2,1)S(1)} async-done(((bf16[128,8,1536]{2,1,0:T(8,128)(2,1)}), bf16[128,8,1536]{2,1,0:T(8,128)(2,1)S(1)}, u32[]{:S(2)}, u32[]{:S(2)}) %all-to-all-start.1) | async-done | bytes 3145760 | tf_op jit(solution)/shard_map/all_to_all | solution.py:18
  118.8 6.4 %tail.1 = bf16[256,512]{1,0:T(8,128)(2,1)} custom-call(bf16[1024,1536]{1,0:T(8,128)(2,1)S(1)} %bitcast.8, f32[256,128]{1,0:T(8,128)S(1)} %get-tuple-element.8.key_ref, bf16[4,256,1024]{2,1,0:T(8,128)(2,1)} %get-tuple-element.9.pre_hbm, bf16[4,512,1024]{2,1,0:T(8,128)(2,1)} %get-tuple-element.10.up_hbm, bf16[4096,512]{1,0:T(8,128)(2,1)} %down_hbm.1), custom_call_target="tpu_custom_call" | custom-call | tf_op jit(solution)/shard_map/tail/pallas_call | solution.py:320
  (1 shorter events, 0.0 us)
Async XLA Ops:
  3.9 11.5 %copy-start.1 = (s32[3,8,8]{2,1,0:T(8,128)S(1)}, s32[3,8,8]{2,1,0:T(8,128)}, u32[]{:S(2)}) copy-start(s32[3,8,8]{2,1,0:T(8,128)} %param.13) | copy-start | bytes 2308
  3.9 55.2 %all-to-all-start = ((bf16[128,8,1664]{2,1,0:T(8,128)(2,1)}), bf16[128,8,1664]{2,1,0:T(8,128)(2,1)S(1)}, u32[]{:S(2)}, u32[]{:S(2)}) async-start(bf16[128,8,1664]{2,1,0:T(8,128)(2,1)} %bitcast.10), calls=%async_computation | async-start | bytes 6815744 | tf_op jit(solution)/shard_map/all_to_all | solution.py:18
  71.6 6.2 %copy-start = (s32[4,256]{1,0:T(4,128)S(1)}, s32[4,256]{1,0:T(4,128)}, u32[]{:S(2)}) copy-start(s32[4,256]{1,0:T(4,128)} %pos_hbm.1) | copy-start | bytes 12292
  71.6 47.2 %all-to-all-start.1 = ((bf16[128,8,1536]{2,1,0:T(8,128)(2,1)}), bf16[128,8,1536]{2,1,0:T(8,128)(2,1)S(1)}, u32[]{:S(2)}, u32[]{:S(2)}) async-start(bf16[128,8,1536]{2,1,0:T(8,128)(2,1)} %bitcast.11), calls=%async_computation.1 | async-start | bytes 6291456 | tf_op jit(solution)/shard_map/all_to_all | solution.py:18

commit v4 on v3

--- a/solution.py
+++ b/solution.py
@@ -53,7 +53,6 @@
     r = slot % 8
     rf = r.astype(F32)
     shared = (r // 2 + 8).astype(F32)
-    code_row = lax.broadcasted_iota(jnp.int32, (128, nodes), 0)
     for copy in loads:
         copy.wait()
     feats = feat_ref[...]
@@ -63,9 +62,7 @@
         return pltpu.make_async_copy(out_ref.at[span, :], out_hbm.at[span, :], out_sem.at[a])
 
     for a in range(arrows):
-        pos = pos_ref[a : a + 1, :]
-        within = pos % block_rows
-        member = pos // block_rows == slot // 8
+        member = pos_ref[a : a + 1, :] // block_rows == slot // 8
         rank = jnp.where(member, mm(onehot(member), before), -1.0)
         head = jnp.broadcast_to(rank[0:1, :], rank.shape)
         picks = (
@@ -73,18 +70,59 @@
             onehot(jnp.where(r % 2 == 0, rank, head) == shared),
             onehot(head == rf),
         )
-        high = (within // 32 + 1).astype(F32)
-        low = (within % 32).astype(F32)
-        span = pl.ds(a * rows, rows)
-        codes = jnp.zeros((rows, 128), F32)
         for q in range(3):
-            out_ref[span, q * width : (q + 1) * width] = mm(picks[q], feats).astype(BF)
-            table = jnp.where(code_row == 2 * q, high, jnp.where(code_row == 2 * q + 1, low, 0.0))
-            codes = codes + mm_nt(picks[q], table.astype(BF))
-        out_ref[span, 3 * width :] = codes.astype(BF)
+            out_ref[a * rows : (a + 1) * rows, q * width : (q + 1) * width] = mm(
+                picks[q], feats
+            ).astype(BF)
         store(a).start()
     for a in range(arrows):
         store(a).wait()
+
+
+def places_kernel(blocks, block_rows, me_ref, table_ref, p_ref, pt_ref):
+    sources, nodes = table_ref.shape
+    slots = sources * 8
+    half = slots // 2
+    arrows = sources // blocks
+    step = 256
+    arrow = me_ref[0]
+    block = me_ref[1]
+    high = (table_ref[...] // 256).astype(F32).astype(BF)
+    low = (table_ref[...] % 256).astype(F32).astype(BF)
+    n0 = lax.broadcasted_iota(jnp.int32, (nodes, nodes), 0)
+    n1 = lax.broadcasted_iota(jnp.int32, (nodes, nodes), 1)
+    before = onehot(n0 < n1)
+
+    def fill(c, carry):
+        row = lax.broadcasted_iota(jnp.int32, (step, sources), 0) + c * step
+        source = row // 8
+        wanted = ((source % blocks) ^ block) * arrows + ((source // blocks) ^ arrow)
+        spread = onehot(lax.broadcasted_iota(jnp.int32, (step, sources), 1) == wanted)
+        pos = (mm(spread, high) * 256.0 + mm(spread, low)).astype(jnp.int32)
+        r = lax.broadcasted_iota(jnp.int32, (step, nodes), 0) % 8
+        rf = r.astype(F32)
+        shared = (r // 2 + 8).astype(F32)
+        within = (pos % block_rows + 1).astype(F32)
+        member = pos // block_rows == block
+        rank = jnp.where(member, mm(onehot(member), before), -1.0)
+        member = pos // block_rows == 0
+        head = jnp.where(member, mm(onehot(member), before), -1.0)
+        lane = lax.broadcasted_iota(jnp.int32, (step, 128), 1)
+        place = jnp.zeros((step, 128), F32)
+        hits = (rank == rf, jnp.where(r % 2 == 0, rank, head) == shared, head == rf)
+        for q in range(3):
+            at = jnp.sum(jnp.where(hits[q], within, 0.0), axis=1, keepdims=True) - 1.0
+            place = jnp.where(lane == 2 * q, at, place)
+        p_ref[pl.ds(pl.multiple_of(c * step, step), step), :] = place
+        return carry
+
+    lax.fori_loop(0, slots // step, fill, 0)
+    pt_ref[:, 0:slots] = p_ref[0:slots, :].T[0:8, :]
+    for k in range(2):
+        part = p_ref[pl.ds(k, half, stride=2), :]
+        at = slots + k * half
+        p_ref[at : at + half, :] = part
+        pt_ref[:, at : at + half] = part.T[0:8, :]
 
 
 def prep_kernel(arrows, block_rows, width, pos_ref, feat_ref, w_ref, key_ref, pre_ref, up_ref):
@@ -110,8 +148,8 @@
 
 
 def middle_kernel(
-    width, got_ref, mask_ref, diag_hbm, col_hbm, row_hbm, out_hbm,
-    w_ref, x_ref, x0_ref, y_ref, t_ref, p_ref, pt_ref, out_ref, s_ref, gm_ref, gh_ref, w_sem, out_sem,
+    width, got_ref, pt_ref, mask_ref, p_hbm, diag_hbm, col_hbm, row_hbm, out_hbm,
+    w_ref, x_ref, x0_ref, y_ref, t_ref, p_ref, out_ref, s_ref, gm_ref, gh_ref, w_sem, p_sem, out_sem,
 ):
     slots = got_ref.shape[0]
     size = x_ref.shape[0]
@@ -122,19 +160,12 @@
         pltpu.make_async_copy(src, w_ref.at[k], w_sem.at[k])
         for k, src in enumerate((diag_hbm, col_hbm, row_hbm))
     ]
+    loads.append(pltpu.make_async_copy(p_hbm, p_ref, p_sem))
     for copy in loads:
         copy.start()
-    codes = got_ref[:, 3 * width :].astype(F32)
-    place = (codes - 1.0) * 32.0 + pltpu.roll(codes, 127, 1)
-    p_ref[0:slots, :] = place
-    pt_ref[:, 0:slots] = place.T
     for j in lanes:
         s_ref[j // 128] = got_ref[:, width + j : width + j + 128].astype(F32)
     for k, ref in enumerate((gm_ref, gh_ref)):
-        part = p_ref[pl.ds(k, half, stride=2), :]
-        at = slots + k * half
-        p_ref[at : at + half, :] = part
-        pt_ref[:, at : at + half] = part.T
         for j in lanes:
             ref[:, j : j + 128] = s_ref[j // 128, pl.ds(k, half, stride=2), :].astype(BF)
 
@@ -237,6 +268,31 @@
 PRE = BF
 
 
+def gather_positions(positions):
+    arrows = positions.shape[0]
+    blocks = lax.axis_size("blk")
+    mine = lax.axis_index("arrow")
+
+    def partner(x, axis, size, k):
+        return lax.ppermute(x, axis, [(i, i ^ k) for i in range(size)])
+
+    def pick(row):
+        return lax.dynamic_slice_in_dim(positions, row, 1, 0)
+
+    parts = [pick(mine)]
+    for k in range(1, arrows):
+        parts.append(partner(pick(mine ^ k), "arrow", arrows, k))
+    table = jnp.concatenate(parts, axis=0)
+    base = 1
+    while base < blocks:
+        fan = 2 if base == 1 else 4
+        table = jnp.concatenate(
+            [table] + [partner(table, "blk", blocks, base * k) for k in range(1, fan)], axis=0
+        )
+        base *= fan
+    return table
+
+
 def params(limit):
     return pltpu.CompilerParams(vmem_limit_bytes=limit * MIB)
 
@@ -251,7 +307,7 @@
     hidden = down_weight.shape[0]
     tiles = tile_masks.shape[1]
     rows = devices * 8
-    longest = 3 * width + 128
+    longest = 3 * width
     count = hidden // CHUNK
     dma = pltpu.SemaphoreType.DMA
 
@@ -272,6 +328,17 @@
     )(in_hbm(features), in_hbm(positions))
     got = exchange(message.reshape(devices, 8, longest)).reshape(rows, longest)
 
+    table = gather_positions(lax.optimization_barrier((positions, message))[0])
+    me = jnp.stack([lax.axis_index("arrow"), lax.axis_index("blk")]).astype(jnp.int32)
+    places, places_t = pl.pallas_call(
+        functools.partial(places_kernel, devices // arrows, size),
+        in_specs=[pl.BlockSpec(memory_space=pltpu.SMEM), VM],
+        out_specs=[pl.BlockSpec((2 * rows, 128)), VM],
+        out_shape=[pltpu.HBM((2 * rows, 128), F32), jax.ShapeDtypeStruct((8, 2 * rows), F32)],
+        compiler_params=params(16),
+        name="places",
+    )(me, table)
+
     key, pre, up = pl.pallas_call(
         functools.partial(prep_kernel, arrows, size, width),
         grid=(count,),
@@ -297,24 +364,24 @@
 
     reply = pl.pallas_call(
         functools.partial(middle_kernel, width),
-        in_specs=[VM, VM, HB, HB, HB],
+        in_specs=[VM, VM, VM, HB, HB, HB, HB],
         out_specs=HB,
         out_shape=pltpu.HBM((rows, 3 * width), BF),
         scratch_shapes=[pltpu.VMEM((3, size, size), BF)]
         + [pltpu.VMEM((size, width), BF)] * 4
         + [
             pltpu.VMEM((2 * rows, 128), F32),
-            pltpu.VMEM((128, 2 * rows), F32),
             pltpu.VMEM((rows, 3 * width), BF),
             pltpu.VMEM((width // 128, rows, 128), F32),
             pltpu.VMEM((rows // 2, width), BF),
             pltpu.VMEM((rows // 2, width), BF),
             dma((3,)),
+            dma,
             dma((rows // 256,)),
         ],
         compiler_params=params(40),
         name="middle",
-    )(got, keep, in_hbm(diag_values), in_hbm(column_values), in_hbm(row_values))
+    )(got, places_t, keep, in_hbm(places), in_hbm(diag_values), in_hbm(column_values), in_hbm(row_values))
     reply = exchange(reply.reshape(devices, 8, 3 * width)).reshape(rows, 3 * width)
 
     return pl.pallas_call(

time: 126 us -> 147 us (1.17)
  starting transfers between devices: 17.6 us -> 66.2 us
  waiting for transfers between devices: 76.1 us -> 43.5 us
  Pallas kernels: 31.1 us -> 35.2 us
    all_to_all x2, waiting for transfers between devices: 76.1 us -> 32.5 us  [exchange(): lax.all_to_all(block, ('arrow', 'blk'), split_axis=0, concat_axis=0, tile...]
    ppermute x0 -> x10, starting transfers between devices: none -> 43.2 us  [partner(): return lax.ppermute(x, axis, [(i, i ^ k) for i in range(size)])]
    ppermute x0 -> x10, waiting for transfers between devices: none -> 11 us  [partner(): return lax.ppermute(x, axis, [(i, i ^ k) for i in range(size)])]
    all_to_all x2, starting transfers between devices: 17.6 us -> 23 us  [exchange(): lax.all_to_all(block, ('arrow', 'blk'), split_axis=0, concat_axis=0, tile...]
    pallas_call x0 -> x1, Pallas kernels: none -> 4.93 us  [body(): pl.pallas_call(functools.partial(places_kernel, devices // arrows, size),...]
  transfers between devices with their start and end apart: 2 -> 12, of which waited for: 2 -> 8; matrix products, arithmetic and copies ran while one was open for 0% -> 1% of each run, Pallas kernels for 7% -> 9%
where the time goes in v4:
time: 147 us; the launch traced here: 146 us
  starting transfers between devices  66.2 us (45%)
  waiting for transfers between devices  43.5 us (30%)
  Pallas kernels  35.2 us (24%)
    ppermute x10, starting transfers between devices, partner(): return lax.ppermute(x, axis, [(i, i ^ k) for i in range(size)])  43.2 us
    all_to_all x2, waiting for transfers between devices, exchange(): lax.all_to_all(block, ('arrow', 'blk'), split_axis=0, concat_axis=0, tile...  32.5 us
    all_to_all x2, starting transfers between devices, exchange(): lax.all_to_all(block, ('arrow', 'blk'), split_axis=0, concat_axis=0, tile...  23 us
    pallas_call x1, Pallas kernels, body(): pl.pallas_call(functools.partial(middle_kernel, width), in_specs=[VM, VM,...  12 us
    ppermute x10, waiting for transfers between devices, partner(): return lax.ppermute(x, axis, [(i, i ^ k) for i in range(size)])  11 us
    pallas_call x1, Pallas kernels, body(): pl.pallas_call(functools.partial(prep_kernel, arrows, size, width), grid=...  8.35 us
    pallas_call x1, Pallas kernels, body(): pl.pallas_call(functools.partial(tail_kernel, width, arrows), in_specs=[V...  6.41 us
    pallas_call x1, Pallas kernels, body(): pl.pallas_call(functools.partial(places_kernel, devices // arrows, size),...  4.93 us
  transfers between devices with their start and end apart: 12, of which 8 were waited for; matrix products, arithmetic and copies ran while one was open for 1% of the time, Pallas kernels for 9%

profile of v4, /device:TPU:1, one launch (start us, length us, event | category | flops | bytes accessed | tf_op | source)
XLA Modules:
  0.0 146.4 jit_solution(2088178863927632701)
XLA Ops:
  0.0 3.5 %pack.1 = bf16[1024,1536]{1,0:T(8,128)(2,1)} custom-call(bf16[256,512]{1,0:T(8,128)(2,1)} %feat_ref.1, s32[4,256]{1,0:T(4,128)} %pos_hbm.1), custom_call_target="tpu_custom_call" | custom-call | tf_op jit(solution)/shard_map/pack/pallas_call | solution.py:314
  3.5 0.0 copy-start
  3.5 0.0 copy-start.2
  3.5 11.5 %all-to-all-start = ((bf16[128,8,1536]{2,1,0:T(8,128)(2,1)}), bf16[128,8,1536]{2,1,0:T(8,128)(2,1)S(1)}, u32[]{:S(2)}, u32[]{:S(2)}) async-start(bf16[128,8,1536]{2,1,0:T(8,128)(2,1)} %bitcast.12), calls=%async_computation | async-start | bytes 6291456 | tf_op jit(solution)/shard_map/all_to_all | solution.py:18
  15.0 0.0 copy-done
  15.0 1.8 %collective-permute-start.2 = (s32[1,256]{1,0:T(1,128)S(1)}, s32[1,256]{1,0:T(1,128)S(1)}, u32[]{:S(2)}, u32[]{:S(2)}) collective-permute-start(s32[1,256]{1,0:T(1,128)S(1)} %get-tuple-element.17), channel_id=1, source_target_pairs={{0,96},{32,64},{64,32},{96,0},{1,97},{33,65},{65,33},{97,1},{2,98}... | collective-permute-start | bytes 3080 | tf_op jit(solution)/shard_map/ppermute | solution.py:277
  16.9 0.7 collective-permute-start.1
  17.5 0.0 collective-permute-start
  17.5 2.0 %collective-permute-done.2 = s32[1,256]{1,0:T(1,128)S(1)} collective-permute-done((s32[1,256]{1,0:T(1,128)S(1)}, s32[1,256]{1,0:T(1,128)S(1)}, u32[]{:S(2)}, u32[]{:S(2)}) %collective-permute-start.2) | collective-permute-done | bytes 1056 | tf_op jit(solution)/shard_map/ppermute | solution.py:277
  19.5 0.2 collective-permute-done.1
  19.7 0.0 collective-permute-done
  19.7 0.0 copy-start.1
  19.7 4.3 %collective-permute-start.3 = (s32[4,256]{1,0:T(4,128)S(1)}, s32[4,256]{1,0:T(4,128)S(1)}, u32[]{:S(2)}, u32[]{:S(2)}) collective-permute-start(s32[4,256]{1,0:T(4,128)S(1)} %pad_add_fusion), channel_id=1, source_target_pairs={{0,1},{1,0},{2,3},{3,2},{4,5},{5,4},{6,7},{7,6},{8,9},{9,8},{10,11... | collective-permute-start | bytes 12296 | tf_op jit(solution)/shard_map/ppermute | solution.py:277
  24.0 0.0 copy-done.2
  24.0 0.1 copy.9
  24.1 2.4 %collective-permute-done.3 = s32[4,256]{1,0:T(4,128)S(1)} collective-permute-done((s32[4,256]{1,0:T(4,128)S(1)}, s32[4,256]{1,0:T(4,128)S(1)}, u32[]{:S(2)}, u32[]{:S(2)}) %collective-permute-start.3) | collective-permute-done | bytes 4128 | tf_op jit(solution)/shard_map/ppermute | solution.py:277
  26.5 26.9 %collective-permute-start.6 = (s32[8,256]{1,0:T(8,128)S(1)}, s32[8,256]{1,0:T(8,128)S(1)}, u32[]{:S(2)}, u32[]{:S(2)}) collective-permute-start(s32[8,256]{1,0:T(8,128)S(1)} %concatenate.16), channel_id=1, source_target_pairs={{0,6},{1,7},{2,4},{3,5},{4,2},{5,3},{6,0},{7,1},{8,14},{9,15},{10,... | collective-permute-start | bytes 24584 | tf_op jit(solution)/shard_map/ppermute | solution.py:277
  53.4 0.0 collective-permute-start.5
  53.4 0.7 collective-permute-start.4
  54.1 0.1 broadcast_bitcast_fusion.mask_ref
  54.1 0.6 collective-permute-done.6
  54.7 2.7 %collective-permute-done.5 = s32[8,256]{1,0:T(8,128)S(1)} collective-permute-done((s32[8,256]{1,0:T(8,128)S(1)}, s32[8,256]{1,0:T(8,128)S(1)}, u32[]{:S(2)}, u32[]{:S(2)}) %collective-permute-start.5) | collective-permute-done | bytes 8224 | tf_op jit(solution)/shard_map/ppermute | solution.py:277
  57.4 0.0 collective-permute-done.4
  57.4 0.0 copy-done.1
  57.4 7.8 %collective-permute-start.9 = (s32[32,256]{1,0:T(8,128)S(1)}, s32[32,256]{1,0:T(8,128)S(1)}, u32[]{:S(2)}, u32[]{:S(2)}) collective-permute-start(s32[32,256]{1,0:T(8,128)S(1)} %concatenate.17), channel_id=1, source_target_pairs={{0,24},{1,25},{2,26},{3,27},{4,28},{5,29},{6,30},{7,31},{8,16},{9,... | collective-permute-start | bytes 98312 | tf_op jit(solution)/shard_map/ppermute | solution.py:277
  65.2 1.1 collective-permute-start.8
  66.3 0.0 collective-permute-start.7
  66.3 0.1 pad_add_fusion.1.me_ref
  66.3 0.2 collective-permute-done.9
  66.5 3.0 %collective-permute-done.8 = s32[32,256]{1,0:T(8,128)S(1)} collective-permute-done((s32[32,256]{1,0:T(8,128)S(1)}, s32[32,256]{1,0:T(8,128)S(1)}, u32[]{:S(2)}, u32[]{:S(2)}) %collective-permute-start.8) | collective-permute-done | bytes 32800 | tf_op jit(solution)/shard_map/ppermute | solution.py:277
  69.5 0.0 collective-permute-done.7
  69.5 0.7 concatenate.18.table_ref
  70.2 4.9 %places.1 = (f32[2048,128]{1,0:T(8,128)}, f32[8,2048]{1,0:T(8,128)S(1)}) custom-call(s32[2]{0:T(128)S(1)} %pad_add_fusion.1.me_ref, s32[128,256]{1,0:T(8,128)S(1)} %concatenate.18.table_ref), custom_call_target="tpu_custom_call" | custom-call | tf_op jit(solution)/shard_map/places/pallas_call | solution.py:333
  75.1 0.0 all-to-all-done
  75.1 12.0 %middle.1 = bf16[1024,1536]{1,0:T(8,128)(2,1)} custom-call(bf16[1024,1536]{1,0:T(8,128)(2,1)S(1)} %bitcast.9, f32[8,2048]{1,0:T(8,128)S(1)} %get-tuple-element.12.pt_ref, f32[24,1024]{1,0:T(8,128)S(1)} %broadcast_bitcast_fusion.mask_ref, f32[2048,128]{1,0:T(8,128)} %get-tuple-element.13.p_hbm, bf16[1024,1024]{1,0:T(8,128)(2,1)} %diag_hbm.1, ...), custom_call_target="tpu_custom_call" | custom-call | tf_op jit(solution)/shard_map/middle/pallas_call | solution.py:365
  87.2 11.5 %all-to-all-start.1 = ((bf16[128,8,1536]{2,1,0:T(8,128)(2,1)}), bf16[128,8,1536]{2,1,0:T(8,128)(2,1)S(1)}, u32[]{:S(2)}, u32[]{:S(2)}) async-start(bf16[128,8,1536]{2,1,0:T(8,128)(2,1)} %bitcast.13), calls=%async_computation.1 | async-start | bytes 6291456 | tf_op jit(solution)/shard_map/all_to_all | solution.py:18
  98.7 0.1 copy.10
  98.9 8.4 %prep.1 = (f32[256,128]{1,0:T(8,128)S(1)}, bf16[4,256,1024]{2,1,0:T(8,128)(2,1)}, bf16[4,512,1024]{2,1,0:T(8,128)(2,1)}) custom-call(s32[256,4]{1,0:T(8,128)S(1)} %bitcast.11, bf16[256,512]{1,0:T(8,128)(2,1)} %feat_ref.1, bf16[1024,4096]{1,0:T(8,128)(2,1)} %w_ref.1), custom_call_target="tpu_custom_call" | custom-call | tf_op jit(solution)/shard_map/prep/pallas_call | solution.py:342
  107.2 32.5 %all-to-all-done.1 = bf16[128,8,1536]{2,1,0:T(8,128)(2,1)S(1)} async-done(((bf16[128,8,1536]{2,1,0:T(8,128)(2,1)}), bf16[128,8,1536]{2,1,0:T(8,128)(2,1)S(1)}, u32[]{:S(2)}, u32[]{:S(2)}) %all-to-all-start.1) | async-done | bytes 3145760 | tf_op jit(solution)/shard_map/all_to_all | solution.py:18
  139.8 6.4 %tail.1 = bf16[256,512]{1,0:T(8,128)(2,1)} custom-call(bf16[1024,1536]{1,0:T(8,128)(2,1)S(1)} %bitcast.10, f32[256,128]{1,0:T(8,128)S(1)} %get-tuple-element.14.key_ref, bf16[4,256,1024]{2,1,0:T(8,128)(2,1)} %get-tuple-element.15.pre_hbm, bf16[4,512,1024]{2,1,0:T(8,128)(2,1)} %get-tuple-element.16.up_hbm, bf16[4096,512]{1,0:T(8,128)(2,1)} %down_hbm.1), custom_call_target="tpu_custom_call" | custom-call | tf_op jit(solution)/shard_map/tail/pallas_call | solution.py:387
  (5 shorter events, 0.1 us)
Async XLA Ops:
  3.5 11.5 %copy-start = (s32[4,256]{1,0:T(4,128)S(1)}, s32[4,256]{1,0:T(4,128)}, u32[]{:S(2)}) copy-start(s32[4,256]{1,0:T(4,128)} %pos_hbm.1) | copy-start | bytes 12292
  3.5 20.5 %copy-start.2 = (s32[3,8,8]{2,1,0:T(8,128)S(1)}, s32[3,8,8]{2,1,0:T(8,128)}, u32[]{:S(2)}) copy-start(s32[3,8,8]{2,1,0:T(8,128)} %param.13) | copy-start | bytes 2308
  3.5 71.6 %all-to-all-start = ((bf16[128,8,1536]{2,1,0:T(8,128)(2,1)}), bf16[128,8,1536]{2,1,0:T(8,128)(2,1)S(1)}, u32[]{:S(2)}, u32[]{:S(2)}) async-start(bf16[128,8,1536]{2,1,0:T(8,128)(2,1)} %bitcast.12), calls=%async_computation | async-start | bytes 6291456 | tf_op jit(solution)/shard_map/all_to_all | solution.py:18
  15.0 4.5 %collective-permute-start.2 = (s32[1,256]{1,0:T(1,128)S(1)}, s32[1,256]{1,0:T(1,128)S(1)}, u32[]{:S(2)}, u32[]{:S(2)}) collective-permute-start(s32[1,256]{1,0:T(1,128)S(1)} %get-tuple-element.17), channel_id=1, source_target_pairs={{0,96},{32,64},{64,32},{96,0},{1,97},{33,65},{65,33},{97,1},{2,98}... | collective-permute-start | bytes 3080 | tf_op jit(solution)/shard_map/ppermute | solution.py:277
  16.9 2.8 %collective-permute-start.1 = (s32[1,256]{1,0:T(1,128)S(1)}, s32[1,256]{1,0:T(1,128)S(1)}, u32[]{:S(2)}, u32[]{:S(2)}) collective-permute-start(s32[1,256]{1,0:T(1,128)S(1)} %get-tuple-element.18), channel_id=1, source_target_pairs={{0,64},{32,96},{64,0},{96,32},{1,65},{33,97},{65,1},{97,33},{2,66}... | collective-permute-start | bytes 3080 | tf_op jit(solution)/shard_map/ppermute | solution.py:277
  17.5 2.2 %collective-permute-start = (s32[1,256]{1,0:T(1,128)S(1)}, s32[1,256]{1,0:T(1,128)S(1)}, u32[]{:S(2)}, u32[]{:S(2)}) collective-permute-start(s32[1,256]{1,0:T(1,128)S(1)} %get-tuple-element.19), channel_id=1, source_target_pairs={{0,32},{32,0},{64,96},{96,64},{1,33},{33,1},{65,97},{97,65},{2,34}... | collective-permute-start | bytes 3080 | tf_op jit(solution)/shard_map/ppermute | solution.py:277
  19.7 37.7 %copy-start.1 = (s32[1,256]{1,0:T(1,128)}, s32[1,256]{1,0:T(1,128)S(1)}, u32[]{:S(2)}) copy-start(s32[1,256]{1,0:T(1,128)S(1)} %collective-permute-done) | copy-start | bytes 3076
  19.7 6.8 %collective-permute-start.3 = (s32[4,256]{1,0:T(4,128)S(1)}, s32[4,256]{1,0:T(4,128)S(1)}, u32[]{:S(2)}, u32[]{:S(2)}) collective-permute-start(s32[4,256]{1,0:T(4,128)S(1)} %pad_add_fusion), channel_id=1, source_target_pairs={{0,1},{1,0},{2,3},{3,2},{4,5},{5,4},{6,7},{7,6},{8,9},{9,8},{10,11... | collective-permute-start | bytes 12296 | tf_op jit(solution)/shard_map/ppermute | solution.py:277
  26.5 28.2 %collective-permute-start.6 = (s32[8,256]{1,0:T(8,128)S(1)}, s32[8,256]{1,0:T(8,128)S(1)}, u32[]{:S(2)}, u32[]{:S(2)}) collective-permute-start(s32[8,256]{1,0:T(8,128)S(1)} %concatenate.16), channel_id=1, source_target_pairs={{0,6},{1,7},{2,4},{3,5},{4,2},{5,3},{6,0},{7,1},{8,14},{9,15},{10,... | collective-permute-start | bytes 24584 | tf_op jit(solution)/shard_map/ppermute | solution.py:277
  53.4 4.0 %collective-permute-start.5 = (s32[8,256]{1,0:T(8,128)S(1)}, s32[8,256]{1,0:T(8,128)S(1)}, u32[]{:S(2)}, u32[]{:S(2)}) collective-permute-start(s32[8,256]{1,0:T(8,128)S(1)} %concatenate.16), channel_id=1, source_target_pairs={{0,4},{1,5},{2,6},{3,7},{4,0},{5,1},{6,2},{7,3},{8,12},{9,13},{10,... | collective-permute-start | bytes 24584 | tf_op jit(solution)/shard_map/ppermute | solution.py:277
  53.4 4.0 %collective-permute-start.4 = (s32[8,256]{1,0:T(8,128)S(1)}, s32[8,256]{1,0:T(8,128)S(1)}, u32[]{:S(2)}, u32[]{:S(2)}) collective-permute-start(s32[8,256]{1,0:T(8,128)S(1)} %concatenate.16), channel_id=1, source_target_pairs={{0,2},{1,3},{2,0},{3,1},{4,6},{5,7},{6,4},{7,5},{8,10},{9,11},{10,... | collective-permute-start | bytes 24584 | tf_op jit(solution)/shard_map/ppermute | solution.py:277
  57.4 9.1 %collective-permute-start.9 = (s32[32,256]{1,0:T(8,128)S(1)}, s32[32,256]{1,0:T(8,128)S(1)}, u32[]{:S(2)}, u32[]{:S(2)}) collective-permute-start(s32[32,256]{1,0:T(8,128)S(1)} %concatenate.17), channel_id=1, source_target_pairs={{0,24},{1,25},{2,26},{3,27},{4,28},{5,29},{6,30},{7,31},{8,16},{9,... | collective-permute-start | bytes 98312 | tf_op jit(solution)/shard_map/ppermute | solution.py:277
  65.2 4.3 %collective-permute-start.8 = (s32[32,256]{1,0:T(8,128)S(1)}, s32[32,256]{1,0:T(8,128)S(1)}, u32[]{:S(2)}, u32[]{:S(2)}) collective-permute-start(s32[32,256]{1,0:T(8,128)S(1)} %concatenate.17), channel_id=1, source_target_pairs={{0,16},{1,17},{2,18},{3,19},{4,20},{5,21},{6,22},{7,23},{8,24},{9,... | collective-permute-start | bytes 98312 | tf_op jit(solution)/shard_map/ppermute | solution.py:277
  66.3 3.2 %collective-permute-start.7 = (s32[32,256]{1,0:T(8,128)S(1)}, s32[32,256]{1,0:T(8,128)S(1)}, u32[]{:S(2)}, u32[]{:S(2)}) collective-permute-start(s32[32,256]{1,0:T(8,128)S(1)} %concatenate.17), channel_id=1, source_target_pairs={{0,8},{1,9},{2,10},{3,11},{4,12},{5,13},{6,14},{7,15},{8,0},{9,1},... | collective-permute-start | bytes 98312 | tf_op jit(solution)/shard_map/ppermute | solution.py:277
  87.2 52.6 %all-to-all-start.1 = ((bf16[128,8,1536]{2,1,0:T(8,128)(2,1)}), bf16[128,8,1536]{2,1,0:T(8,128)(2,1)S(1)}, u32[]{:S(2)}, u32[]{:S(2)}) async-start(bf16[128,8,1536]{2,1,0:T(8,128)(2,1)} %bitcast.13), calls=%async_computation.1 | async-start | bytes 6291456 | tf_op jit(solution)/shard_map/all_to_all | solution.py:18

commit v5 on v3

--- a/solution.py
+++ b/solution.py
@@ -109,95 +109,176 @@
         key_ref[...] = keys
 
 
-def middle_kernel(
-    width, got_ref, mask_ref, diag_hbm, col_hbm, row_hbm, out_hbm,
-    w_ref, x_ref, x0_ref, y_ref, t_ref, p_ref, pt_ref, out_ref, s_ref, gm_ref, gh_ref, w_sem, out_sem,
+STEP = 256
+
+
+def keep_of(mask_ref, row, edge):
+    return jnp.broadcast_to(mask_ref[row : row + 1, :], (edge, mask_ref.shape[1])).astype(BF)
+
+
+def take(places):
+    ids = lax.broadcasted_iota(jnp.int32, (places.shape[0], 1024), 1).astype(F32)
+    return onehot(places == ids)
+
+
+def arm_kernel(
+    width, class_ref, got_ref, mask_ref, row_hbm,
+    x_ref, t_ref, p_ref, pt_ref, gh_ref, own_ref, s0_ref, s1_ref, s2_ref, s3_ref,
+    w_ref, s_ref, gm_ref, other_ref, w_sem,
 ):
     slots = got_ref.shape[0]
     size = x_ref.shape[0]
     half = slots // 2
-    step = 256
     lanes = range(0, width, 128)
-    loads = [
-        pltpu.make_async_copy(src, w_ref.at[k], w_sem.at[k])
-        for k, src in enumerate((diag_hbm, col_hbm, row_hbm))
-    ]
-    for copy in loads:
-        copy.start()
+    load = pltpu.make_async_copy(row_hbm, w_ref, w_sem)
+    load.start()
     codes = got_ref[:, 3 * width :].astype(F32)
     place = (codes - 1.0) * 32.0 + pltpu.roll(codes, 127, 1)
     p_ref[0:slots, :] = place
-    pt_ref[:, 0:slots] = place.T
+    pt_ref[:, 0:slots] = place.T[0:8, :]
     for j in lanes:
         s_ref[j // 128] = got_ref[:, width + j : width + j + 128].astype(F32)
     for k, ref in enumerate((gm_ref, gh_ref)):
         part = p_ref[pl.ds(k, half, stride=2), :]
         at = slots + k * half
         p_ref[at : at + half, :] = part
-        pt_ref[:, at : at + half] = part.T
+        pt_ref[:, at : at + half] = part.T[0:8, :]
         for j in lanes:
             ref[:, j : j + 128] = s_ref[j // 128, pl.ds(k, half, stride=2), :].astype(BF)
+    first = class_ref[0] == 0
+    for at, count, col, to in ((0, half, 4, 0), (slots + half, half // 2, 2, half)):
+        even = p_ref[pl.ds(at, count, stride=2), :][:, col : col + 1]
+        odd = p_ref[pl.ds(at + 1, count, stride=2), :][:, col : col + 1]
+        own_ref[to : to + count, :] = jnp.broadcast_to(jnp.where(first, even, odd), (count, 128))
+        other_ref[to : to + count, :] = jnp.broadcast_to(jnp.where(first, odd, even), (count, 128))
 
     def unpack(c, carry):
         def put(row, start, count):
-            ids = (lax.broadcasted_iota(jnp.int32, (step, count), 0) + c * step).astype(F32)
+            ids = (lax.broadcasted_iota(jnp.int32, (STEP, count), 0) + c * STEP).astype(F32)
             return onehot(pt_ref[row : row + 1, start : start + count] == ids)
 
-        span = pl.ds(pl.multiple_of(c * step, step), step)
+        span = pl.ds(pl.multiple_of(c * STEP, STEP), STEP)
         x_ref[span, :] = (
             mm(put(0, 0, slots), got_ref[:, 0:width]) + mm(put(2, slots, half), gm_ref[...])
         ).astype(BF)
+        return carry
+
+    lax.fori_loop(0, size // STEP, unpack, 0)
+    load.wait()
+    tiles = mask_ref.shape[0] // 3
+    edge = size // tiles
+    for c in range(tiles):
+        span = slice(c * edge, (c + 1) * edge)
+        kept = w_ref[span, :] * keep_of(mask_ref, 2 * tiles + c, edge)
+        t_ref[span, :] = mm(kept, x_ref[...]).astype(BF)
+    n4 = half // 4
+    n2 = half // 8
+    for d, ref in enumerate((s0_ref, s1_ref, s2_ref, s3_ref)):
+        ref[0:n4, :] = mm(take(other_ref[d * n4 : (d + 1) * n4, 0:1]), t_ref[...]).astype(BF)
+        at = half + d * n2
+        ref[n4:, :] = mm(take(other_ref[at : at + n2, 0:1]), t_ref[...]).astype(BF)
+
+
+def block_kernel(
+    width, got_ref, x_ref, t_ref, p_ref, pt_ref, gh_ref, own_ref, mask_ref, diag_hbm, col_hbm,
+    out_hbm, extra_ref, arm_ref,
+    w_ref, x0_ref, y_ref, out_ref, w_sem, out_sem,
+):
+    slots = got_ref.shape[0]
+    size = x_ref.shape[0]
+    half = slots // 2
+    loads = [
+        pltpu.make_async_copy(src, w_ref.at[k], w_sem.at[k])
+        for k, src in enumerate((diag_hbm, col_hbm))
+    ]
+    for copy in loads:
+        copy.start()
+
+    def unpack(c, carry):
+        def put(row, start, count):
+            ids = (lax.broadcasted_iota(jnp.int32, (STEP, count), 0) + c * STEP).astype(F32)
+            return onehot(pt_ref[row : row + 1, start : start + count] == ids)
+
+        span = pl.ds(pl.multiple_of(c * STEP, STEP), STEP)
         x0_ref[span, :] = (
             mm(put(4, 0, slots), got_ref[:, 2 * width : 3 * width])
             + mm(put(2, slots + half, half), gh_ref[...])
         ).astype(BF)
         return carry
 
-    lax.fori_loop(0, size // step, unpack, 0)
+    lax.fori_loop(0, size // STEP, unpack, 0)
     for copy in loads:
         copy.wait()
     tiles = mask_ref.shape[0] // 3
     edge = size // tiles
     for c in range(tiles):
         span = slice(c * edge, (c + 1) * edge)
-        kept = []
-        for k in range(3):
-            keep = jnp.broadcast_to(mask_ref[k * tiles + c : k * tiles + c + 1, :], (edge, size))
-            kept.append(w_ref[k, span, :] * keep.astype(BF))
-        t_ref[span, :] = mm(kept[2], x_ref[...]).astype(BF)
-        y_ref[span, :] = (mm(kept[0], x_ref[...]) + mm(kept[1], x0_ref[...])).astype(BF)
+        diag = w_ref[0, span, :] * keep_of(mask_ref, c, edge)
+        col = w_ref[1, span, :] * keep_of(mask_ref, tiles + c, edge)
+        y_ref[span, :] = (mm(diag, x_ref[...]) + mm(col, x0_ref[...])).astype(BF)
 
     def store(c):
-        span = pl.ds(c * step, step)
-        return pltpu.make_async_copy(out_ref.at[span, :], out_hbm.at[span, :], out_sem.at[c])
-
-    for c in range(slots // step):
-        span = slice(c * step, (c + 1) * step)
-
-        def take(base, count, col):
-            ids = lax.broadcasted_iota(jnp.int32, (count, size), 1).astype(F32)
-            at = base + c * count
-            return onehot(p_ref[at : at + count, col : col + 1] == ids)
-
-        out_ref[span, 0:width] = mm(take(0, step, 0), y_ref[...]).astype(BF)
-        even = mm(take(slots, step // 2, 2), y_ref[...])
-        odd = mm(take(slots + half, step // 2, 2), t_ref[...])
-        for j in lanes:
-            s_ref[j // 128, pl.ds(0, step // 2, stride=2), :] = even[:, j : j + 128]
-            s_ref[j // 128, pl.ds(1, step // 2, stride=2), :] = odd[:, j : j + 128]
-            out_ref[span, width + j : width + j + 128] = s_ref[j // 128, 0:step, :].astype(BF)
-        out_ref[span, 2 * width : 3 * width] = mm(take(0, step, 4), t_ref[...]).astype(BF)
+        span = pl.ds(c * STEP, STEP)
+        return pltpu.make_async_copy(
+            out_ref.at[span, :], out_hbm.at[span, pl.ds(0, width)], out_sem.at[c]
+        )
+
+    for c in range(slots // STEP):
+        span = slice(c * STEP, (c + 1) * STEP)
+        out_ref[span, :] = mm(take(p_ref[span, 0:1]), y_ref[...]).astype(BF)
         store(c).start()
-    for c in range(slots // step):
+    for c in range(half // STEP):
+        span = slice(c * STEP, (c + 1) * STEP)
+        extra_ref[span, :] = mm(
+            take(p_ref[slots + c * STEP : slots + (c + 1) * STEP, 2:3]), y_ref[...]
+        )
+    for c in range(own_ref.shape[0] // STEP):
+        span = slice(c * STEP, (c + 1) * STEP)
+        arm_ref[span, :] = mm(take(own_ref[span, 0:1]), t_ref[...])
+    for c in range(slots // STEP):
         store(c).wait()
+
+
+def join_kernel(
+    width, extra_ref, arm_ref, r0_ref, r1_ref, r2_ref, r3_ref, kept_hbm, out_hbm,
+    out_ref, s_ref, e_ref, out_sem,
+):
+    slots = out_ref.shape[0]
+    half = slots // 2
+    n4 = half // 4
+    n2 = half // 8
+
+    def store(c):
+        span = pl.ds(c * STEP, STEP)
+        return pltpu.make_async_copy(
+            out_ref.at[span, :], out_hbm.at[span, pl.ds(width, width + 128)], out_sem.at[c]
+        )
+
+    for d, ref in enumerate((r0_ref, r1_ref, r2_ref, r3_ref)):
+        span = slice(d * STEP, (d + 1) * STEP)
+        four = arm_ref[d * n4 : (d + 1) * n4, :] + ref[0:n4, :].astype(F32)
+        at = half + d * n2
+        two = arm_ref[at : at + n2, :] + ref[n4:, :].astype(F32)
+        more = extra_ref[d * n4 : (d + 1) * n4, :]
+        for j in range(0, width, 128):
+            t = j // 128
+            s_ref[d, t, pl.ds(0, n4, stride=2), :] = more[:, j : j + 128]
+            s_ref[d, t, pl.ds(1, n4, stride=2), :] = four[:, j : j + 128]
+            e_ref[d, pl.ds(t, n2, stride=4), :] = two[:, j : j + 128]
+        for t in range(width // 128):
+            out_ref[span, t * 128 : (t + 1) * 128] = s_ref[d, t].astype(BF)
+        out_ref[span, width:] = e_ref[d].astype(BF)
+        store(d).start()
+    for d in range(4):
+        store(d).wait()
 
 
 def tail_kernel(
     width, arrows, reply_ref, key_ref, pre_hbm, up_hbm, down_hbm, out_ref,
-    pick_ref, pre_ref, up_ref, down_ref, agg_ref, acc_ref, sem,
+    pick_ref, part_ref, pre_ref, up_ref, down_ref, agg_ref, acc_ref, sem,
 ):
     slots = reply_ref.shape[0]
-    count, _, chunk = pre_ref.shape
+    count, nodes, chunk = pre_ref.shape
     loads = []
     for c in range(count):
         span = pl.ds(c * chunk, chunk)
@@ -212,16 +293,28 @@
             copy.start()
     rows = slots // arrows
     lane = lax.broadcasted_iota(jnp.int32, (1, rows), 1)
-    block = lane // 8 * 16
+    blk = lane // 8
+    block = blk * 16
+    side = (blk // 8 + blk // 2) % 2
     r = lane % 8
-    goals = (block + r, jnp.where(r % 2 == 0, block, 0) + 8 + r // 2, r)
+
+    def hits(goal, a):
+        return onehot(key_ref[:, a : a + 1] == goal.astype(F32))
+
+    goals = (block + r, jnp.where(r % 2 == 0, block + 8 + r // 2, r - 1 + side))
     total = jnp.zeros(agg_ref.shape, F32)
-    for q in range(3):
-        goal = goals[q].astype(F32)
+    for q in range(2):
         for a in range(arrows):
-            pick_ref[:, a * rows : (a + 1) * rows] = onehot(key_ref[:, a : a + 1] == goal)
+            pick_ref[:, a * rows : (a + 1) * rows] = hits(goals[q], a)
         total = total + mm(pick_ref[...], reply_ref[:, q * width : (q + 1) * width])
-    agg_ref[...] = total.astype(BF)
+    for t in range(width // 128):
+        goal = jnp.where(r % 4 == t, 8 + r // 4 * 2 + side, -1)
+        for a in range(arrows):
+            part_ref[t * nodes : (t + 1) * nodes, a * rows : (a + 1) * rows] = hits(goal, a)
+    rest = mm(part_ref[...], reply_ref[:, 2 * width :])
+    for t in range(width // 128):
+        span = slice(t * 128, (t + 1) * 128)
+        agg_ref[:, span] = (total[:, span] + rest[t * nodes : (t + 1) * nodes, :]).astype(BF)
     acc_ref[...] = jnp.zeros(acc_ref.shape, F32)
     for c in range(count):
         loads[c][0].wait()
@@ -235,6 +328,16 @@
 
 CHUNK = 1024
 PRE = BF
+
+
+def neighbours(dx, dy):
+    pairs = []
+    for x in range(4):
+        for y in range(4):
+            for z in range(2):
+                to = ((x + dx) % 4) * 8 + ((y + dy) % 4) * 2 + z
+                pairs.append((x * 8 + y * 2 + z, to))
+    return pairs
 
 
 def params(limit):
@@ -295,27 +398,77 @@
     )(positions.T, in_hbm(features), in_hbm(up_weight))
     keep = jnp.repeat(tile_masks.astype(F32), size // tiles, axis=2).reshape(3 * tiles, size)
 
+    blk = lax.axis_index("blk")
+    side = ((blk // 8 + blk // 2) % 2).astype(jnp.int32).reshape(1)
+    sm = pl.BlockSpec(memory_space=pltpu.SMEM)
+    half = rows // 2
+    part = jax.ShapeDtypeStruct((half // 4 + half // 8, width), BF)
+    full = jax.ShapeDtypeStruct((size, width), BF)
+    x, t, p, pt, gh, own, *given = pl.pallas_call(
+        functools.partial(arm_kernel, width),
+        in_specs=[sm, VM, VM, HB],
+        out_specs=[VM] * 10,
+        out_shape=[
+            full,
+            full,
+            jax.ShapeDtypeStruct((2 * rows, 128), F32),
+            jax.ShapeDtypeStruct((8, 2 * rows), F32),
+            jax.ShapeDtypeStruct((half, width), BF),
+            jax.ShapeDtypeStruct((half + half // 2, 128), F32),
+            part,
+            part,
+            part,
+            part,
+        ],
+        scratch_shapes=[
+            pltpu.VMEM((size, size), BF),
+            pltpu.VMEM((width // 128, rows, 128), F32),
+            pltpu.VMEM((half, width), BF),
+            pltpu.VMEM((half + half // 2, 128), F32),
+            dma,
+        ],
+        compiler_params=params(16),
+        name="arms",
+    )(side, got, keep, in_hbm(row_values))
+    taken = [
+        lax.ppermute(g, "blk", neighbours(*move)) for g, move in zip(given, ((1, 0), (3, 0), (0, 1), (0, 3)))
+    ]
+    reply, extra, arm = pl.pallas_call(
+        functools.partial(block_kernel, width),
+        in_specs=[VM] * 8 + [HB, HB],
+        out_specs=[HB, VM, VM],
+        out_shape=[
+            pltpu.HBM((rows, 2 * width + 128), BF),
+            jax.ShapeDtypeStruct((half, width), F32),
+            jax.ShapeDtypeStruct((half + half // 2, width), F32),
+        ],
+        scratch_shapes=[
+            pltpu.VMEM((2, size, size), BF),
+            pltpu.VMEM((size, width), BF),
+            pltpu.VMEM((size, width), BF),
+            pltpu.VMEM((rows, width), BF),
+            dma((2,)),
+            dma((rows // STEP,)),
+        ],
+        compiler_params=params(16),
+        name="blocks",
+    )(got, x, t, p, pt, gh, own, keep, in_hbm(diag_values), in_hbm(column_values))
     reply = pl.pallas_call(
-        functools.partial(middle_kernel, width),
-        in_specs=[VM, VM, HB, HB, HB],
+        functools.partial(join_kernel, width),
+        in_specs=[VM] * 6 + [HB],
         out_specs=HB,
-        out_shape=pltpu.HBM((rows, 3 * width), BF),
-        scratch_shapes=[pltpu.VMEM((3, size, size), BF)]
-        + [pltpu.VMEM((size, width), BF)] * 4
-        + [
-            pltpu.VMEM((2 * rows, 128), F32),
-            pltpu.VMEM((128, 2 * rows), F32),
-            pltpu.VMEM((rows, 3 * width), BF),
-            pltpu.VMEM((width // 128, rows, 128), F32),
-            pltpu.VMEM((rows // 2, width), BF),
-            pltpu.VMEM((rows // 2, width), BF),
-            dma((3,)),
-            dma((rows // 256,)),
-        ],
-        compiler_params=params(40),
-        name="middle",
-    )(got, keep, in_hbm(diag_values), in_hbm(column_values), in_hbm(row_values))
-    reply = exchange(reply.reshape(devices, 8, 3 * width)).reshape(rows, 3 * width)
+        out_shape=pltpu.HBM((rows, 2 * width + 128), BF),
+        input_output_aliases={6: 0},
+        scratch_shapes=[
+            pltpu.VMEM((rows, width + 128), BF),
+            pltpu.VMEM((4, width // 128, STEP, 128), F32),
+            pltpu.VMEM((4, STEP, 128), F32),
+            dma((4,)),
+        ],
+        compiler_params=params(16),
+        name="join",
+    )(extra, arm, *taken, reply)
+    reply = exchange(reply.reshape(devices, 8, 2 * width + 128)).reshape(rows, 2 * width + 128)
 
     return pl.pallas_call(
         functools.partial(tail_kernel, width, arrows),
@@ -324,6 +477,7 @@
         out_shape=jax.ShapeDtypeStruct((row_count, width), BF),
         scratch_shapes=[
             pltpu.VMEM((row_count, rows), BF),
+            pltpu.VMEM((row_count * (width // 128), rows), BF),
             pltpu.VMEM((count, row_count, CHUNK), PRE),
             pltpu.VMEM((count, width, CHUNK), BF),
             pltpu.VMEM((hidden, width), BF),

time: 126 us -> 126 us (level)
  waiting for transfers between devices: 76.1 us -> 68 us
  starting transfers between devices: 17.6 us -> 21.9 us
  Pallas kernels: 31.1 us -> 35.3 us
    all_to_all x2, waiting for transfers between devices: 76.1 us -> 68 us  [exchange(): lax.all_to_all(block, ('arrow', 'blk'), split_axis=0, concat_axis=0, tile...]
    ppermute x0 -> x4, starting transfers between devices: none -> 5.41 us  [body(): lax.ppermute(g, 'blk', neighbours(*move))]
    pallas_call x1, Pallas kernels: 6.41 us -> 8.82 us  [body(): pl.pallas_call(functools.partial(tail_kernel, width, arrows), in_specs=[V...]
    pallas_call x1 -> x3, Pallas kernels: 12.4 us -> 14.3 us  [the longest x1 7.14 us: body(): pl.pallas_call(functools.partial(block_kernel, width), in_specs=[VM] * 8...]
  transfers between devices with their start and end apart: 2 -> 6, of which waited for: 2 -> 2; matrix products, arithmetic and copies ran while one was open for 0% -> 0% of each run, Pallas kernels for 7% -> 12%
where the time goes in v5:
time: 126 us
  waiting for transfers between devices  68 us (54%)
  Pallas kernels  35.3 us (28%)
  starting transfers between devices  21.9 us (17%)
    all_to_all x2, waiting for transfers between devices, exchange(): lax.all_to_all(block, ('arrow', 'blk'), split_axis=0, concat_axis=0, tile...  68 us
    all_to_all x2, starting transfers between devices, exchange(): lax.all_to_all(block, ('arrow', 'blk'), split_axis=0, concat_axis=0, tile...  16.4 us
    pallas_call x1, Pallas kernels, body(): pl.pallas_call(functools.partial(tail_kernel, width, arrows), in_specs=[V...  8.82 us
    pallas_call x1, Pallas kernels, body(): pl.pallas_call(functools.partial(prep_kernel, arrows, size, width), grid=...  8.3 us
    pallas_call x1, Pallas kernels, body(): pl.pallas_call(functools.partial(block_kernel, width), in_specs=[VM] * 8...  7.14 us
    pallas_call x1, Pallas kernels, body(): pl.pallas_call(functools.partial(arm_kernel, width), in_specs=[sm, VM, VM...  5.87 us
    ppermute x4, starting transfers between devices, body(): lax.ppermute(g, 'blk', neighbours(*move))  5.41 us
    pallas_call x1, Pallas kernels, body(): pl.pallas_call(functools.partial(pack_kernel, size, width), in_specs=[HB,...  3.86 us
  transfers between devices with their start and end apart: 6, of which 2 were waited for; matrix products, arithmetic and copies ran while one was open for 0% of the time, Pallas kernels for 12%

profile of v5, /device:TPU:1, one launch (start us, length us, event | category | flops | bytes accessed | tf_op | source)
XLA Modules:
  0.0 125.8 jit_solution(3204764899435868886)
XLA Ops:
  0.0 3.9 %pack.1 = bf16[1024,1664]{1,0:T(8,128)(2,1)} custom-call(bf16[256,512]{1,0:T(8,128)(2,1)} %feat_ref.1, s32[4,256]{1,0:T(4,128)} %pos_hbm.1), custom_call_target="tpu_custom_call" | custom-call | tf_op jit(solution)/shard_map/pack/pallas_call | solution.py:361
  3.9 0.0 copy-start.1
  3.9 11.5 %all-to-all-start = ((bf16[128,8,1664]{2,1,0:T(8,128)(2,1)}), bf16[128,8,1664]{2,1,0:T(8,128)(2,1)S(1)}, u32[]{:S(2)}, u32[]{:S(2)}) async-start(bf16[128,8,1664]{2,1,0:T(8,128)(2,1)} %bitcast.12), calls=%async_computation | async-start | bytes 6815744 | tf_op jit(solution)/shard_map/all_to_all | solution.py:18
  15.4 0.0 copy-done.1
  15.4 0.1 copy.10
  15.5 0.1 broadcast_bitcast_fusion.mask_ref
  15.6 43.5 %all-to-all-done = bf16[128,8,1664]{2,1,0:T(8,128)(2,1)S(1)} async-done(((bf16[128,8,1664]{2,1,0:T(8,128)(2,1)}), bf16[128,8,1664]{2,1,0:T(8,128)(2,1)S(1)}, u32[]{:S(2)}, u32[]{:S(2)}) %all-to-all-start) | async-done | bytes 3407904 | tf_op jit(solution)/shard_map/all_to_all | solution.py:18
  59.1 5.9 %arms.1 = (bf16[1024,512]{1,0:T(8,128)(2,1)S(1)}, bf16[1024,512]{1,0:T(8,128)(2,1)S(1)}, f32[2048,128]{1,0:T(8,128)S(1)}, f32[8,2048]{1,0:T(8,128)S(1)}, bf16[51...) custom-call(s32[1]{0:T(128)} %bitcast.2.class_ref, ...), custom_call_target="tpu_custom_call" | custom-call | tf_op jit(solution)/shard_map/arms/pallas_call | solution.py:407
  65.0 0.1 collective-permute-start
  65.1 2.7 %collective-permute-start.1 = (bf16[192,512]{1,0:T(8,128)(2,1)S(1)}, bf16[192,512]{1,0:T(8,128)(2,1)S(1)}, u32[]{:S(2)}, u32[]{:S(2)}) collective-permute-start(bf16[192,512]{1,0:T(8,128)(2,1)S(1)} %get-tuple-element.30), channel_id=1, source_target_pairs={{0,24},{1,25},{2,26},{3,27},{4,28},{5,29},{6,30},{7,31},{8,0},{9,1... | collective-permute-start | bytes 589832 | tf_op jit(solution)/shard_map/ppermute | solution.py:434
  67.8 1.4 %collective-permute-start.2 = (bf16[192,512]{1,0:T(8,128)(2,1)S(1)}, bf16[192,512]{1,0:T(8,128)(2,1)S(1)}, u32[]{:S(2)}, u32[]{:S(2)}) collective-permute-start(bf16[192,512]{1,0:T(8,128)(2,1)S(1)} %get-tuple-element.31), channel_id=1, source_target_pairs={{0,2},{1,3},{2,4},{3,5},{4,6},{5,7},{6,0},{7,1},{8,10},{9,11},{10,... | collective-permute-start | bytes 589832 | tf_op jit(solution)/shard_map/ppermute | solution.py:434
  69.2 1.3 %collective-permute-start.3 = (bf16[192,512]{1,0:T(8,128)(2,1)S(1)}, bf16[192,512]{1,0:T(8,128)(2,1)S(1)}, u32[]{:S(2)}, u32[]{:S(2)}) collective-permute-start(bf16[192,512]{1,0:T(8,128)(2,1)S(1)} %get-tuple-element.32), channel_id=1, source_target_pairs={{0,6},{1,7},{2,0},{3,1},{4,2},{5,3},{6,4},{7,5},{8,14},{9,15},{10,... | collective-permute-start | bytes 589832 | tf_op jit(solution)/shard_map/ppermute | solution.py:434
  70.4 7.1 %blocks.1 = (bf16[1024,1152]{1,0:T(8,128)(2,1)}, f32[512,512]{1,0:T(8,128)S(1)}, f32[768,512]{1,0:T(8,128)S(1)}) custom-call(bf16[1024,1664]{1,0:T(8,128)(2,1)S(1)} %bitcast.9, bf16[1024,512]{1,0:T(8,128)(2,1)S(1)} %get-tuple-element.21.x_ref, bf16[1024,512]{1,0:T(8,128)(2,1)S(1)} %get-tuple-element.22.t_ref, f32[2048,128]{1,0:T(8,128)S(1)} %get-tuple-element.23.p_ref, ...), custom_call_target="tpu_custom_call" | custom-call | tf_op jit(solution)/shard_map/blocks/pallas_call | solution.py:436
  77.6 0.0 collective-permute-done.r0_ref
  77.6 0.0 collective-permute-done.1.r1_ref
  77.6 0.0 collective-permute-done.2.r2_ref
  77.6 0.0 collective-permute-done.3.r3_ref
  77.6 1.3 %join.1 = bf16[1024,1152]{1,0:T(8,128)(2,1)} custom-call(f32[512,512]{1,0:T(8,128)S(1)} %get-tuple-element.27.extra_ref, f32[768,512]{1,0:T(8,128)S(1)} %get-tuple-element.28.arm_ref, bf16[192,512]{1,0:T(8,128)(2,1)S(1)} %collective-permute-done.r0_ref, bf16[192,512]{1,0:T(8,128)(2,1)S(1)} %collective-permute-done.1.r1_ref, ...), custom_call_target="tpu_custom_call", output_to_operand_aliasing={{}: (6, {})} | custom-call | tf_op jit(solution)/shard_map/join/pallas_call | solution.py:456
  78.9 0.0 copy-start
  78.9 5.0 %all-to-all-start.1 = ((bf16[128,8,1152]{2,1,0:T(8,128)(2,1)}), bf16[128,8,1152]{2,1,0:T(8,128)(2,1)S(1)}, u32[]{:S(2)}, u32[]{:S(2)}) async-start(bf16[128,8,1152]{2,1,0:T(8,128)(2,1)} %bitcast.13), calls=%async_computation.1 | async-start | bytes 4718592 | tf_op jit(solution)/shard_map/all_to_all | solution.py:18
  83.9 0.0 copy-done
  83.9 0.1 copy.11
  84.0 8.3 %prep.1 = (f32[256,128]{1,0:T(8,128)S(1)}, bf16[4,256,1024]{2,1,0:T(8,128)(2,1)}, bf16[4,512,1024]{2,1,0:T(8,128)(2,1)}) custom-call(s32[256,4]{1,0:T(8,128)S(1)} %bitcast.11, bf16[256,512]{1,0:T(8,128)(2,1)} %feat_ref.1, bf16[1024,4096]{1,0:T(8,128)(2,1)} %w_ref.1), custom_call_target="tpu_custom_call" | custom-call | tf_op jit(solution)/shard_map/prep/pallas_call | solution.py:378
  92.3 24.5 %all-to-all-done.1 = bf16[128,8,1152]{2,1,0:T(8,128)(2,1)S(1)} async-done(((bf16[128,8,1152]{2,1,0:T(8,128)(2,1)}), bf16[128,8,1152]{2,1,0:T(8,128)(2,1)S(1)}, u32[]{:S(2)}, u32[]{:S(2)}) %all-to-all-start.1) | async-done | bytes 2359328 | tf_op jit(solution)/shard_map/all_to_all | solution.py:18
  116.8 8.8 %tail.1 = bf16[256,512]{1,0:T(8,128)(2,1)} custom-call(bf16[1024,1152]{1,0:T(8,128)(2,1)S(1)} %bitcast.10, f32[256,128]{1,0:T(8,128)S(1)} %get-tuple-element.34.key_ref, bf16[4,256,1024]{2,1,0:T(8,128)(2,1)} %get-tuple-element.35.pre_hbm, bf16[4,512,1024]{2,1,0:T(8,128)(2,1)} %get-tuple-element.36.up_hbm, bf16[4096,512]{1,0:T(8,128)(2,1)} %down_hbm.1), custom_call_target="tpu_custom_call" | custom-call | tf_op jit(solution)/shard_map/tail/pallas_call | solution.py:473
  (1 shorter events, 0.0 us)
Async XLA Ops:
  3.9 11.5 %copy-start.1 = (s32[3,8,8]{2,1,0:T(8,128)S(1)}, s32[3,8,8]{2,1,0:T(8,128)}, u32[]{:S(2)}) copy-start(s32[3,8,8]{2,1,0:T(8,128)} %param.13) | copy-start | bytes 2308
  3.9 55.2 %all-to-all-start = ((bf16[128,8,1664]{2,1,0:T(8,128)(2,1)}), bf16[128,8,1664]{2,1,0:T(8,128)(2,1)S(1)}, u32[]{:S(2)}, u32[]{:S(2)}) async-start(bf16[128,8,1664]{2,1,0:T(8,128)(2,1)} %bitcast.12), calls=%async_computation | async-start | bytes 6815744 | tf_op jit(solution)/shard_map/all_to_all | solution.py:18
  65.0 12.6 %collective-permute-start = (bf16[192,512]{1,0:T(8,128)(2,1)S(1)}, bf16[192,512]{1,0:T(8,128)(2,1)S(1)}, u32[]{:S(2)}, u32[]{:S(2)}) collective-permute-start(bf16[192,512]{1,0:T(8,128)(2,1)S(1)} %get-tuple-element.29), channel_id=1, source_target_pairs={{0,8},{1,9},{2,10},{3,11},{4,12},{5,13},{6,14},{7,15},{8,16},{9,17... | collective-permute-start | bytes 589832 | tf_op jit(solution)/shard_map/ppermute | solution.py:434
  65.1 12.5 %collective-permute-start.1 = (bf16[192,512]{1,0:T(8,128)(2,1)S(1)}, bf16[192,512]{1,0:T(8,128)(2,1)S(1)}, u32[]{:S(2)}, u32[]{:S(2)}) collective-permute-start(bf16[192,512]{1,0:T(8,128)(2,1)S(1)} %get-tuple-element.30), channel_id=1, source_target_pairs={{0,24},{1,25},{2,26},{3,27},{4,28},{5,29},{6,30},{7,31},{8,0},{9,1... | collective-permute-start | bytes 589832 | tf_op jit(solution)/shard_map/ppermute | solution.py:434
  67.8 9.8 %collective-permute-start.2 = (bf16[192,512]{1,0:T(8,128)(2,1)S(1)}, bf16[192,512]{1,0:T(8,128)(2,1)S(1)}, u32[]{:S(2)}, u32[]{:S(2)}) collective-permute-start(bf16[192,512]{1,0:T(8,128)(2,1)S(1)} %get-tuple-element.31), channel_id=1, source_target_pairs={{0,2},{1,3},{2,4},{3,5},{4,6},{5,7},{6,0},{7,1},{8,10},{9,11},{10,... | collective-permute-start | bytes 589832 | tf_op jit(solution)/shard_map/ppermute | solution.py:434
  69.2 8.5 %collective-permute-start.3 = (bf16[192,512]{1,0:T(8,128)(2,1)S(1)}, bf16[192,512]{1,0:T(8,128)(2,1)S(1)}, u32[]{:S(2)}, u32[]{:S(2)}) collective-permute-start(bf16[192,512]{1,0:T(8,128)(2,1)S(1)} %get-tuple-element.32), channel_id=1, source_target_pairs={{0,6},{1,7},{2,0},{3,1},{4,2},{5,3},{6,4},{7,5},{8,14},{9,15},{10,... | collective-permute-start | bytes 589832 | tf_op jit(solution)/shard_map/ppermute | solution.py:434
  78.9 5.0 %copy-start = (s32[4,256]{1,0:T(4,128)S(1)}, s32[4,256]{1,0:T(4,128)}, u32[]{:S(2)}) copy-start(s32[4,256]{1,0:T(4,128)} %pos_hbm.1) | copy-start | bytes 12292
  78.9 37.9 %all-to-all-start.1 = ((bf16[128,8,1152]{2,1,0:T(8,128)(2,1)}), bf16[128,8,1152]{2,1,0:T(8,128)(2,1)S(1)}, u32[]{:S(2)}, u32[]{:S(2)}) async-start(bf16[128,8,1152]{2,1,0:T(8,128)(2,1)} %bitcast.13), calls=%async_computation.1 | async-start | bytes 4718592 | tf_op jit(solution)/shard_map/all_to_all | solution.py:18

commit v6 on v5

--- a/solution.py
+++ b/solution.py
@@ -123,7 +123,7 @@
 
 def arm_kernel(
     width, class_ref, got_ref, mask_ref, row_hbm,
-    x_ref, t_ref, p_ref, pt_ref, gh_ref, own_ref, s0_ref, s1_ref, s2_ref, s3_ref,
+    x_ref, t_ref, p_ref, pt_ref, gh_ref, own_ref, s0_ref, s1_ref,
     w_ref, s_ref, gm_ref, other_ref, w_sem,
 ):
     slots = got_ref.shape[0]
@@ -171,9 +171,9 @@
         span = slice(c * edge, (c + 1) * edge)
         kept = w_ref[span, :] * keep_of(mask_ref, 2 * tiles + c, edge)
         t_ref[span, :] = mm(kept, x_ref[...]).astype(BF)
-    n4 = half // 4
-    n2 = half // 8
-    for d, ref in enumerate((s0_ref, s1_ref, s2_ref, s3_ref)):
+    n4 = half // 2
+    n2 = half // 4
+    for d, ref in enumerate((s0_ref, s1_ref)):
         ref[0:n4, :] = mm(take(other_ref[d * n4 : (d + 1) * n4, 0:1]), t_ref[...]).astype(BF)
         at = half + d * n2
         ref[n4:, :] = mm(take(other_ref[at : at + n2, 0:1]), t_ref[...]).astype(BF)
@@ -240,7 +240,7 @@
 
 
 def join_kernel(
-    width, extra_ref, arm_ref, r0_ref, r1_ref, r2_ref, r3_ref, kept_hbm, out_hbm,
+    width, extra_ref, arm_ref, r0_ref, r1_ref, kept_hbm, out_hbm,
     out_ref, s_ref, e_ref, out_sem,
 ):
     slots = out_ref.shape[0]
@@ -254,11 +254,14 @@
             out_ref.at[span, :], out_hbm.at[span, pl.ds(width, width + 128)], out_sem.at[c]
         )
 
-    for d, ref in enumerate((r0_ref, r1_ref, r2_ref, r3_ref)):
+    for d in range(4):
+        ref = (r0_ref, r1_ref)[d // 2]
         span = slice(d * STEP, (d + 1) * STEP)
-        four = arm_ref[d * n4 : (d + 1) * n4, :] + ref[0:n4, :].astype(F32)
+        at = d % 2 * n4
+        four = arm_ref[d * n4 : (d + 1) * n4, :] + ref[at : at + n4, :].astype(F32)
         at = half + d * n2
-        two = arm_ref[at : at + n2, :] + ref[n4:, :].astype(F32)
+        to = 2 * n4 + d % 2 * n2
+        two = arm_ref[at : at + n2, :] + ref[to : to + n2, :].astype(F32)
         more = extra_ref[d * n4 : (d + 1) * n4, :]
         for j in range(0, width, 128):
             t = j // 128
@@ -275,7 +278,7 @@
 
 def tail_kernel(
     width, arrows, reply_ref, key_ref, pre_hbm, up_hbm, down_hbm, out_ref,
-    pick_ref, part_ref, pre_ref, up_ref, down_ref, agg_ref, acc_ref, sem,
+    pick_ref, fold_ref, flat_ref, pre_ref, up_ref, down_ref, agg_ref, acc_ref, sem,
 ):
     slots = reply_ref.shape[0]
     count, nodes, chunk = pre_ref.shape
@@ -307,14 +310,19 @@
         for a in range(arrows):
             pick_ref[:, a * rows : (a + 1) * rows] = hits(goals[q], a)
         total = total + mm(pick_ref[...], reply_ref[:, q * width : (q + 1) * width])
+    folded = slots // 4
+    fold_ref[...] = reply_ref[:, 2 * width :].astype(F32)
     for t in range(width // 128):
-        goal = jnp.where(r % 4 == t, 8 + r // 4 * 2 + side, -1)
-        for a in range(arrows):
-            part_ref[t * nodes : (t + 1) * nodes, a * rows : (a + 1) * rows] = hits(goal, a)
-    rest = mm(part_ref[...], reply_ref[:, 2 * width :])
-    for t in range(width // 128):
-        span = slice(t * 128, (t + 1) * 128)
-        agg_ref[:, span] = (total[:, span] + rest[t * nodes : (t + 1) * nodes, :]).astype(BF)
+        flat_ref[:, t * 128 : (t + 1) * 128] = fold_ref[pl.ds(t, folded, stride=4), :].astype(BF)
+    lane = lax.broadcasted_iota(jnp.int32, (1, folded), 1)
+    per = folded // arrows
+    blk = lane % per // 2
+    goal = 8 + lane % 2 * 2 + (blk // 8 + blk // 2) % 2
+    key = key_ref[:, 0:1]
+    for a in range(1, arrows):
+        key = jnp.where(lane >= a * per, key_ref[:, a : a + 1], key)
+    total = total + mm(onehot(key == goal.astype(F32)), flat_ref[...])
+    agg_ref[...] = total.astype(BF)
     acc_ref[...] = jnp.zeros(acc_ref.shape, F32)
     for c in range(count):
         loads[c][0].wait()
@@ -330,13 +338,15 @@
 PRE = BF
 
 
-def neighbours(dx, dy):
+def neighbours(arrows, move):
     pairs = []
-    for x in range(4):
-        for y in range(4):
-            for z in range(2):
-                to = ((x + dx) % 4) * 8 + ((y + dy) % 4) * 2 + z
-                pairs.append((x * 8 + y * 2 + z, to))
+    for a in range(arrows):
+        for x in range(4):
+            for y in range(4):
+                for z in range(2):
+                    to_x = (x + move * (1 - a % 2)) % 4
+                    to_y = (y + move * (a % 2)) % 4
+                    pairs.append((a * 32 + x * 8 + y * 2 + z, a * 32 + to_x * 8 + to_y * 2 + z))
     return pairs
 
 
@@ -402,12 +412,12 @@
     side = ((blk // 8 + blk // 2) % 2).astype(jnp.int32).reshape(1)
     sm = pl.BlockSpec(memory_space=pltpu.SMEM)
     half = rows // 2
-    part = jax.ShapeDtypeStruct((half // 4 + half // 8, width), BF)
+    part = jax.ShapeDtypeStruct((half // 2 + half // 4, width), BF)
     full = jax.ShapeDtypeStruct((size, width), BF)
     x, t, p, pt, gh, own, *given = pl.pallas_call(
         functools.partial(arm_kernel, width),
         in_specs=[sm, VM, VM, HB],
-        out_specs=[VM] * 10,
+        out_specs=[VM] * 8,
         out_shape=[
             full,
             full,
@@ -417,8 +427,6 @@
             jax.ShapeDtypeStruct((half + half // 2, 128), F32),
             part,
             part,
-            part,
-            part,
         ],
         scratch_shapes=[
             pltpu.VMEM((size, size), BF),
@@ -431,7 +439,7 @@
         name="arms",
     )(side, got, keep, in_hbm(row_values))
     taken = [
-        lax.ppermute(g, "blk", neighbours(*move)) for g, move in zip(given, ((1, 0), (3, 0), (0, 1), (0, 3)))
+        lax.ppermute(g, ("arrow", "blk"), neighbours(arrows, move)) for g, move in zip(given, (1, 3))
     ]
     reply, extra, arm = pl.pallas_call(
         functools.partial(block_kernel, width),
@@ -455,10 +463,10 @@
     )(got, x, t, p, pt, gh, own, keep, in_hbm(diag_values), in_hbm(column_values))
     reply = pl.pallas_call(
         functools.partial(join_kernel, width),
-        in_specs=[VM] * 6 + [HB],
+        in_specs=[VM] * 4 + [HB],
         out_specs=HB,
         out_shape=pltpu.HBM((rows, 2 * width + 128), BF),
-        input_output_aliases={6: 0},
+        input_output_aliases={4: 0},
         scratch_shapes=[
             pltpu.VMEM((rows, width + 128), BF),
             pltpu.VMEM((4, width // 128, STEP, 128), F32),
@@ -477,7 +485,8 @@
         out_shape=jax.ShapeDtypeStruct((row_count, width), BF),
         scratch_shapes=[
             pltpu.VMEM((row_count, rows), BF),
-            pltpu.VMEM((row_count * (width // 128), rows), BF),
+            pltpu.VMEM((rows, 128), F32),
+            pltpu.VMEM((rows // 4, width), BF),
             pltpu.VMEM((count, row_count, CHUNK), PRE),
             pltpu.VMEM((count, width, CHUNK), BF),
             pltpu.VMEM((hidden, width), BF),

time: 126 us -> 121 us (0.960)
  Pallas kernels: 35.3 us -> 32.1 us
  starting transfers between devices: 21.9 us -> 20 us
    ppermute x4 -> x2, starting transfers between devices: 5.41 us -> 2.75 us  [body(): lax.ppermute(g, ('arrow', 'blk'), neighbours(arrows, move))]
    pallas_call x1, Pallas kernels: 8.82 us -> 6.26 us  [body(): pl.pallas_call(functools.partial(tail_kernel, width, arrows), in_specs=[V...]
  transfers between devices with their start and end apart: 6 -> 4, of which waited for: 2 -> 2; matrix products, arithmetic and copies ran while one was open for 0% -> 0% of each run, Pallas kernels for 12% -> 13%
where the time goes in v6:
time: 121 us
  waiting for transfers between devices  68 us (56%)
  Pallas kernels  32.1 us (27%)
  starting transfers between devices  20 us (17%)
    all_to_all x2, waiting for transfers between devices, exchange(): lax.all_to_all(block, ('arrow', 'blk'), split_axis=0, concat_axis=0, tile...  68 us
    all_to_all x2, starting transfers between devices, exchange(): lax.all_to_all(block, ('arrow', 'blk'), split_axis=0, concat_axis=0, tile...  17.2 us
    pallas_call x1, Pallas kernels, body(): pl.pallas_call(functools.partial(prep_kernel, arrows, size, width), grid=...  8.3 us
    pallas_call x1, Pallas kernels, body(): pl.pallas_call(functools.partial(block_kernel, width), in_specs=[VM] * 8...  7.13 us
    pallas_call x1, Pallas kernels, body(): pl.pallas_call(functools.partial(tail_kernel, width, arrows), in_specs=[V...  6.26 us
    pallas_call x1, Pallas kernels, body(): pl.pallas_call(functools.partial(arm_kernel, width), in_specs=[sm, VM, VM...  5.35 us
    pallas_call x1, Pallas kernels, body(): pl.pallas_call(functools.partial(pack_kernel, size, width), in_specs=[HB,...  3.85 us
    ppermute x2, starting transfers between devices, body(): lax.ppermute(g, ('arrow', 'blk'), neighbours(arrows, move))  2.75 us
  transfers between devices with their start and end apart: 4, of which 2 were waited for; matrix products, arithmetic and copies ran while one was open for 0% of the time, Pallas kernels for 13%

profile of v6, /device:TPU:1, one launch (start us, length us, event | category | flops | bytes accessed | tf_op | source)
XLA Modules:
  0.0 120.7 jit_solution(1071600472614903392)
XLA Ops:
  0.0 3.9 %pack.1 = bf16[1024,1664]{1,0:T(8,128)(2,1)} custom-call(bf16[256,512]{1,0:T(8,128)(2,1)} %feat_ref.1, s32[4,256]{1,0:T(4,128)} %pos_hbm.1), custom_call_target="tpu_custom_call" | custom-call | tf_op jit(solution)/shard_map/pack/pallas_call | solution.py:371
  3.9 0.0 copy-start.1
  3.9 11.5 %all-to-all-start = ((bf16[128,8,1664]{2,1,0:T(8,128)(2,1)}), bf16[128,8,1664]{2,1,0:T(8,128)(2,1)S(1)}, u32[]{:S(2)}, u32[]{:S(2)}) async-start(bf16[128,8,1664]{2,1,0:T(8,128)(2,1)} %bitcast.12), calls=%async_computation | async-start | bytes 6815744 | tf_op jit(solution)/shard_map/all_to_all | solution.py:18
  15.4 0.0 copy-done.1
  15.4 0.1 copy.10
  15.5 0.1 broadcast_bitcast_fusion.mask_ref
  15.6 43.5 %all-to-all-done = bf16[128,8,1664]{2,1,0:T(8,128)(2,1)S(1)} async-done(((bf16[128,8,1664]{2,1,0:T(8,128)(2,1)}), bf16[128,8,1664]{2,1,0:T(8,128)(2,1)S(1)}, u32[]{:S(2)}, u32[]{:S(2)}) %all-to-all-start) | async-done | bytes 3407904 | tf_op jit(solution)/shard_map/all_to_all | solution.py:18
  59.1 5.4 %arms.1 = (bf16[1024,512]{1,0:T(8,128)(2,1)S(1)}, bf16[1024,512]{1,0:T(8,128)(2,1)S(1)}, f32[2048,128]{1,0:T(8,128)S(1)}, f32[8,2048]{1,0:T(8,128)S(1)}, bf16[51...) custom-call(s32[1]{0:T(128)} %bitcast.2.class_ref, ...), custom_call_target="tpu_custom_call" | custom-call | tf_op jit(solution)/shard_map/arms/pallas_call | solution.py:417
  64.5 1.5 %collective-permute-start = (bf16[384,512]{1,0:T(8,128)(2,1)S(1)}, bf16[384,512]{1,0:T(8,128)(2,1)S(1)}, u32[]{:S(2)}, u32[]{:S(2)}) collective-permute-start(bf16[384,512]{1,0:T(8,128)(2,1)S(1)} %get-tuple-element.27), channel_id=1, source_target_pairs={{0,8},{1,9},{2,10},{3,11},{4,12},{5,13},{6,14},{7,15},{8,16},{9,17... | collective-permute-start | bytes 1179656 | tf_op jit(solution)/shard_map/ppermute | solution.py:442
  65.9 1.3 %collective-permute-start.1 = (bf16[384,512]{1,0:T(8,128)(2,1)S(1)}, bf16[384,512]{1,0:T(8,128)(2,1)S(1)}, u32[]{:S(2)}, u32[]{:S(2)}) collective-permute-start(bf16[384,512]{1,0:T(8,128)(2,1)S(1)} %get-tuple-element.28), channel_id=1, source_target_pairs={{0,24},{1,25},{2,26},{3,27},{4,28},{5,29},{6,30},{7,31},{8,0},{9,1... | collective-permute-start | bytes 1179656 | tf_op jit(solution)/shard_map/ppermute | solution.py:442
  67.2 7.1 %blocks.1 = (bf16[1024,1152]{1,0:T(8,128)(2,1)}, f32[512,512]{1,0:T(8,128)S(1)}, f32[768,512]{1,0:T(8,128)S(1)}) custom-call(bf16[1024,1664]{1,0:T(8,128)(2,1)S(1)} %bitcast.9, bf16[1024,512]{1,0:T(8,128)(2,1)S(1)} %get-tuple-element.19.x_ref, bf16[1024,512]{1,0:T(8,128)(2,1)S(1)} %get-tuple-element.20.t_ref, f32[2048,128]{1,0:T(8,128)S(1)} %get-tuple-element.21.p_ref, ...), custom_call_target="tpu_custom_call" | custom-call | tf_op jit(solution)/shard_map/blocks/pallas_call | solution.py:444
  74.4 0.0 collective-permute-done.r0_ref
  74.4 0.0 collective-permute-done.1.r1_ref
  74.4 1.2 %join.1 = bf16[1024,1152]{1,0:T(8,128)(2,1)} custom-call(f32[512,512]{1,0:T(8,128)S(1)} %get-tuple-element.25.extra_ref, f32[768,512]{1,0:T(8,128)S(1)} %get-tuple-element.26.arm_ref, bf16[384,512]{1,0:T(8,128)(2,1)S(1)} %collective-permute-done.r0_ref, bf16[384,512]{1,0:T(8,128)(2,1)S(1)} %collective-permute-done.1.r1_ref, ...), custom_call_target="tpu_custom_call", output_to_operand_aliasing={{}: (4, {})} | custom-call | tf_op jit(solution)/shard_map/join/pallas_call | solution.py:464
  75.6 0.0 copy-start
  75.6 5.8 %all-to-all-start.1 = ((bf16[128,8,1152]{2,1,0:T(8,128)(2,1)}), bf16[128,8,1152]{2,1,0:T(8,128)(2,1)S(1)}, u32[]{:S(2)}, u32[]{:S(2)}) async-start(bf16[128,8,1152]{2,1,0:T(8,128)(2,1)} %bitcast.13), calls=%async_computation.1 | async-start | bytes 4718592 | tf_op jit(solution)/shard_map/all_to_all | solution.py:18
  81.4 0.0 copy-done
  81.4 0.1 copy.11
  81.5 8.3 %prep.1 = (f32[256,128]{1,0:T(8,128)S(1)}, bf16[4,256,1024]{2,1,0:T(8,128)(2,1)}, bf16[4,512,1024]{2,1,0:T(8,128)(2,1)}) custom-call(s32[256,4]{1,0:T(8,128)S(1)} %bitcast.11, bf16[256,512]{1,0:T(8,128)(2,1)} %feat_ref.1, bf16[1024,4096]{1,0:T(8,128)(2,1)} %w_ref.1), custom_call_target="tpu_custom_call" | custom-call | tf_op jit(solution)/shard_map/prep/pallas_call | solution.py:388
  89.8 24.5 %all-to-all-done.1 = bf16[128,8,1152]{2,1,0:T(8,128)(2,1)S(1)} async-done(((bf16[128,8,1152]{2,1,0:T(8,128)(2,1)}), bf16[128,8,1152]{2,1,0:T(8,128)(2,1)S(1)}, u32[]{:S(2)}, u32[]{:S(2)}) %all-to-all-start.1) | async-done | bytes 2359328 | tf_op jit(solution)/shard_map/all_to_all | solution.py:18
  114.3 6.3 %tail.1 = bf16[256,512]{1,0:T(8,128)(2,1)} custom-call(bf16[1024,1152]{1,0:T(8,128)(2,1)S(1)} %bitcast.10, f32[256,128]{1,0:T(8,128)S(1)} %get-tuple-element.30.key_ref, bf16[4,256,1024]{2,1,0:T(8,128)(2,1)} %get-tuple-element.31.pre_hbm, bf16[4,512,1024]{2,1,0:T(8,128)(2,1)} %get-tuple-element.32.up_hbm, bf16[4096,512]{1,0:T(8,128)(2,1)} %down_hbm.1), custom_call_target="tpu_custom_call" | custom-call | tf_op jit(solution)/shard_map/tail/pallas_call | solution.py:481
  (1 shorter events, 0.0 us)
Async XLA Ops:
  3.9 11.5 %copy-start.1 = (s32[3,8,8]{2,1,0:T(8,128)S(1)}, s32[3,8,8]{2,1,0:T(8,128)}, u32[]{:S(2)}) copy-start(s32[3,8,8]{2,1,0:T(8,128)} %param.13) | copy-start | bytes 2308
  3.9 55.2 %all-to-all-start = ((bf16[128,8,1664]{2,1,0:T(8,128)(2,1)}), bf16[128,8,1664]{2,1,0:T(8,128)(2,1)S(1)}, u32[]{:S(2)}, u32[]{:S(2)}) async-start(bf16[128,8,1664]{2,1,0:T(8,128)(2,1)} %bitcast.12), calls=%async_computation | async-start | bytes 6815744 | tf_op jit(solution)/shard_map/all_to_all | solution.py:18
  64.5 9.9 %collective-permute-start = (bf16[384,512]{1,0:T(8,128)(2,1)S(1)}, bf16[384,512]{1,0:T(8,128)(2,1)S(1)}, u32[]{:S(2)}, u32[]{:S(2)}) collective-permute-start(bf16[384,512]{1,0:T(8,128)(2,1)S(1)} %get-tuple-element.27), channel_id=1, source_target_pairs={{0,8},{1,9},{2,10},{3,11},{4,12},{5,13},{6,14},{7,15},{8,16},{9,17... | collective-permute-start | bytes 1179656 | tf_op jit(solution)/shard_map/ppermute | solution.py:442
  65.9 8.4 %collective-permute-start.1 = (bf16[384,512]{1,0:T(8,128)(2,1)S(1)}, bf16[384,512]{1,0:T(8,128)(2,1)S(1)}, u32[]{:S(2)}, u32[]{:S(2)}) collective-permute-start(bf16[384,512]{1,0:T(8,128)(2,1)S(1)} %get-tuple-element.28), channel_id=1, source_target_pairs={{0,24},{1,25},{2,26},{3,27},{4,28},{5,29},{6,30},{7,31},{8,0},{9,1... | collective-permute-start | bytes 1179656 | tf_op jit(solution)/shard_map/ppermute | solution.py:442
  75.6 5.8 %copy-start = (s32[4,256]{1,0:T(4,128)S(1)}, s32[4,256]{1,0:T(4,128)}, u32[]{:S(2)}) copy-start(s32[4,256]{1,0:T(4,128)} %pos_hbm.1) | copy-start | bytes 12292
  75.6 38.7 %all-to-all-start.1 = ((bf16[128,8,1152]{2,1,0:T(8,128)(2,1)}), bf16[128,8,1152]{2,1,0:T(8,128)(2,1)S(1)}, u32[]{:S(2)}, u32[]{:S(2)}) async-start(bf16[128,8,1152]{2,1,0:T(8,128)(2,1)} %bitcast.13), calls=%async_computation.1 | async-start | bytes 4718592 | tf_op jit(solution)/shard_map/all_to_all | solution.py:18

commit v7 on v6

--- a/solution.py
+++ b/solution.py
@@ -34,8 +34,13 @@
     return jnp.where(mask, 1.0, 0.0).astype(BF)
 
 
+def side_of(blk):
+    return (blk // 8 + blk // 2) % 2
+
+
 def pack_kernel(
-    block_rows, width, feat_hbm, pos_hbm, out_hbm, feat_ref, pos_ref, out_ref, in_sem, out_sem
+    block_rows, width, feat_hbm, pos_hbm, out_hbm,
+    feat_ref, pos_ref, out_ref, fold_ref, in_sem, out_sem,
 ):
     nodes = feat_ref.shape[0]
     arrows = pos_ref.shape[0]
@@ -52,7 +57,11 @@
     slot = lax.broadcasted_iota(jnp.int32, (rows, nodes), 0)
     r = slot % 8
     rf = r.astype(F32)
-    shared = (r // 2 + 8).astype(F32)
+    side = side_of(slot // 8)
+    shared = jnp.where(r % 2 == 0, r // 2 + 8, r - 1 + side).astype(F32)
+    last = (8 + r // 4 * 2 + side).astype(F32)
+    pair = lax.broadcasted_iota(jnp.int32, (rows // 4, nodes), 0)
+    folded = (8 + pair % 2 * 2 + side_of(pair // 2)).astype(F32)
     code_row = lax.broadcasted_iota(jnp.int32, (128, nodes), 0)
     for copy in loads:
         copy.wait()
@@ -71,17 +80,22 @@
         picks = (
             onehot(rank == rf),
             onehot(jnp.where(r % 2 == 0, rank, head) == shared),
-            onehot(head == rf),
+            onehot(head == last),
         )
         high = (within // 32 + 1).astype(F32)
         low = (within % 32).astype(F32)
         span = pl.ds(a * rows, rows)
         codes = jnp.zeros((rows, 128), F32)
+        rest = mm(onehot(head[0 : rows // 4, :] == folded), feats)
+        for t in range(width // 128):
+            fold_ref[a, pl.ds(t, rows // 4, stride=4), :] = rest[:, t * 128 : (t + 1) * 128]
+        out_ref[span, 2 * width : 2 * width + 128] = fold_ref[a].astype(BF)
         for q in range(3):
-            out_ref[span, q * width : (q + 1) * width] = mm(picks[q], feats).astype(BF)
+            if q < 2:
+                out_ref[span, q * width : (q + 1) * width] = mm(picks[q], feats).astype(BF)
             table = jnp.where(code_row == 2 * q, high, jnp.where(code_row == 2 * q + 1, low, 0.0))
             codes = codes + mm_nt(picks[q], table.astype(BF))
-        out_ref[span, 3 * width :] = codes.astype(BF)
+        out_ref[span, 2 * width + 128 :] = codes.astype(BF)
         store(a).start()
     for a in range(arrows):
         store(a).wait()
@@ -121,10 +135,40 @@
     return onehot(places == ids)
 
 
+def head_kernel(width, got_ref, known_ref, e0_ref, e1_ref, p_ref, s_ref, f_ref):
+    slots = got_ref.shape[0]
+    four = slots // 4
+    two = slots // 8
+    group = four + two
+    codes = got_ref[:, 2 * width + 128 :].astype(F32)
+    p_ref[...] = (codes - 1.0) * 32.0 + pltpu.roll(codes, 127, 1)
+    f_ref[...] = got_ref[:, 2 * width : 2 * width + 128].astype(F32)
+    for t in range(width // 128):
+        at = width + t * 128
+        s_ref[t] = got_ref[:, at : at + 128].astype(F32)
+    row = lax.broadcasted_iota(jnp.int32, (8, width), 0)
+    for h, ref in enumerate((e0_ref, e1_ref)):
+        base = h * (slots // 2)
+        at = h * group
+        some = p_ref[pl.ds(base + 1, four, stride=2), :][:, 2:3]
+        known_ref[at : at + four, :] = jnp.broadcast_to(some, (four, 128))
+        some = p_ref[pl.ds(base, two, stride=4), :][:, 4:5]
+        known_ref[at + four : at + group, :] = jnp.broadcast_to(some, (two, 128))
+        for t in range(width // 128):
+            span = slice(t * 128, (t + 1) * 128)
+            ref[0:four, span] = s_ref[t, pl.ds(base + 1, four, stride=2), :].astype(BF)
+            ref[four:group, span] = f_ref[pl.ds(base + t, two, stride=4), :].astype(BF)
+        place = known_ref[at : at + group, :].T[0:1, :]
+        place = jnp.concatenate([place, jnp.zeros((1, width - group), F32)], axis=1)
+        high = jnp.floor(place * (1.0 / 32.0)) + 1.0
+        low = place - (high - 1.0) * 32.0
+        ref[group:, :] = jnp.where(row == 0, high, jnp.where(row == 1, low, 0.0)).astype(BF)
+
+
 def arm_kernel(
-    width, class_ref, got_ref, mask_ref, row_hbm,
-    x_ref, t_ref, p_ref, pt_ref, gh_ref, own_ref, s0_ref, s1_ref,
-    w_ref, s_ref, gm_ref, other_ref, w_sem,
+    width, got_ref, known_ref, mask_ref, row_hbm,
+    x_ref, t_ref, p_ref, s0_ref, s1_ref,
+    w_ref, pt_ref, s_ref, gm_ref, w_sem,
 ):
     slots = got_ref.shape[0]
     size = x_ref.shape[0]
@@ -132,25 +176,16 @@
     lanes = range(0, width, 128)
     load = pltpu.make_async_copy(row_hbm, w_ref, w_sem)
     load.start()
-    codes = got_ref[:, 3 * width :].astype(F32)
+    codes = got_ref[:, 2 * width + 128 :].astype(F32)
     place = (codes - 1.0) * 32.0 + pltpu.roll(codes, 127, 1)
     p_ref[0:slots, :] = place
     pt_ref[:, 0:slots] = place.T[0:8, :]
+    part = p_ref[pl.ds(0, half, stride=2), :]
+    p_ref[slots:, :] = part
+    pt_ref[:, slots:] = part.T[0:8, :]
     for j in lanes:
         s_ref[j // 128] = got_ref[:, width + j : width + j + 128].astype(F32)
-    for k, ref in enumerate((gm_ref, gh_ref)):
-        part = p_ref[pl.ds(k, half, stride=2), :]
-        at = slots + k * half
-        p_ref[at : at + half, :] = part
-        pt_ref[:, at : at + half] = part.T[0:8, :]
-        for j in lanes:
-            ref[:, j : j + 128] = s_ref[j // 128, pl.ds(k, half, stride=2), :].astype(BF)
-    first = class_ref[0] == 0
-    for at, count, col, to in ((0, half, 4, 0), (slots + half, half // 2, 2, half)):
-        even = p_ref[pl.ds(at, count, stride=2), :][:, col : col + 1]
-        odd = p_ref[pl.ds(at + 1, count, stride=2), :][:, col : col + 1]
-        own_ref[to : to + count, :] = jnp.broadcast_to(jnp.where(first, even, odd), (count, 128))
-        other_ref[to : to + count, :] = jnp.broadcast_to(jnp.where(first, odd, even), (count, 128))
+        gm_ref[:, j : j + 128] = s_ref[j // 128, pl.ds(0, half, stride=2), :].astype(BF)
 
     def unpack(c, carry):
         def put(row, start, count):
@@ -171,20 +206,17 @@
         span = slice(c * edge, (c + 1) * edge)
         kept = w_ref[span, :] * keep_of(mask_ref, 2 * tiles + c, edge)
         t_ref[span, :] = mm(kept, x_ref[...]).astype(BF)
-    n4 = half // 2
-    n2 = half // 4
+    group = s0_ref.shape[0]
     for d, ref in enumerate((s0_ref, s1_ref)):
-        ref[0:n4, :] = mm(take(other_ref[d * n4 : (d + 1) * n4, 0:1]), t_ref[...]).astype(BF)
-        at = half + d * n2
-        ref[n4:, :] = mm(take(other_ref[at : at + n2, 0:1]), t_ref[...]).astype(BF)
+        ref[...] = mm(take(known_ref[d * group : (d + 1) * group, 0:1]), t_ref[...]).astype(BF)
 
 
 def block_kernel(
-    width, got_ref, x_ref, t_ref, p_ref, pt_ref, gh_ref, own_ref, mask_ref, diag_hbm, col_hbm,
+    width, x_ref, t_ref, p_ref, e0_ref, e1_ref, f0_ref, f1_ref, mask_ref, diag_hbm, col_hbm,
     out_hbm, extra_ref, arm_ref,
-    w_ref, x0_ref, y_ref, out_ref, w_sem, out_sem,
+    w_ref, x0_ref, y_ref, out_ref, g_ref, pt_ref, own_ref, w_sem, out_sem,
 ):
-    slots = got_ref.shape[0]
+    slots = out_ref.shape[0]
     size = x_ref.shape[0]
     half = slots // 2
     loads = [
@@ -194,16 +226,18 @@
     for copy in loads:
         copy.start()
 
+    group = arm_ref.shape[0] // 2
+    for i, ref in enumerate((e0_ref, e1_ref, f0_ref, f1_ref)):
+        span = slice(i * group, (i + 1) * group)
+        g_ref[span, :] = ref[0:group, :]
+        codes = ref[group:, :].astype(F32)
+        pt_ref[0:1, span] = ((codes[0:1, :] - 1.0) * 32.0 + codes[1:2, :])[:, 0:group]
+    own_ref[...] = jnp.broadcast_to(pt_ref[0:1, 2 * group :], (128, 2 * group)).T
+
     def unpack(c, carry):
-        def put(row, start, count):
-            ids = (lax.broadcasted_iota(jnp.int32, (STEP, count), 0) + c * STEP).astype(F32)
-            return onehot(pt_ref[row : row + 1, start : start + count] == ids)
-
+        ids = lax.broadcasted_iota(jnp.int32, (STEP, g_ref.shape[0]), 0) + c * STEP
         span = pl.ds(pl.multiple_of(c * STEP, STEP), STEP)
-        x0_ref[span, :] = (
-            mm(put(4, 0, slots), got_ref[:, 2 * width : 3 * width])
-            + mm(put(2, slots + half, half), gh_ref[...])
-        ).astype(BF)
+        x0_ref[span, :] = mm(onehot(pt_ref[0:1, :] == ids.astype(F32)), g_ref[...]).astype(BF)
         return carry
 
     lax.fori_loop(0, size // STEP, unpack, 0)
@@ -257,11 +291,11 @@
     for d in range(4):
         ref = (r0_ref, r1_ref)[d // 2]
         span = slice(d * STEP, (d + 1) * STEP)
+        base = d // 2 * ref.shape[0]
         at = d % 2 * n4
-        four = arm_ref[d * n4 : (d + 1) * n4, :] + ref[at : at + n4, :].astype(F32)
-        at = half + d * n2
-        to = 2 * n4 + d % 2 * n2
-        two = arm_ref[at : at + n2, :] + ref[to : to + n2, :].astype(F32)
+        four = arm_ref[base + at : base + at + n4, :] + ref[at : at + n4, :].astype(F32)
+        at = 2 * n4 + d % 2 * n2
+        two = arm_ref[base + at : base + at + n2, :] + ref[at : at + n2, :].astype(F32)
         more = extra_ref[d * n4 : (d + 1) * n4, :]
         for j in range(0, width, 128):
             t = j // 128
@@ -298,7 +332,7 @@
     lane = lax.broadcasted_iota(jnp.int32, (1, rows), 1)
     blk = lane // 8
     block = blk * 16
-    side = (blk // 8 + blk // 2) % 2
+    side = 1 - side_of(blk)
     r = lane % 8
 
     def hits(goal, a):
@@ -317,7 +351,7 @@
     lane = lax.broadcasted_iota(jnp.int32, (1, folded), 1)
     per = folded // arrows
     blk = lane % per // 2
-    goal = 8 + lane % 2 * 2 + (blk // 8 + blk // 2) % 2
+    goal = 9 + lane % 2 * 2 - side_of(blk)
     key = key_ref[:, 0:1]
     for a in range(1, arrows):
         key = jnp.where(lane >= a * per, key_ref[:, a : a + 1], key)
@@ -364,7 +398,7 @@
     hidden = down_weight.shape[0]
     tiles = tile_masks.shape[1]
     rows = devices * 8
-    longest = 3 * width + 128
+    longest = 2 * width + 256
     count = hidden // CHUNK
     dma = pltpu.SemaphoreType.DMA
 
@@ -377,6 +411,7 @@
             pltpu.VMEM(features.shape, BF),
             pltpu.VMEM(positions.shape, jnp.int32),
             pltpu.VMEM((rows, longest), BF),
+            pltpu.VMEM((arrows, rows // arrows, 128), F32),
             dma((2,)),
             dma((arrows,)),
         ],
@@ -408,39 +443,42 @@
     )(positions.T, in_hbm(features), in_hbm(up_weight))
     keep = jnp.repeat(tile_masks.astype(F32), size // tiles, axis=2).reshape(3 * tiles, size)
 
-    blk = lax.axis_index("blk")
-    side = ((blk // 8 + blk // 2) % 2).astype(jnp.int32).reshape(1)
-    sm = pl.BlockSpec(memory_space=pltpu.SMEM)
     half = rows // 2
-    part = jax.ShapeDtypeStruct((half // 2 + half // 4, width), BF)
+    group = half // 2 + half // 4
+    part = jax.ShapeDtypeStruct((group, width), BF)
     full = jax.ShapeDtypeStruct((size, width), BF)
-    x, t, p, pt, gh, own, *given = pl.pallas_call(
+    piece = jax.ShapeDtypeStruct((group + 8, width), BF)
+    known, *heads = pl.pallas_call(
+        functools.partial(head_kernel, width),
+        in_specs=[VM],
+        out_specs=[VM] * 3,
+        out_shape=[jax.ShapeDtypeStruct((2 * group, 128), F32), piece, piece],
+        scratch_shapes=[
+            pltpu.VMEM((rows, 128), F32),
+            pltpu.VMEM((width // 128, rows, 128), F32),
+            pltpu.VMEM((rows, 128), F32),
+        ],
+        compiler_params=params(8),
+        name="heads",
+    )(got)
+    moves = [neighbours(arrows, m) for m in (1, 3)]
+    heads += [lax.ppermute(g, ("arrow", "blk"), m) for g, m in zip(heads, moves)]
+    x, t, p, *given = pl.pallas_call(
         functools.partial(arm_kernel, width),
-        in_specs=[sm, VM, VM, HB],
-        out_specs=[VM] * 8,
-        out_shape=[
-            full,
-            full,
-            jax.ShapeDtypeStruct((2 * rows, 128), F32),
-            jax.ShapeDtypeStruct((8, 2 * rows), F32),
-            jax.ShapeDtypeStruct((half, width), BF),
-            jax.ShapeDtypeStruct((half + half // 2, 128), F32),
-            part,
-            part,
-        ],
+        in_specs=[VM, VM, VM, HB],
+        out_specs=[VM] * 5,
+        out_shape=[full, full, jax.ShapeDtypeStruct((rows + half, 128), F32), part, part],
         scratch_shapes=[
             pltpu.VMEM((size, size), BF),
+            pltpu.VMEM((8, rows + half), F32),
             pltpu.VMEM((width // 128, rows, 128), F32),
             pltpu.VMEM((half, width), BF),
-            pltpu.VMEM((half + half // 2, 128), F32),
             dma,
         ],
         compiler_params=params(16),
         name="arms",
-    )(side, got, keep, in_hbm(row_values))
-    taken = [
-        lax.ppermute(g, ("arrow", "blk"), neighbours(arrows, move)) for g, move in zip(given, (1, 3))
-    ]
+    )(got, known, keep, in_hbm(row_values))
+    taken = [lax.ppermute(g, ("arrow", "blk"), m) for g, m in zip(given, moves)]
     reply, extra, arm = pl.pallas_call(
         functools.partial(block_kernel, width),
         in_specs=[VM] * 8 + [HB, HB],
@@ -448,19 +486,22 @@
         out_shape=[
             pltpu.HBM((rows, 2 * width + 128), BF),
             jax.ShapeDtypeStruct((half, width), F32),
-            jax.ShapeDtypeStruct((half + half // 2, width), F32),
+            jax.ShapeDtypeStruct((2 * group, width), F32),
         ],
         scratch_shapes=[
             pltpu.VMEM((2, size, size), BF),
             pltpu.VMEM((size, width), BF),
             pltpu.VMEM((size, width), BF),
             pltpu.VMEM((rows, width), BF),
+            pltpu.VMEM((4 * group, width), BF),
+            pltpu.VMEM((8, 4 * group), F32),
+            pltpu.VMEM((2 * group, 128), F32),
             dma((2,)),
             dma((rows // STEP,)),
         ],
         compiler_params=params(16),
         name="blocks",
-    )(got, x, t, p, pt, gh, own, keep, in_hbm(diag_values), in_hbm(column_values))
+    )(x, t, p, *heads, keep, in_hbm(diag_values), in_hbm(column_values))
     reply = pl.pallas_call(
         functools.partial(join_kernel, width),
         in_specs=[VM] * 4 + [HB],

time: 121 us -> 116 us (0.959)
  waiting for transfers between devices: 68 us -> 60 us
  starting transfers between devices: 20 us -> 22.7 us
    all_to_all x2, waiting for transfers between devices: 68 us -> 60 us  [exchange(): lax.all_to_all(block, ('arrow', 'blk'), split_axis=0, concat_axis=0, tile...]
    ppermute x2 -> x4, starting transfers between devices: 2.75 us -> 5.48 us  [the longest x2 2.75 us: body(): lax.ppermute(g, ('arrow', 'blk'), m)]
    pallas_call x1 -> x2, Pallas kernels: 5.35 us -> 5.47 us  [the longest x1 4.88 us: body(): pl.pallas_call(functools.partial(arm_kernel, width), in_specs=[VM, VM, VM...]
  transfers between devices with their start and end apart: 4 -> 6, of which waited for: 2 -> 2; matrix products, arithmetic and copies ran while one was open for 0% -> 0% of each run, Pallas kernels for 13% -> 18%
where the time goes in v7:
time: 116 us
  waiting for transfers between devices  60 us (52%)
  Pallas kernels  32.3 us (28%)
  starting transfers between devices  22.7 us (20%)
    all_to_all x2, waiting for transfers between devices, exchange(): lax.all_to_all(block, ('arrow', 'blk'), split_axis=0, concat_axis=0, tile...  60 us
    all_to_all x2, starting transfers between devices, exchange(): lax.all_to_all(block, ('arrow', 'blk'), split_axis=0, concat_axis=0, tile...  17.2 us
    pallas_call x1, Pallas kernels, body(): pl.pallas_call(functools.partial(prep_kernel, arrows, size, width), grid=...  8.32 us
    pallas_call x1, Pallas kernels, body(): pl.pallas_call(functools.partial(block_kernel, width), in_specs=[VM] * 8...  7.36 us
    pallas_call x1, Pallas kernels, body(): pl.pallas_call(functools.partial(tail_kernel, width, arrows), in_specs=[V...  6.26 us
    pallas_call x1, Pallas kernels, body(): pl.pallas_call(functools.partial(arm_kernel, width), in_specs=[VM, VM, VM...  4.88 us
    pallas_call x1, Pallas kernels, body(): pl.pallas_call(functools.partial(pack_kernel, size, width), in_specs=[HB,...  3.58 us
    ppermute x2, starting transfers between devices, body(): lax.ppermute(g, ('arrow', 'blk'), m)  2.75 us
  transfers between devices with their start and end apart: 6, of which 2 were waited for; matrix products, arithmetic and copies ran while one was open for 0% of the time, Pallas kernels for 18%

profile of v7, /device:TPU:1, one launch (start us, length us, event | category | flops | bytes accessed | tf_op | source)
XLA Modules:
  0.0 115.6 jit_solution(6624830632982782823)
XLA Ops:
  0.0 3.6 %pack.1 = bf16[1024,1280]{1,0:T(8,128)(2,1)} custom-call(bf16[256,512]{1,0:T(8,128)(2,1)} %feat_ref.1, s32[4,256]{1,0:T(4,128)} %pos_hbm.1), custom_call_target="tpu_custom_call" | custom-call | tf_op jit(solution)/shard_map/pack/pallas_call | solution.py:405
  3.6 0.0 copy-start.1
  3.6 11.5 %all-to-all-start = ((bf16[128,8,1280]{2,1,0:T(8,128)(2,1)}), bf16[128,8,1280]{2,1,0:T(8,128)(2,1)S(1)}, u32[]{:S(2)}, u32[]{:S(2)}) async-start(bf16[128,8,1280]{2,1,0:T(8,128)(2,1)} %bitcast.11), calls=%async_computation | async-start | bytes 5242880 | tf_op jit(solution)/shard_map/all_to_all | solution.py:18
  15.1 0.0 copy-done.1
  15.1 0.1 copy.10
  15.2 35.5 %all-to-all-done = bf16[128,8,1280]{2,1,0:T(8,128)(2,1)S(1)} async-done(((bf16[128,8,1280]{2,1,0:T(8,128)(2,1)}), bf16[128,8,1280]{2,1,0:T(8,128)(2,1)S(1)}, u32[]{:S(2)}, u32[]{:S(2)}) %all-to-all-start) | async-done | bytes 2621472 | tf_op jit(solution)/shard_map/all_to_all | solution.py:18
  50.7 0.6 heads.1
  51.3 0.4 collective-permute-start
  51.8 2.3 %collective-permute-start.1 = (bf16[392,512]{1,0:T(8,128)(2,1)S(1)}, bf16[392,512]{1,0:T(8,128)(2,1)S(1)}, u32[]{:S(2)}, u32[]{:S(2)}) collective-permute-start(bf16[392,512]{1,0:T(8,128)(2,1)S(1)} %get-tuple-element.24.e1_ref), channel_id=1, source_target_pairs={{0,24},{1,25},{2,26},{3,27},{4,28},{5,29},{6,30},{7,31},{8,0},{9,1... | collective-permute-start | bytes 1204232 | tf_op jit(solution)/shard_map/ppermute | solution.py:465
  54.1 0.1 broadcast_bitcast_fusion.mask_ref
  54.2 4.9 %arms.1 = (bf16[1024,512]{1,0:T(8,128)(2,1)S(1)}, bf16[1024,512]{1,0:T(8,128)(2,1)S(1)}, f32[1536,128]{1,0:T(8,128)S(1)}, bf16[384,512]{1,0:T(8,128)(2,1)S(1)}, bf16[384,512]{1,0:T(8,128)(2,1)S(1)}) custom-call(bf16[1024,1280]{1,0:T(8,128)(2,1)S(1)} %bitcast.8, f32[768,128]{1,0:T(8,128)S(1)} %get-tuple-element.19.known_ref, ...), custom_call_target="tpu_custom_call" | custom-call | tf_op jit(solution)/shard_map/arms/pallas_call | solution.py:466
  59.1 0.1 collective-permute-start.2
  59.1 2.7 %collective-permute-start.3 = (bf16[384,512]{1,0:T(8,128)(2,1)S(1)}, bf16[384,512]{1,0:T(8,128)(2,1)S(1)}, u32[]{:S(2)}, u32[]{:S(2)}) collective-permute-start(bf16[384,512]{1,0:T(8,128)(2,1)S(1)} %get-tuple-element.28), channel_id=1, source_target_pairs={{0,24},{1,25},{2,26},{3,27},{4,28},{5,29},{6,30},{7,31},{8,0},{9,1... | collective-permute-start | bytes 1179656 | tf_op jit(solution)/shard_map/ppermute | solution.py:481
  61.8 0.0 collective-permute-done.f0_ref
  61.8 0.0 collective-permute-done.1.f1_ref
  61.8 7.4 %blocks.1 = (bf16[1024,1152]{1,0:T(8,128)(2,1)}, f32[512,512]{1,0:T(8,128)S(1)}, f32[768,512]{1,0:T(8,128)S(1)}) custom-call(bf16[1024,512]{1,0:T(8,128)(2,1)S(1)} %get-tuple-element.20.x_ref, bf16[1024,512]{1,0:T(8,128)(2,1)S(1)} %get-tuple-element.21.t_ref, f32[1536,128]{1,0:T(8,128)S(1)} %get-tuple-element.22.p_ref, ...), custom_call_target="tpu_custom_call" | custom-call | tf_op jit(solution)/shard_map/blocks/pallas_call | solution.py:482
  69.2 0.0 collective-permute-done.2.r0_ref
  69.2 0.0 collective-permute-done.3.r1_ref
  69.2 1.3 %join.1 = bf16[1024,1152]{1,0:T(8,128)(2,1)} custom-call(f32[512,512]{1,0:T(8,128)S(1)} %get-tuple-element.25.extra_ref, f32[768,512]{1,0:T(8,128)S(1)} %get-tuple-element.26.arm_ref, bf16[384,512]{1,0:T(8,128)(2,1)S(1)} %collective-permute-done.2.r0_ref, bf16[384,512]{1,0:T(8,128)(2,1)S(1)} %collective-permute-done.3.r1_ref, ...), custom_call_target="tpu_custom_call", output_to_operand_aliasing={{}: (4, {})} | custom-call | tf_op jit(solution)/shard_map/join/pallas_call | solution.py:505
  70.5 0.0 copy-start
  70.5 5.7 %all-to-all-start.1 = ((bf16[128,8,1152]{2,1,0:T(8,128)(2,1)}), bf16[128,8,1152]{2,1,0:T(8,128)(2,1)S(1)}, u32[]{:S(2)}, u32[]{:S(2)}) async-start(bf16[128,8,1152]{2,1,0:T(8,128)(2,1)} %bitcast.12), calls=%async_computation.1 | async-start | bytes 4718592 | tf_op jit(solution)/shard_map/all_to_all | solution.py:18
  76.2 0.0 copy-done
  76.2 0.1 copy.11
  76.4 8.3 %prep.1 = (f32[256,128]{1,0:T(8,128)S(1)}, bf16[4,256,1024]{2,1,0:T(8,128)(2,1)}, bf16[4,512,1024]{2,1,0:T(8,128)(2,1)}) custom-call(s32[256,4]{1,0:T(8,128)S(1)} %bitcast.10, bf16[256,512]{1,0:T(8,128)(2,1)} %feat_ref.1, bf16[1024,4096]{1,0:T(8,128)(2,1)} %w_ref.1), custom_call_target="tpu_custom_call" | custom-call | tf_op jit(solution)/shard_map/prep/pallas_call | solution.py:423
  84.7 24.5 %all-to-all-done.1 = bf16[128,8,1152]{2,1,0:T(8,128)(2,1)S(1)} async-done(((bf16[128,8,1152]{2,1,0:T(8,128)(2,1)}), bf16[128,8,1152]{2,1,0:T(8,128)(2,1)S(1)}, u32[]{:S(2)}, u32[]{:S(2)}) %all-to-all-start.1) | async-done | bytes 2359328 | tf_op jit(solution)/shard_map/all_to_all | solution.py:18
  109.1 6.3 %tail.1 = bf16[256,512]{1,0:T(8,128)(2,1)} custom-call(bf16[1024,1152]{1,0:T(8,128)(2,1)S(1)} %bitcast.9, f32[256,128]{1,0:T(8,128)S(1)} %get-tuple-element.30.key_ref, bf16[4,256,1024]{2,1,0:T(8,128)(2,1)} %get-tuple-element.31.pre_hbm, bf16[4,512,1024]{2,1,0:T(8,128)(2,1)} %get-tuple-element.32.up_hbm, bf16[4096,512]{1,0:T(8,128)(2,1)} %down_hbm.1), custom_call_target="tpu_custom_call" | custom-call | tf_op jit(solution)/shard_map/tail/pallas_call | solution.py:522
  (1 shorter events, 0.0 us)
Async XLA Ops:
  3.6 11.5 %copy-start.1 = (s32[3,8,8]{2,1,0:T(8,128)S(1)}, s32[3,8,8]{2,1,0:T(8,128)}, u32[]{:S(2)}) copy-start(s32[3,8,8]{2,1,0:T(8,128)} %param.13) | copy-start | bytes 2308
  3.6 47.1 %all-to-all-start = ((bf16[128,8,1280]{2,1,0:T(8,128)(2,1)}), bf16[128,8,1280]{2,1,0:T(8,128)(2,1)S(1)}, u32[]{:S(2)}, u32[]{:S(2)}) async-start(bf16[128,8,1280]{2,1,0:T(8,128)(2,1)} %bitcast.11), calls=%async_computation | async-start | bytes 5242880 | tf_op jit(solution)/shard_map/all_to_all | solution.py:18
  51.3 10.5 %collective-permute-start = (bf16[392,512]{1,0:T(8,128)(2,1)S(1)}, bf16[392,512]{1,0:T(8,128)(2,1)S(1)}, u32[]{:S(2)}, u32[]{:S(2)}) collective-permute-start(bf16[392,512]{1,0:T(8,128)(2,1)S(1)} %get-tuple-element.23.e0_ref), channel_id=1, source_target_pairs={{0,8},{1,9},{2,10},{3,11},{4,12},{5,13},{6,14},{7,15},{8,16},{9,17... | collective-permute-start | bytes 1204232 | tf_op jit(solution)/shard_map/ppermute | solution.py:465
  51.8 10.0 %collective-permute-start.1 = (bf16[392,512]{1,0:T(8,128)(2,1)S(1)}, bf16[392,512]{1,0:T(8,128)(2,1)S(1)}, u32[]{:S(2)}, u32[]{:S(2)}) collective-permute-start(bf16[392,512]{1,0:T(8,128)(2,1)S(1)} %get-tuple-element.24.e1_ref), channel_id=1, source_target_pairs={{0,24},{1,25},{2,26},{3,27},{4,28},{5,29},{6,30},{7,31},{8,0},{9,1... | collective-permute-start | bytes 1204232 | tf_op jit(solution)/shard_map/ppermute | solution.py:465
  59.1 10.1 %collective-permute-start.2 = (bf16[384,512]{1,0:T(8,128)(2,1)S(1)}, bf16[384,512]{1,0:T(8,128)(2,1)S(1)}, u32[]{:S(2)}, u32[]{:S(2)}) collective-permute-start(bf16[384,512]{1,0:T(8,128)(2,1)S(1)} %get-tuple-element.27), channel_id=1, source_target_pairs={{0,8},{1,9},{2,10},{3,11},{4,12},{5,13},{6,14},{7,15},{8,16},{9,17... | collective-permute-start | bytes 1179656 | tf_op jit(solution)/shard_map/ppermute | solution.py:481
  59.1 10.1 %collective-permute-start.3 = (bf16[384,512]{1,0:T(8,128)(2,1)S(1)}, bf16[384,512]{1,0:T(8,128)(2,1)S(1)}, u32[]{:S(2)}, u32[]{:S(2)}) collective-permute-start(bf16[384,512]{1,0:T(8,128)(2,1)S(1)} %get-tuple-element.28), channel_id=1, source_target_pairs={{0,24},{1,25},{2,26},{3,27},{4,28},{5,29},{6,30},{7,31},{8,0},{9,1... | collective-permute-start | bytes 1179656 | tf_op jit(solution)/shard_map/ppermute | solution.py:481
  70.5 5.7 %copy-start = (s32[4,256]{1,0:T(4,128)S(1)}, s32[4,256]{1,0:T(4,128)}, u32[]{:S(2)}) copy-start(s32[4,256]{1,0:T(4,128)} %pos_hbm.1) | copy-start | bytes 12292
  70.5 38.7 %all-to-all-start.1 = ((bf16[128,8,1152]{2,1,0:T(8,128)(2,1)}), bf16[128,8,1152]{2,1,0:T(8,128)(2,1)S(1)}, u32[]{:S(2)}, u32[]{:S(2)}) async-start(bf16[128,8,1152]{2,1,0:T(8,128)(2,1)} %bitcast.12), calls=%async_computation.1 | async-start | bytes 4718592 | tf_op jit(solution)/shard_map/all_to_all | solution.py:18

commit v8 on v7

--- a/solution.py
+++ b/solution.py
@@ -85,16 +85,17 @@
         high = (within // 32 + 1).astype(F32)
         low = (within % 32).astype(F32)
         span = pl.ds(a * rows, rows)
-        codes = jnp.zeros((rows, 128), F32)
         rest = mm(onehot(head[0 : rows // 4, :] == folded), feats)
         for t in range(width // 128):
             fold_ref[a, pl.ds(t, rows // 4, stride=4), :] = rest[:, t * 128 : (t + 1) * 128]
         out_ref[span, 2 * width : 2 * width + 128] = fold_ref[a].astype(BF)
+        tables = []
         for q in range(3):
             if q < 2:
                 out_ref[span, q * width : (q + 1) * width] = mm(picks[q], feats).astype(BF)
             table = jnp.where(code_row == 2 * q, high, jnp.where(code_row == 2 * q + 1, low, 0.0))
-            codes = codes + mm_nt(picks[q], table.astype(BF))
+            tables.append(table.astype(BF))
+        codes = mm_nt(jnp.concatenate(picks, axis=1), jnp.concatenate(tables, axis=1))
         out_ref[span, 2 * width + 128 :] = codes.astype(BF)
         store(a).start()
     for a in range(arrows):
@@ -124,6 +125,7 @@
 
 
 STEP = 256
+WIDE = 512
 
 
 def keep_of(mask_ref, row, edge):
@@ -189,22 +191,23 @@
 
     def unpack(c, carry):
         def put(row, start, count):
-            ids = (lax.broadcasted_iota(jnp.int32, (STEP, count), 0) + c * STEP).astype(F32)
+            ids = (lax.broadcasted_iota(jnp.int32, (WIDE, count), 0) + c * WIDE).astype(F32)
             return onehot(pt_ref[row : row + 1, start : start + count] == ids)
 
-        span = pl.ds(pl.multiple_of(c * STEP, STEP), STEP)
+        span = pl.ds(pl.multiple_of(c * WIDE, WIDE), WIDE)
         x_ref[span, :] = (
             mm(put(0, 0, slots), got_ref[:, 0:width]) + mm(put(2, slots, half), gm_ref[...])
         ).astype(BF)
         return carry
 
-    lax.fori_loop(0, size // STEP, unpack, 0)
+    lax.fori_loop(0, size // WIDE, unpack, 0)
     load.wait()
     tiles = mask_ref.shape[0] // 3
     edge = size // tiles
-    for c in range(tiles):
-        span = slice(c * edge, (c + 1) * edge)
-        kept = w_ref[span, :] * keep_of(mask_ref, 2 * tiles + c, edge)
+    for c in range(0, tiles, 2):
+        span = slice(c * edge, (c + 2) * edge)
+        keep = [keep_of(mask_ref, 2 * tiles + c + i, edge) for i in range(2)]
+        kept = w_ref[span, :] * jnp.concatenate(keep, axis=0)
         t_ref[span, :] = mm(kept, x_ref[...]).astype(BF)
     group = s0_ref.shape[0]
     for d, ref in enumerate((s0_ref, s1_ref)):
@@ -235,12 +238,12 @@
     own_ref[...] = jnp.broadcast_to(pt_ref[0:1, 2 * group :], (128, 2 * group)).T
 
     def unpack(c, carry):
-        ids = lax.broadcasted_iota(jnp.int32, (STEP, g_ref.shape[0]), 0) + c * STEP
-        span = pl.ds(pl.multiple_of(c * STEP, STEP), STEP)
+        ids = lax.broadcasted_iota(jnp.int32, (WIDE, g_ref.shape[0]), 0) + c * WIDE
+        span = pl.ds(pl.multiple_of(c * WIDE, WIDE), WIDE)
         x0_ref[span, :] = mm(onehot(pt_ref[0:1, :] == ids.astype(F32)), g_ref[...]).astype(BF)
         return carry
 
-    lax.fori_loop(0, size // STEP, unpack, 0)
+    lax.fori_loop(0, size // WIDE, unpack, 0)
     for copy in loads:
         copy.wait()
     tiles = mask_ref.shape[0] // 3

time: 116 us -> 116 us (level)
  transfers between devices with their start and end apart: 6 -> 6, of which waited for: 2 -> 2; matrix products, arithmetic and copies ran while one was open for 0% -> 0% of each run, Pallas kernels for 18% -> 17%
where the time goes in v8:
time: 116 us; the launch traced here: 115 us
  waiting for transfers between devices  60 us (52%)
  Pallas kernels  31.8 us (27%)
  starting transfers between devices  22.9 us (20%)
    all_to_all x2, waiting for transfers between devices, exchange(): lax.all_to_all(block, ('arrow', 'blk'), split_axis=0, concat_axis=0, tile...  60 us
    all_to_all x2, starting transfers between devices, exchange(): lax.all_to_all(block, ('arrow', 'blk'), split_axis=0, concat_axis=0, tile...  17.4 us
    pallas_call x1, Pallas kernels, body(): pl.pallas_call(functools.partial(prep_kernel, arrows, size, width), grid=...  8.31 us
    pallas_call x1, Pallas kernels, body(): pl.pallas_call(functools.partial(block_kernel, width), in_specs=[VM] * 8...  7.17 us
    pallas_call x1, Pallas kernels, body(): pl.pallas_call(functools.partial(tail_kernel, width, arrows), in_specs=[V...  6.27 us
    pallas_call x1, Pallas kernels, body(): pl.pallas_call(functools.partial(arm_kernel, width), in_specs=[VM, VM, VM...  4.54 us
    pallas_call x1, Pallas kernels, body(): pl.pallas_call(functools.partial(pack_kernel, size, width), in_specs=[HB,...  3.62 us
    ppermute x2, starting transfers between devices, body(): lax.ppermute(g, ('arrow', 'blk'), m)  2.75 us
  transfers between devices with their start and end apart: 6, of which 2 were waited for; matrix products, arithmetic and copies ran while one was open for 0% of the time, Pallas kernels for 17%

profile of v8, /device:TPU:1, one launch (start us, length us, event | category | flops | bytes accessed | tf_op | source)
XLA Modules:
  0.0 115.3 jit_solution(17471231282626050466)
XLA Ops:
  0.0 3.6 %pack.1 = bf16[1024,1280]{1,0:T(8,128)(2,1)} custom-call(bf16[256,512]{1,0:T(8,128)(2,1)} %feat_ref.1, s32[4,256]{1,0:T(4,128)} %pos_hbm.1), custom_call_target="tpu_custom_call" | custom-call | tf_op jit(solution)/shard_map/pack/pallas_call | solution.py:408
  3.6 0.0 copy-start.1
  3.6 11.5 %all-to-all-start = ((bf16[128,8,1280]{2,1,0:T(8,128)(2,1)}), bf16[128,8,1280]{2,1,0:T(8,128)(2,1)S(1)}, u32[]{:S(2)}, u32[]{:S(2)}) async-start(bf16[128,8,1280]{2,1,0:T(8,128)(2,1)} %bitcast.11), calls=%async_computation | async-start | bytes 5242880 | tf_op jit(solution)/shard_map/all_to_all | solution.py:18
  15.1 0.0 copy-done.1
  15.1 0.1 copy.10
  15.2 35.5 %all-to-all-done = bf16[128,8,1280]{2,1,0:T(8,128)(2,1)S(1)} async-done(((bf16[128,8,1280]{2,1,0:T(8,128)(2,1)}), bf16[128,8,1280]{2,1,0:T(8,128)(2,1)S(1)}, u32[]{:S(2)}, u32[]{:S(2)}) %all-to-all-start) | async-done | bytes 2621472 | tf_op jit(solution)/shard_map/all_to_all | solution.py:18
  50.8 0.6 heads.1
  51.4 0.4 collective-permute-start
  51.8 2.3 %collective-permute-start.1 = (bf16[392,512]{1,0:T(8,128)(2,1)S(1)}, bf16[392,512]{1,0:T(8,128)(2,1)S(1)}, u32[]{:S(2)}, u32[]{:S(2)}) collective-permute-start(bf16[392,512]{1,0:T(8,128)(2,1)S(1)} %get-tuple-element.24.e1_ref), channel_id=1, source_target_pairs={{0,24},{1,25},{2,26},{3,27},{4,28},{5,29},{6,30},{7,31},{8,0},{9,1... | collective-permute-start | bytes 1204232 | tf_op jit(solution)/shard_map/ppermute | solution.py:468
  54.1 0.1 broadcast_bitcast_fusion.mask_ref
  54.2 4.5 %arms.1 = (bf16[1024,512]{1,0:T(8,128)(2,1)S(1)}, bf16[1024,512]{1,0:T(8,128)(2,1)S(1)}, f32[1536,128]{1,0:T(8,128)S(1)}, bf16[384,512]{1,0:T(8,128)(2,1)S(1)}, bf16[384,512]{1,0:T(8,128)(2,1)S(1)}) custom-call(bf16[1024,1280]{1,0:T(8,128)(2,1)S(1)} %bitcast.8, f32[768,128]{1,0:T(8,128)S(1)} %get-tuple-element.19.known_ref, ...), custom_call_target="tpu_custom_call" | custom-call | tf_op jit(solution)/shard_map/arms/pallas_call | solution.py:469
  58.7 0.1 collective-permute-start.2
  58.8 2.7 %collective-permute-start.3 = (bf16[384,512]{1,0:T(8,128)(2,1)S(1)}, bf16[384,512]{1,0:T(8,128)(2,1)S(1)}, u32[]{:S(2)}, u32[]{:S(2)}) collective-permute-start(bf16[384,512]{1,0:T(8,128)(2,1)S(1)} %get-tuple-element.28), channel_id=1, source_target_pairs={{0,24},{1,25},{2,26},{3,27},{4,28},{5,29},{6,30},{7,31},{8,0},{9,1... | collective-permute-start | bytes 1179656 | tf_op jit(solution)/shard_map/ppermute | solution.py:484
  61.5 0.0 collective-permute-done.f0_ref
  61.5 0.0 collective-permute-done.1.f1_ref
  61.5 7.2 %blocks.1 = (bf16[1024,1152]{1,0:T(8,128)(2,1)}, f32[512,512]{1,0:T(8,128)S(1)}, f32[768,512]{1,0:T(8,128)S(1)}) custom-call(bf16[1024,512]{1,0:T(8,128)(2,1)S(1)} %get-tuple-element.20.x_ref, bf16[1024,512]{1,0:T(8,128)(2,1)S(1)} %get-tuple-element.21.t_ref, f32[1536,128]{1,0:T(8,128)S(1)} %get-tuple-element.22.p_ref, ...), custom_call_target="tpu_custom_call" | custom-call | tf_op jit(solution)/shard_map/blocks/pallas_call | solution.py:485
  68.7 0.0 collective-permute-done.2.r0_ref
  68.7 0.0 collective-permute-done.3.r1_ref
  68.7 1.3 %join.1 = bf16[1024,1152]{1,0:T(8,128)(2,1)} custom-call(f32[512,512]{1,0:T(8,128)S(1)} %get-tuple-element.25.extra_ref, f32[768,512]{1,0:T(8,128)S(1)} %get-tuple-element.26.arm_ref, bf16[384,512]{1,0:T(8,128)(2,1)S(1)} %collective-permute-done.2.r0_ref, bf16[384,512]{1,0:T(8,128)(2,1)S(1)} %collective-permute-done.3.r1_ref, ...), custom_call_target="tpu_custom_call", output_to_operand_aliasing={{}: (4, {})} | custom-call | tf_op jit(solution)/shard_map/join/pallas_call | solution.py:508
  70.0 0.0 copy-start
  70.0 5.9 %all-to-all-start.1 = ((bf16[128,8,1152]{2,1,0:T(8,128)(2,1)}), bf16[128,8,1152]{2,1,0:T(8,128)(2,1)S(1)}, u32[]{:S(2)}, u32[]{:S(2)}) async-start(bf16[128,8,1152]{2,1,0:T(8,128)(2,1)} %bitcast.12), calls=%async_computation.1 | async-start | bytes 4718592 | tf_op jit(solution)/shard_map/all_to_all | solution.py:18
  75.9 0.0 copy-done
  75.9 0.1 copy.11
  76.0 8.3 %prep.1 = (f32[256,128]{1,0:T(8,128)S(1)}, bf16[4,256,1024]{2,1,0:T(8,128)(2,1)}, bf16[4,512,1024]{2,1,0:T(8,128)(2,1)}) custom-call(s32[256,4]{1,0:T(8,128)S(1)} %bitcast.10, bf16[256,512]{1,0:T(8,128)(2,1)} %feat_ref.1, bf16[1024,4096]{1,0:T(8,128)(2,1)} %w_ref.1), custom_call_target="tpu_custom_call" | custom-call | tf_op jit(solution)/shard_map/prep/pallas_call | solution.py:426
  84.4 24.5 %all-to-all-done.1 = bf16[128,8,1152]{2,1,0:T(8,128)(2,1)S(1)} async-done(((bf16[128,8,1152]{2,1,0:T(8,128)(2,1)}), bf16[128,8,1152]{2,1,0:T(8,128)(2,1)S(1)}, u32[]{:S(2)}, u32[]{:S(2)}) %all-to-all-start.1) | async-done | bytes 2359328 | tf_op jit(solution)/shard_map/all_to_all | solution.py:18
  108.8 6.3 %tail.1 = bf16[256,512]{1,0:T(8,128)(2,1)} custom-call(bf16[1024,1152]{1,0:T(8,128)(2,1)S(1)} %bitcast.9, f32[256,128]{1,0:T(8,128)S(1)} %get-tuple-element.30.key_ref, bf16[4,256,1024]{2,1,0:T(8,128)(2,1)} %get-tuple-element.31.pre_hbm, bf16[4,512,1024]{2,1,0:T(8,128)(2,1)} %get-tuple-element.32.up_hbm, bf16[4096,512]{1,0:T(8,128)(2,1)} %down_hbm.1), custom_call_target="tpu_custom_call" | custom-call | tf_op jit(solution)/shard_map/tail/pallas_call | solution.py:525
  (1 shorter events, 0.0 us)
Async XLA Ops:
  3.6 11.5 %copy-start.1 = (s32[3,8,8]{2,1,0:T(8,128)S(1)}, s32[3,8,8]{2,1,0:T(8,128)}, u32[]{:S(2)}) copy-start(s32[3,8,8]{2,1,0:T(8,128)} %param.13) | copy-start | bytes 2308
  3.6 47.1 %all-to-all-start = ((bf16[128,8,1280]{2,1,0:T(8,128)(2,1)}), bf16[128,8,1280]{2,1,0:T(8,128)(2,1)S(1)}, u32[]{:S(2)}, u32[]{:S(2)}) async-start(bf16[128,8,1280]{2,1,0:T(8,128)(2,1)} %bitcast.11), calls=%async_computation | async-start | bytes 5242880 | tf_op jit(solution)/shard_map/all_to_all | solution.py:18
  51.4 10.1 %collective-permute-start = (bf16[392,512]{1,0:T(8,128)(2,1)S(1)}, bf16[392,512]{1,0:T(8,128)(2,1)S(1)}, u32[]{:S(2)}, u32[]{:S(2)}) collective-permute-start(bf16[392,512]{1,0:T(8,128)(2,1)S(1)} %get-tuple-element.23.e0_ref), channel_id=1, source_target_pairs={{0,8},{1,9},{2,10},{3,11},{4,12},{5,13},{6,14},{7,15},{8,16},{9,17... | collective-permute-start | bytes 1204232 | tf_op jit(solution)/shard_map/ppermute | solution.py:468
  51.8 9.7 %collective-permute-start.1 = (bf16[392,512]{1,0:T(8,128)(2,1)S(1)}, bf16[392,512]{1,0:T(8,128)(2,1)S(1)}, u32[]{:S(2)}, u32[]{:S(2)}) collective-permute-start(bf16[392,512]{1,0:T(8,128)(2,1)S(1)} %get-tuple-element.24.e1_ref), channel_id=1, source_target_pairs={{0,24},{1,25},{2,26},{3,27},{4,28},{5,29},{6,30},{7,31},{8,0},{9,1... | collective-permute-start | bytes 1204232 | tf_op jit(solution)/shard_map/ppermute | solution.py:468
  58.7 9.9 %collective-permute-start.2 = (bf16[384,512]{1,0:T(8,128)(2,1)S(1)}, bf16[384,512]{1,0:T(8,128)(2,1)S(1)}, u32[]{:S(2)}, u32[]{:S(2)}) collective-permute-start(bf16[384,512]{1,0:T(8,128)(2,1)S(1)} %get-tuple-element.27), channel_id=1, source_target_pairs={{0,8},{1,9},{2,10},{3,11},{4,12},{5,13},{6,14},{7,15},{8,16},{9,17... | collective-permute-start | bytes 1179656 | tf_op jit(solution)/shard_map/ppermute | solution.py:484
  58.8 9.9 %collective-permute-start.3 = (bf16[384,512]{1,0:T(8,128)(2,1)S(1)}, bf16[384,512]{1,0:T(8,128)(2,1)S(1)}, u32[]{:S(2)}, u32[]{:S(2)}) collective-permute-start(bf16[384,512]{1,0:T(8,128)(2,1)S(1)} %get-tuple-element.28), channel_id=1, source_target_pairs={{0,24},{1,25},{2,26},{3,27},{4,28},{5,29},{6,30},{7,31},{8,0},{9,1... | collective-permute-start | bytes 1179656 | tf_op jit(solution)/shard_map/ppermute | solution.py:484
  70.0 5.9 %copy-start = (s32[4,256]{1,0:T(4,128)S(1)}, s32[4,256]{1,0:T(4,128)}, u32[]{:S(2)}) copy-start(s32[4,256]{1,0:T(4,128)} %pos_hbm.1) | copy-start | bytes 12292
  70.0 38.9 %all-to-all-start.1 = ((bf16[128,8,1152]{2,1,0:T(8,128)(2,1)}), bf16[128,8,1152]{2,1,0:T(8,128)(2,1)S(1)}, u32[]{:S(2)}, u32[]{:S(2)}) async-start(bf16[128,8,1152]{2,1,0:T(8,128)(2,1)} %bitcast.12), calls=%async_computation.1 | async-start | bytes 4718592 | tf_op jit(solution)/shard_map/all_to_all | solution.py:18

commit v9 on v8

--- a/solution.py
+++ b/solution.py
@@ -102,12 +102,17 @@
         store(a).wait()
 
 
-def prep_kernel(arrows, block_rows, width, pos_ref, feat_ref, w_ref, key_ref, pre_ref, up_ref):
+def prep_kernel(
+    arrows, block_rows, width, pos_ref, feat_ref, w_ref, key_ref, pre_ref, first_ref, up_ref
+):
     pre_ref[0] = mm(feat_ref[...], w_ref[:width, :]).astype(pre_ref.dtype)
-    up_ref[0] = w_ref[width:, :]
+    @pl.when(pl.program_id(0) > 0)
+    def _():
+        up_ref[0] = w_ref[width:, :]
 
     @pl.when(pl.program_id(0) == 0)
     def _():
+        first_ref[...] = w_ref[width:, :]
         nodes = feat_ref.shape[0]
         n0 = lax.broadcasted_iota(jnp.int32, (nodes, nodes), 0)
         n1 = lax.broadcasted_iota(jnp.int32, (nodes, nodes), 1)
@@ -121,7 +126,7 @@
             rank = jnp.where(member & (slot % 8 == 0), mm(before, onehot(member)), 0.0)
             key = jnp.sum(rank, axis=1, keepdims=True) + (block * 16).astype(F32)
             keys = jnp.where(lane == a, key, keys)
-        key_ref[...] = keys
+        key_ref[...] = keys.T[0:8, :]
 
 
 STEP = 256
@@ -314,8 +319,8 @@
 
 
 def tail_kernel(
-    width, arrows, reply_ref, key_ref, pre_hbm, up_hbm, down_hbm, out_ref,
-    pick_ref, fold_ref, flat_ref, pre_ref, up_ref, down_ref, agg_ref, acc_ref, sem,
+    width, arrows, reply_ref, keys_ref, first_ref, pre_hbm, up_hbm, down_hbm, out_ref,
+    key_ref, pick_ref, fold_ref, flat_ref, pre_ref, up_ref, down_ref, agg_ref, acc_ref, sem,
 ):
     slots = reply_ref.shape[0]
     count, nodes, chunk = pre_ref.shape
@@ -324,14 +329,18 @@
         span = pl.ds(c * chunk, chunk)
         loads.append(
             (
-                pltpu.make_async_copy(up_hbm.at[c], up_ref.at[c], sem.at[0, c]),
                 pltpu.make_async_copy(pre_hbm.at[c], pre_ref.at[c], sem.at[1, c]),
                 pltpu.make_async_copy(down_hbm.at[span, :], down_ref.at[span, :], sem.at[2, c]),
             )
         )
+        if c > 0:
+            up = pltpu.make_async_copy(up_hbm.at[c - 1], up_ref.at[c - 1], sem.at[0, c])
+            loads[c] = (up, *loads[c])
         for copy in loads[c]:
             copy.start()
     rows = slots // arrows
+    empty = jnp.zeros((120, nodes), F32)
+    key_ref[...] = jnp.concatenate([keys_ref[...], empty], axis=0).T
     lane = lax.broadcasted_iota(jnp.int32, (1, rows), 1)
     blk = lane // 8
     block = blk * 16
@@ -362,11 +371,12 @@
     agg_ref[...] = total.astype(BF)
     acc_ref[...] = jnp.zeros(acc_ref.shape, F32)
     for c in range(count):
-        loads[c][0].wait()
-        loads[c][1].wait()
-        half = 0.5 * (pre_ref[c].astype(F32) + mm(agg_ref[...], up_ref[c]))
+        for copy in loads[c][:-1]:
+            copy.wait()
+        up = up_ref[c - 1] if c else first_ref[...]
+        half = 0.5 * (pre_ref[c].astype(F32) + mm(agg_ref[...], up))
         hidden = (half * jnp.tanh(half) + half).astype(BF)
-        loads[c][2].wait()
+        loads[c][-1].wait()
         acc_ref[...] += mm(hidden, down_ref[c * chunk : (c + 1) * chunk, :])
     out_ref[...] = acc_ref[...].astype(BF)
 
@@ -423,7 +433,7 @@
     )(in_hbm(features), in_hbm(positions))
     got = exchange(message.reshape(devices, 8, longest)).reshape(rows, longest)
 
-    key, pre, up = pl.pallas_call(
+    key, pre, first, up = pl.pallas_call(
         functools.partial(prep_kernel, arrows, size, width),
         grid=(count,),
         in_specs=[
@@ -432,14 +442,16 @@
             pl.BlockSpec((2 * width, CHUNK), lambda c: (0, c)),
         ],
         out_specs=[
-            pl.BlockSpec((row_count, 128), lambda c: (0, 0)),
+            pl.BlockSpec((8, row_count), lambda c: (0, 0)),
             pl.BlockSpec((1, row_count, CHUNK), lambda c: (c, 0, 0)),
-            pl.BlockSpec((1, width, CHUNK), lambda c: (c, 0, 0)),
+            pl.BlockSpec((width, CHUNK), lambda c: (0, 0)),
+            pl.BlockSpec((1, width, CHUNK), lambda c: (jnp.maximum(c - 1, 0), 0, 0)),
         ],
         out_shape=[
-            jax.ShapeDtypeStruct((row_count, 128), F32),
+            jax.ShapeDtypeStruct((8, row_count), F32),
             pltpu.HBM((count, row_count, CHUNK), PRE),
-            pltpu.HBM((count, width, CHUNK), BF),
+            jax.ShapeDtypeStruct((width, CHUNK), BF),
+            pltpu.HBM((count - 1, width, CHUNK), BF),
         ],
         compiler_params=params(20),
         name="prep",
@@ -524,15 +536,16 @@
 
     return pl.pallas_call(
         functools.partial(tail_kernel, width, arrows),
-        in_specs=[VM, VM, HB, HB, HB],
+        in_specs=[VM, VM, VM, HB, HB, HB],
         out_specs=VM,
         out_shape=jax.ShapeDtypeStruct((row_count, width), BF),
         scratch_shapes=[
+            pltpu.VMEM((row_count, 128), F32),
             pltpu.VMEM((row_count, rows), BF),
             pltpu.VMEM((rows, 128), F32),
             pltpu.VMEM((rows // 4, width), BF),
             pltpu.VMEM((count, row_count, CHUNK), PRE),
-            pltpu.VMEM((count, width, CHUNK), BF),
+            pltpu.VMEM((count - 1, width, CHUNK), BF),
             pltpu.VMEM((hidden, width), BF),
             pltpu.VMEM((row_count, width), BF),
             pltpu.VMEM((row_count, width), F32),
@@ -540,7 +553,7 @@
         ],
         compiler_params=params(40),
         name="tail",
-    )(reply, key, in_hbm(pre), in_hbm(up), in_hbm(down_weight))
+    )(reply, key, first, in_hbm(pre), in_hbm(up), in_hbm(down_weight))
 
 
 def solution(mesh):

time: 116 us -> 115 us (level)
  no operation moved by 1% of the time
where the time goes in v9:
time: 115 us
  waiting for transfers between devices  60.6 us (53%)
  Pallas kernels  31 us (27%)
  starting transfers between devices  22.9 us (20%)
    all_to_all x2, waiting for transfers between devices, exchange(): lax.all_to_all(block, ('arrow', 'blk'), split_axis=0, concat_axis=0, tile...  60.6 us
    all_to_all x2, starting transfers between devices, exchange(): lax.all_to_all(block, ('arrow', 'blk'), split_axis=0, concat_axis=0, tile...  17.4 us
    pallas_call x1, Pallas kernels, body(): pl.pallas_call(functools.partial(prep_kernel, arrows, size, width), grid=...  7.73 us
    pallas_call x1, Pallas kernels, body(): pl.pallas_call(functools.partial(block_kernel, width), in_specs=[VM] * 8...  7.17 us
    pallas_call x1, Pallas kernels, body(): pl.pallas_call(functools.partial(tail_kernel, width, arrows), in_specs=[V...  6.09 us
    pallas_call x1, Pallas kernels, body(): pl.pallas_call(functools.partial(arm_kernel, width), in_specs=[VM, VM, VM...  4.54 us
    pallas_call x1, Pallas kernels, body(): pl.pallas_call(functools.partial(pack_kernel, size, width), in_specs=[HB,...  3.62 us
    ppermute x2, starting transfers between devices, body(): lax.ppermute(g, ('arrow', 'blk'), m)  2.75 us
  transfers between devices with their start and end apart: 6, of which 2 were waited for; matrix products, arithmetic and copies ran while one was open for 0% of the time, Pallas kernels for 17%

profile of v9, /device:TPU:1, one launch (start us, length us, event | category | flops | bytes accessed | tf_op | source)
XLA Modules:
  0.0 115.1 jit_solution(11929113044452469563)
XLA Ops:
  0.0 3.6 %pack.1 = bf16[1024,1280]{1,0:T(8,128)(2,1)} custom-call(bf16[256,512]{1,0:T(8,128)(2,1)} %feat_ref.1, s32[4,256]{1,0:T(4,128)} %pos_hbm.1), custom_call_target="tpu_custom_call" | custom-call | tf_op jit(solution)/shard_map/pack/pallas_call | solution.py:418
  3.6 0.0 copy-start.1
  3.6 11.5 %all-to-all-start = ((bf16[128,8,1280]{2,1,0:T(8,128)(2,1)}), bf16[128,8,1280]{2,1,0:T(8,128)(2,1)S(1)}, u32[]{:S(2)}, u32[]{:S(2)}) async-start(bf16[128,8,1280]{2,1,0:T(8,128)(2,1)} %bitcast.11), calls=%async_computation | async-start | bytes 5242880 | tf_op jit(solution)/shard_map/all_to_all | solution.py:18
  15.1 0.0 copy-done.1
  15.1 0.1 copy.10
  15.2 35.5 %all-to-all-done = bf16[128,8,1280]{2,1,0:T(8,128)(2,1)S(1)} async-done(((bf16[128,8,1280]{2,1,0:T(8,128)(2,1)}), bf16[128,8,1280]{2,1,0:T(8,128)(2,1)S(1)}, u32[]{:S(2)}, u32[]{:S(2)}) %all-to-all-start) | async-done | bytes 2621472 | tf_op jit(solution)/shard_map/all_to_all | solution.py:18
  50.8 0.6 heads.1
  51.4 0.4 collective-permute-start
  51.8 2.3 %collective-permute-start.1 = (bf16[392,512]{1,0:T(8,128)(2,1)S(1)}, bf16[392,512]{1,0:T(8,128)(2,1)S(1)}, u32[]{:S(2)}, u32[]{:S(2)}) collective-permute-start(bf16[392,512]{1,0:T(8,128)(2,1)S(1)} %get-tuple-element.25.e1_ref), channel_id=1, source_target_pairs={{0,24},{1,25},{2,26},{3,27},{4,28},{5,29},{6,30},{7,31},{8,0},{9,1... | collective-permute-start | bytes 1204232 | tf_op jit(solution)/shard_map/ppermute | solution.py:480
  54.1 0.1 broadcast_bitcast_fusion.mask_ref
  54.2 4.5 %arms.1 = (bf16[1024,512]{1,0:T(8,128)(2,1)S(1)}, bf16[1024,512]{1,0:T(8,128)(2,1)S(1)}, f32[1536,128]{1,0:T(8,128)S(1)}, bf16[384,512]{1,0:T(8,128)(2,1)S(1)}, bf16[384,512]{1,0:T(8,128)(2,1)S(1)}) custom-call(bf16[1024,1280]{1,0:T(8,128)(2,1)S(1)} %bitcast.8, f32[768,128]{1,0:T(8,128)S(1)} %get-tuple-element.20.known_ref, ...), custom_call_target="tpu_custom_call" | custom-call | tf_op jit(solution)/shard_map/arms/pallas_call | solution.py:481
  58.7 0.1 collective-permute-start.2
  58.8 2.7 %collective-permute-start.3 = (bf16[384,512]{1,0:T(8,128)(2,1)S(1)}, bf16[384,512]{1,0:T(8,128)(2,1)S(1)}, u32[]{:S(2)}, u32[]{:S(2)}) collective-permute-start(bf16[384,512]{1,0:T(8,128)(2,1)S(1)} %get-tuple-element.29), channel_id=1, source_target_pairs={{0,24},{1,25},{2,26},{3,27},{4,28},{5,29},{6,30},{7,31},{8,0},{9,1... | collective-permute-start | bytes 1179656 | tf_op jit(solution)/shard_map/ppermute | solution.py:496
  61.5 0.0 collective-permute-done.f0_ref
  61.5 0.0 collective-permute-done.1.f1_ref
  61.5 7.2 %blocks.1 = (bf16[1024,1152]{1,0:T(8,128)(2,1)}, f32[512,512]{1,0:T(8,128)S(1)}, f32[768,512]{1,0:T(8,128)S(1)}) custom-call(bf16[1024,512]{1,0:T(8,128)(2,1)S(1)} %get-tuple-element.21.x_ref, bf16[1024,512]{1,0:T(8,128)(2,1)S(1)} %get-tuple-element.22.t_ref, f32[1536,128]{1,0:T(8,128)S(1)} %get-tuple-element.23.p_ref, ...), custom_call_target="tpu_custom_call" | custom-call | tf_op jit(solution)/shard_map/blocks/pallas_call | solution.py:497
  68.7 0.0 collective-permute-done.2.r0_ref
  68.7 0.0 collective-permute-done.3.r1_ref
  68.7 1.2 %join.1 = bf16[1024,1152]{1,0:T(8,128)(2,1)} custom-call(f32[512,512]{1,0:T(8,128)S(1)} %get-tuple-element.26.extra_ref, f32[768,512]{1,0:T(8,128)S(1)} %get-tuple-element.27.arm_ref, bf16[384,512]{1,0:T(8,128)(2,1)S(1)} %collective-permute-done.2.r0_ref, bf16[384,512]{1,0:T(8,128)(2,1)S(1)} %collective-permute-done.3.r1_ref, ...), custom_call_target="tpu_custom_call", output_to_operand_aliasing={{}: (4, {})} | custom-call | tf_op jit(solution)/shard_map/join/pallas_call | solution.py:520
  69.9 0.0 copy-start
  70.0 5.9 %all-to-all-start.1 = ((bf16[128,8,1152]{2,1,0:T(8,128)(2,1)}), bf16[128,8,1152]{2,1,0:T(8,128)(2,1)S(1)}, u32[]{:S(2)}, u32[]{:S(2)}) async-start(bf16[128,8,1152]{2,1,0:T(8,128)(2,1)} %bitcast.12), calls=%async_computation.1 | async-start | bytes 4718592 | tf_op jit(solution)/shard_map/all_to_all | solution.py:18
  75.9 0.0 copy-done
  75.9 0.1 copy.11
  76.0 7.7 %prep.1 = (f32[8,256]{1,0:T(8,128)S(1)}, bf16[4,256,1024]{2,1,0:T(8,128)(2,1)}, bf16[512,1024]{1,0:T(8,128)(2,1)S(1)}, bf16[3,512,1024]{2,1,0:T(8,128)(2,1)}) custom-call(s32[256,4]{1,0:T(8,128)S(1)} %bitcast.10, bf16[256,512]{1,0:T(8,128)(2,1)} %feat_ref.1, bf16[1024,4096]{1,0:T(8,128)(2,1)} %w_ref.1), custom_call_target="tpu_custom_call" | custom-call | tf_op jit(solution)/shard_map/prep/pallas_call | solution.py:436
  83.7 25.1 %all-to-all-done.1 = bf16[128,8,1152]{2,1,0:T(8,128)(2,1)S(1)} async-done(((bf16[128,8,1152]{2,1,0:T(8,128)(2,1)}), bf16[128,8,1152]{2,1,0:T(8,128)(2,1)S(1)}, u32[]{:S(2)}, u32[]{:S(2)}) %all-to-all-start.1) | async-done | bytes 2359328 | tf_op jit(solution)/shard_map/all_to_all | solution.py:18
  108.8 6.1 %tail.1 = bf16[256,512]{1,0:T(8,128)(2,1)} custom-call(bf16[1024,1152]{1,0:T(8,128)(2,1)S(1)} %bitcast.9, f32[8,256]{1,0:T(8,128)S(1)} %get-tuple-element.31.keys_ref, bf16[512,1024]{1,0:T(8,128)(2,1)S(1)} %get-tuple-element.32.first_ref, bf16[4,256,1024]{2,1,0:T(8,128)(2,1)} %get-tuple-element.33.pre_hbm, bf16[3,512,1024]{2,1,0:T(8,128)(2,1)} %get-tuple-element.34.up_hbm, ...), custom_call_target="tpu_custom_call" | custom-call | tf_op jit(solution)/shard_map/tail/pallas_call | solution.py:537
  (1 shorter events, 0.0 us)
Async XLA Ops:
  3.6 11.5 %copy-start.1 = (s32[3,8,8]{2,1,0:T(8,128)S(1)}, s32[3,8,8]{2,1,0:T(8,128)}, u32[]{:S(2)}) copy-start(s32[3,8,8]{2,1,0:T(8,128)} %param.13) | copy-start | bytes 2308
  3.6 47.1 %all-to-all-start = ((bf16[128,8,1280]{2,1,0:T(8,128)(2,1)}), bf16[128,8,1280]{2,1,0:T(8,128)(2,1)S(1)}, u32[]{:S(2)}, u32[]{:S(2)}) async-start(bf16[128,8,1280]{2,1,0:T(8,128)(2,1)} %bitcast.11), calls=%async_computation | async-start | bytes 5242880 | tf_op jit(solution)/shard_map/all_to_all | solution.py:18
  51.4 10.1 %collective-permute-start = (bf16[392,512]{1,0:T(8,128)(2,1)S(1)}, bf16[392,512]{1,0:T(8,128)(2,1)S(1)}, u32[]{:S(2)}, u32[]{:S(2)}) collective-permute-start(bf16[392,512]{1,0:T(8,128)(2,1)S(1)} %get-tuple-element.24.e0_ref), channel_id=1, source_target_pairs={{0,8},{1,9},{2,10},{3,11},{4,12},{5,13},{6,14},{7,15},{8,16},{9,17... | collective-permute-start | bytes 1204232 | tf_op jit(solution)/shard_map/ppermute | solution.py:480
  51.8 9.7 %collective-permute-start.1 = (bf16[392,512]{1,0:T(8,128)(2,1)S(1)}, bf16[392,512]{1,0:T(8,128)(2,1)S(1)}, u32[]{:S(2)}, u32[]{:S(2)}) collective-permute-start(bf16[392,512]{1,0:T(8,128)(2,1)S(1)} %get-tuple-element.25.e1_ref), channel_id=1, source_target_pairs={{0,24},{1,25},{2,26},{3,27},{4,28},{5,29},{6,30},{7,31},{8,0},{9,1... | collective-permute-start | bytes 1204232 | tf_op jit(solution)/shard_map/ppermute | solution.py:480
  58.7 9.9 %collective-permute-start.2 = (bf16[384,512]{1,0:T(8,128)(2,1)S(1)}, bf16[384,512]{1,0:T(8,128)(2,1)S(1)}, u32[]{:S(2)}, u32[]{:S(2)}) collective-permute-start(bf16[384,512]{1,0:T(8,128)(2,1)S(1)} %get-tuple-element.28), channel_id=1, source_target_pairs={{0,8},{1,9},{2,10},{3,11},{4,12},{5,13},{6,14},{7,15},{8,16},{9,17... | collective-permute-start | bytes 1179656 | tf_op jit(solution)/shard_map/ppermute | solution.py:496
  58.8 9.9 %collective-permute-start.3 = (bf16[384,512]{1,0:T(8,128)(2,1)S(1)}, bf16[384,512]{1,0:T(8,128)(2,1)S(1)}, u32[]{:S(2)}, u32[]{:S(2)}) collective-permute-start(bf16[384,512]{1,0:T(8,128)(2,1)S(1)} %get-tuple-element.29), channel_id=1, source_target_pairs={{0,24},{1,25},{2,26},{3,27},{4,28},{5,29},{6,30},{7,31},{8,0},{9,1... | collective-permute-start | bytes 1179656 | tf_op jit(solution)/shard_map/ppermute | solution.py:496
  69.9 5.9 %copy-start = (s32[4,256]{1,0:T(4,128)S(1)}, s32[4,256]{1,0:T(4,128)}, u32[]{:S(2)}) copy-start(s32[4,256]{1,0:T(4,128)} %pos_hbm.1) | copy-start | bytes 12292
  70.0 38.9 %all-to-all-start.1 = ((bf16[128,8,1152]{2,1,0:T(8,128)(2,1)}), bf16[128,8,1152]{2,1,0:T(8,128)(2,1)S(1)}, u32[]{:S(2)}, u32[]{:S(2)}) async-start(bf16[128,8,1152]{2,1,0:T(8,128)(2,1)} %bitcast.12), calls=%async_computation.1 | async-start | bytes 4718592 | tf_op jit(solution)/shard_map/all_to_all | solution.py:18
